TPU v7x, 128 devices: a whole 4x4x4 slice. The times are simulated.
128 devices in a mesh: fsdp: 32 (over x, y, core), tensor: 4 (over z).
Axes of the slice: x: 4, y: 4, z: 4, core: 2. Of those that a mesh axis runs over, the one named last changes fastest.
Arguments:
- tokens: bfloat16 [4096, 4096], P(('fsdp', 'tensor')), may hold values from -6 to 6
- gate_blocks: bfloat16 [4, 544, 128, 128], P('tensor', 'fsdp'), may hold values from -0.125 to 0.125
- gate_index: int32 [4, 544], P('tensor', 'fsdp'), may hold values from 0 to 896, as said below
- up_blocks: bfloat16 [4, 544, 128, 128], P('tensor', 'fsdp'), may hold values from -0.125 to 0.125
- up_index: int32 [4, 544], P('tensor', 'fsdp'), may hold values from 0 to 896, as said below
- d_hidden: bfloat16 [4096, 14336], P('fsdp', 'tensor'), may hold values from -6 to 6
Outputs:
- hidden: bfloat16 [4096, 14336], P('fsdp', 'tensor')
- d_tokens: bfloat16 [4096, 4096], P(('fsdp', 'tensor'))
Inputs may be any that keep to these rules, and one draw needn't show every extreme that they name: `gate_index`: row t, slots f * 17 to (f + 1) * 17 - 1 belong to fsdp index f: its live slots come first and hold distinct values r * 28 + c with r among row blocks f * 1 to (f + 1) - 1; the remaining slots hold 896. Each such shard has 11 to 17 live slots, both reached in every row; shards 2i and 2i + 1 together hold exactly 28 live slots. `up_index`: as for gate_index, drawn independently.
All inputs are finite; a program needn't handle non-finite values.
Results may differ from a plain program's by a relative error of at most 0.005.
Values may be sent and summed in bfloat16 or wider, within the bound.
No kernel may reach another device: no remote copies, remote signals or barrier semaphores. Data moves between devices by JAX's collectives and lax.ppermute only.
A program may use at most 128 MiB of HBM per device.

v0:
```python
import jax
import jax.numpy as jnp
from jax import lax
from jax.sharding import PartitionSpec as P


def positions(block_index, row_blocks, col_blocks):
    valid = block_index < row_blocks * col_blocks
    row_of = jnp.minimum(block_index // col_blocks, row_blocks - 1)
    col_of = block_index % col_blocks
    row_target = jnp.where(valid, row_of, row_blocks)
    col_target = jnp.where(valid, col_of, col_blocks)
    return (row_of, col_of, row_target, col_target)


def forward_group(total, rows_split, blocks, block_index, row_blocks, col_blocks):
    row_of, col_of, row_target, col_target = positions(block_index, row_blocks, col_blocks)
    picked = jnp.take(rows_split, row_of, axis=1)
    product = jnp.einsum("tsk,skn->tsn", picked, blocks, preferred_element_type=jnp.float32)
    return total.at[:, col_target].add(product, mode="drop")


def backward_group(total, grad_split, blocks, block_index, row_blocks, col_blocks):
    row_of, col_of, row_target, col_target = positions(block_index, row_blocks, col_blocks)
    chosen = jnp.take(grad_split, col_of, axis=1)
    product = jnp.einsum("tsn,skn->tsk", chosen, blocks, preferred_element_type=jnp.float32)
    return total.at[:, row_target].add(product, mode="drop")


def shards(tokens, gate_blocks, gate_index, up_blocks, up_index, d_hidden):
    block = gate_blocks.shape[-1]
    gathered_rows = lax.all_gather(tokens, "tensor", axis=0, tiled=True)
    row_count = gathered_rows.shape[0]
    model_width = gathered_rows.shape[1]
    row_blocks = model_width // block
    local_units = d_hidden.shape[1]
    col_blocks = local_units // block
    shard_count = lax.axis_size("fsdp")
    own_gate, own_gate_index = (gate_blocks[0], gate_index[0])
    own_up, own_up_index = (up_blocks[0], up_index[0])
    all_gate, all_gate_index, all_up, all_up_index = (
        lax.all_gather(own_gate, "fsdp", axis=0, tiled=True),
        lax.all_gather(own_gate_index, "fsdp", axis=0, tiled=True),
        lax.all_gather(own_up, "fsdp", axis=0, tiled=True),
        lax.all_gather(own_up_index, "fsdp", axis=0, tiled=True),
    )
    per_shard = own_gate.shape[0]
    group_shards = 4
    group_count = shard_count // group_shards
    group_slots = group_shards * per_shard
    grouped = (
        all_gate.reshape(group_count, group_slots, block, block),
        all_gate_index.reshape(group_count, group_slots),
        all_up.reshape(group_count, group_slots, block, block),
        all_up_index.reshape(group_count, group_slots),
    )
    rows_split = gathered_rows.reshape(row_count, row_blocks, block)

    def forward_step(carry, pieces):
        gate_acc, up_acc = carry
        gate_acc = forward_group(gate_acc, rows_split, pieces[0], pieces[1], row_blocks, col_blocks)
        up_acc = forward_group(up_acc, rows_split, pieces[2], pieces[3], row_blocks, col_blocks)
        return ((gate_acc, up_acc), None)

    empty_cols = jnp.zeros((row_count, col_blocks, block), jnp.float32)
    (gate, up), _ = lax.scan(forward_step, (empty_cols, empty_cols), grouped)
    gate = gate.reshape(row_count, local_units)
    up = up.reshape(row_count, local_units)
    sig = jax.nn.sigmoid(gate)
    active = gate * sig
    hidden = (active * up).astype(jnp.bfloat16)
    d_slice = d_hidden.astype(jnp.float32)
    d_gate = (
        (d_slice * up * sig * (1.0 + gate * (1.0 - sig)))
        .astype(jnp.bfloat16)
        .reshape(row_count, col_blocks, block)
    )
    d_up = (d_slice * active).astype(jnp.bfloat16).reshape(row_count, col_blocks, block)

    def backward_step(total, pieces):
        total = backward_group(total, d_gate, pieces[0], pieces[1], row_blocks, col_blocks)
        total = backward_group(total, d_up, pieces[2], pieces[3], row_blocks, col_blocks)
        return (total, None)

    empty_rows = jnp.zeros((row_count, row_blocks, block), jnp.float32)
    partial_grad, _ = lax.scan(backward_step, empty_rows, grouped)
    partial_grad = partial_grad.reshape(row_count, model_width)
    d_tokens = lax.psum_scatter(partial_grad, "tensor", scatter_dimension=0, tiled=True).astype(
        jnp.bfloat16
    )
    return (hidden, d_tokens)


def solution(mesh):
    in_specs = (
        P(("fsdp", "tensor"), None),
        P("tensor", "fsdp", None, None),
        P("tensor", "fsdp"),
        P("tensor", "fsdp", None, None),
        P("tensor", "fsdp"),
        P("fsdp", "tensor"),
    )
    out_specs = (P("fsdp", "tensor"), P(("fsdp", "tensor"), None))
    return jax.shard_map(shards, mesh=mesh, in_specs=in_specs, out_specs=out_specs, check_vma=False)
```

profile of v0, /device:TPU:1, one launch (start us, length us, event | category | flops | bytes accessed | tf_op | source)
XLA Modules:
  0.0 901.3 jit_solution(12688166231259519169)
XLA Ops:
  12.8 14.7 %all-reduce.2 = (s32[544]{0:T(1024)S(1)}, s32[544]{0:T(1024)S(1)}) all-reduce(s32[544]{0:T(1024)S(1)} %bitcast_dynamic-update-slice_fusion.1, s32[544]{0:T(1024)S(1)} %bitcast_dynamic-update-slice_fusion), channel_id=2, replica_groups=mesh['fsdp'=32,'tensor'=4] {'fsdp'}, use_global_device_ids=true, to_apply=%add | all-reduce | flops 1088 | bytes 8704
  38.5 76.5 %all-gather.10.cloned.1.call-done = bf16[1,544,128,128]{3,2,0,1:T(8,128)(2,1)} async-done(((bf16[1,17,128,128]{3,2,0,1:T(8,128)(2,1)}), bf16[1,544,128,128]{3,2,0,1:T(8,128)(2,1)}) %all-gather.10.cloned.1.call-update) | async-done | bytes 17825808 | tf_op jit(solution)/shard_map/all_gather | solution.py:42
  115.0 76.6 %all-gather.12.cloned.1.call-done = bf16[1,544,128,128]{3,2,0,1:T(8,128)(2,1)} async-done(((bf16[1,17,128,128]{3,2,0,1:T(8,128)(2,1)}), bf16[1,544,128,128]{3,2,0,1:T(8,128)(2,1)}) %all-gather.12.cloned.1.call-update) | async-done | bytes 17825808 | tf_op jit(solution)/shard_map/all_gather | solution.py:44
  193.3 340.2 %while.28 = (s32[]{:T(128)}, f32[128,28,128]{2,0,1:T(8,128)S(1)}, f32[128,28,128]{2,0,1:T(8,128)}, s32[8,68]{1,0:T(8,128)S(1)}, bf16[8,68,128,128]{3,2,1,0:T(8,1...) while((s32[]{:T(128)}, f32[128,28,128]{2,0,1:T(8,128)S(1)}, ...), condition=%wide.region_3.5_spmd, body=%wide.region_0.4_spmd.sunk | while | flops 574887424 | bytes 53490772 | solution.py:66
  201.0 16.9 %scatter_fusion.1 = f32[128,28,128]{2,0,1:T(8,128)} fusion(f32[128,28,128]{2,0,1:T(8,128)} %get-tuple-element.504, s32[68]{0:T(128)S(1)} %get-tuple-element.476, f32[68,128,128]{2,1,0:T(8,128)} %fusion.70), kind=kCustom, calls=%fused_computation.5.clone.1 | custom fusion | flops 1114112 | bytes 13369616 | tf_op jit(solution)/shard_map/while/body/eval_jaxpr/scatter-add | solution.py:20
  225.5 10.6 %scatter_fusion = f32[128,28,128]{2,0,1:T(8,128)S(1)} fusion(f32[128,28,128]{2,0,1:T(8,128)S(1)} %get-tuple-element.503, s32[68]{0:T(128)S(1)} %get-tuple-element.473, f32[68,128,128]{2,1,0:T(8,128)} %fusion.69), kind=kCustom, calls=%fused_computation.4.clone.1 | custom fusion | flops 1114112 | bytes 13369616 | tf_op jit(solution)/shard_map/while/body/eval_jaxpr/scatter-add | solution.py:20
  243.7 16.4 %scatter_fusion.1 = f32[128,28,128]{2,0,1:T(8,128)} fusion(f32[128,28,128]{2,0,1:T(8,128)} %get-tuple-element.504, s32[68]{0:T(128)S(1)} %get-tuple-element.476, f32[68,128,128]{2,1,0:T(8,128)} %fusion.70), kind=kCustom, calls=%fused_computation.5.clone.1 | custom fusion | flops 1114112 | bytes 13369616 | tf_op jit(solution)/shard_map/while/body/eval_jaxpr/scatter-add | solution.py:20
  267.8 10.6 %scatter_fusion = f32[128,28,128]{2,0,1:T(8,128)S(1)} fusion(f32[128,28,128]{2,0,1:T(8,128)S(1)} %get-tuple-element.503, s32[68]{0:T(128)S(1)} %get-tuple-element.473, f32[68,128,128]{2,1,0:T(8,128)} %fusion.69), kind=kCustom, calls=%fused_computation.4.clone.1 | custom fusion | flops 1114112 | bytes 13369616 | tf_op jit(solution)/shard_map/while/body/eval_jaxpr/scatter-add | solution.py:20
  286.1 16.4 %scatter_fusion.1 = f32[128,28,128]{2,0,1:T(8,128)} fusion(f32[128,28,128]{2,0,1:T(8,128)} %get-tuple-element.504, s32[68]{0:T(128)S(1)} %get-tuple-element.476, f32[68,128,128]{2,1,0:T(8,128)} %fusion.70), kind=kCustom, calls=%fused_computation.5.clone.1 | custom fusion | flops 1114112 | bytes 13369616 | tf_op jit(solution)/shard_map/while/body/eval_jaxpr/scatter-add | solution.py:20
  310.0 10.6 %scatter_fusion = f32[128,28,128]{2,0,1:T(8,128)S(1)} fusion(f32[128,28,128]{2,0,1:T(8,128)S(1)} %get-tuple-element.503, s32[68]{0:T(128)S(1)} %get-tuple-element.473, f32[68,128,128]{2,1,0:T(8,128)} %fusion.69), kind=kCustom, calls=%fused_computation.4.clone.1 | custom fusion | flops 1114112 | bytes 13369616 | tf_op jit(solution)/shard_map/while/body/eval_jaxpr/scatter-add | solution.py:20
  328.3 16.8 %scatter_fusion.1 = f32[128,28,128]{2,0,1:T(8,128)} fusion(f32[128,28,128]{2,0,1:T(8,128)} %get-tuple-element.504, s32[68]{0:T(128)S(1)} %get-tuple-element.476, f32[68,128,128]{2,1,0:T(8,128)} %fusion.70), kind=kCustom, calls=%fused_computation.5.clone.1 | custom fusion | flops 1114112 | bytes 13369616 | tf_op jit(solution)/shard_map/while/body/eval_jaxpr/scatter-add | solution.py:20
  352.7 10.6 %scatter_fusion = f32[128,28,128]{2,0,1:T(8,128)S(1)} fusion(f32[128,28,128]{2,0,1:T(8,128)S(1)} %get-tuple-element.503, s32[68]{0:T(128)S(1)} %get-tuple-element.473, f32[68,128,128]{2,1,0:T(8,128)} %fusion.69), kind=kCustom, calls=%fused_computation.4.clone.1 | custom fusion | flops 1114112 | bytes 13369616 | tf_op jit(solution)/shard_map/while/body/eval_jaxpr/scatter-add | solution.py:20
  371.0 16.4 %scatter_fusion.1 = f32[128,28,128]{2,0,1:T(8,128)} fusion(f32[128,28,128]{2,0,1:T(8,128)} %get-tuple-element.504, s32[68]{0:T(128)S(1)} %get-tuple-element.476, f32[68,128,128]{2,1,0:T(8,128)} %fusion.70), kind=kCustom, calls=%fused_computation.5.clone.1 | custom fusion | flops 1114112 | bytes 13369616 | tf_op jit(solution)/shard_map/while/body/eval_jaxpr/scatter-add | solution.py:20
  395.1 10.6 %scatter_fusion = f32[128,28,128]{2,0,1:T(8,128)S(1)} fusion(f32[128,28,128]{2,0,1:T(8,128)S(1)} %get-tuple-element.503, s32[68]{0:T(128)S(1)} %get-tuple-element.473, f32[68,128,128]{2,1,0:T(8,128)} %fusion.69), kind=kCustom, calls=%fused_computation.4.clone.1 | custom fusion | flops 1114112 | bytes 13369616 | tf_op jit(solution)/shard_map/while/body/eval_jaxpr/scatter-add | solution.py:20
  413.3 16.9 %scatter_fusion.1 = f32[128,28,128]{2,0,1:T(8,128)} fusion(f32[128,28,128]{2,0,1:T(8,128)} %get-tuple-element.504, s32[68]{0:T(128)S(1)} %get-tuple-element.476, f32[68,128,128]{2,1,0:T(8,128)} %fusion.70), kind=kCustom, calls=%fused_computation.5.clone.1 | custom fusion | flops 1114112 | bytes 13369616 | tf_op jit(solution)/shard_map/while/body/eval_jaxpr/scatter-add | solution.py:20
  437.8 10.6 %scatter_fusion = f32[128,28,128]{2,0,1:T(8,128)S(1)} fusion(f32[128,28,128]{2,0,1:T(8,128)S(1)} %get-tuple-element.503, s32[68]{0:T(128)S(1)} %get-tuple-element.473, f32[68,128,128]{2,1,0:T(8,128)} %fusion.69), kind=kCustom, calls=%fused_computation.4.clone.1 | custom fusion | flops 1114112 | bytes 13369616 | tf_op jit(solution)/shard_map/while/body/eval_jaxpr/scatter-add | solution.py:20
  456.1 16.9 %scatter_fusion.1 = f32[128,28,128]{2,0,1:T(8,128)} fusion(f32[128,28,128]{2,0,1:T(8,128)} %get-tuple-element.504, s32[68]{0:T(128)S(1)} %get-tuple-element.476, f32[68,128,128]{2,1,0:T(8,128)} %fusion.70), kind=kCustom, calls=%fused_computation.5.clone.1 | custom fusion | flops 1114112 | bytes 13369616 | tf_op jit(solution)/shard_map/while/body/eval_jaxpr/scatter-add | solution.py:20
  480.6 10.6 %scatter_fusion = f32[128,28,128]{2,0,1:T(8,128)S(1)} fusion(f32[128,28,128]{2,0,1:T(8,128)S(1)} %get-tuple-element.503, s32[68]{0:T(128)S(1)} %get-tuple-element.473, f32[68,128,128]{2,1,0:T(8,128)} %fusion.69), kind=kCustom, calls=%fused_computation.4.clone.1 | custom fusion | flops 1114112 | bytes 13369616 | tf_op jit(solution)/shard_map/while/body/eval_jaxpr/scatter-add | solution.py:20
  498.8 16.5 %scatter_fusion.1 = f32[128,28,128]{2,0,1:T(8,128)} fusion(f32[128,28,128]{2,0,1:T(8,128)} %get-tuple-element.504, s32[68]{0:T(128)S(1)} %get-tuple-element.476, f32[68,128,128]{2,1,0:T(8,128)} %fusion.70), kind=kCustom, calls=%fused_computation.5.clone.1 | custom fusion | flops 1114112 | bytes 13369616 | tf_op jit(solution)/shard_map/while/body/eval_jaxpr/scatter-add | solution.py:20
  522.9 10.6 %scatter_fusion = f32[128,28,128]{2,0,1:T(8,128)S(1)} fusion(f32[128,28,128]{2,0,1:T(8,128)S(1)} %get-tuple-element.503, s32[68]{0:T(128)S(1)} %get-tuple-element.473, f32[68,128,128]{2,1,0:T(8,128)} %fusion.69), kind=kCustom, calls=%fused_computation.4.clone.1 | custom fusion | flops 1114112 | bytes 13369616 | tf_op jit(solution)/shard_map/while/body/eval_jaxpr/scatter-add | solution.py:20
  545.4 315.6 %while.29 = (s32[]{:T(128)}, f32[128,32,128]{2,0,1:T(8,128)S(1)}, s32[8,68]{1,0:T(8,128)S(1)}, bf16[8,68,128,128]{3,2,1,0:T(8,128)(2,1)}, bf16[128,28,128]{2,0,1...) while((s32[]{:T(128)}, f32[128,32,128]{2,0,1:T(8,128)S(1)}, ...), condition=%wide.region_7.10_spmd, body=%wide.region_4.9_spmd.sunk | while | flops 574887424 | bytes 53490772 | solution.py:86
  554.2 10.6 %scatter_fusion.2 = f32[128,32,128]{2,0,1:T(8,128)S(1)} fusion(f32[128,32,128]{2,0,1:T(8,128)S(1)} %get-tuple-element.530, s32[68]{0:T(128)S(1)} %get-tuple-element.487, f32[68,128,128]{2,1,0:T(8,128)} %fusion.76), kind=kCustom, calls=%fused_computation.6.clone.1 | custom fusion | flops 1114112 | bytes 13369616 | tf_op jit(solution)/shard_map/while/body/eval_jaxpr/scatter-add | solution.py:27
  593.6 10.6 %scatter_fusion.2 = f32[128,32,128]{2,0,1:T(8,128)S(1)} fusion(f32[128,32,128]{2,0,1:T(8,128)S(1)} %get-tuple-element.530, s32[68]{0:T(128)S(1)} %get-tuple-element.487, f32[68,128,128]{2,1,0:T(8,128)} %fusion.76), kind=kCustom, calls=%fused_computation.6.clone.1 | custom fusion | flops 1114112 | bytes 13369616 | tf_op jit(solution)/shard_map/while/body/eval_jaxpr/scatter-add | solution.py:27
  613.9 10.6 %scatter_fusion.3 = f32[128,32,128]{2,0,1:T(8,128)S(1)} fusion(f32[128,32,128]{2,0,1:T(8,128)S(1)} %scatter_fusion.2, s32[68]{0:T(128)S(1)} %get-tuple-element.490, f32[68,128,128]{2,1,0:T(8,128)} %fusion.77), kind=kCustom, calls=%fused_computation.7.clone.1 | custom fusion | flops 1114112 | bytes 13369616 | tf_op jit(solution)/shard_map/while/body/eval_jaxpr/scatter-add | solution.py:27
  633.0 10.6 %scatter_fusion.2 = f32[128,32,128]{2,0,1:T(8,128)S(1)} fusion(f32[128,32,128]{2,0,1:T(8,128)S(1)} %get-tuple-element.530, s32[68]{0:T(128)S(1)} %get-tuple-element.487, f32[68,128,128]{2,1,0:T(8,128)} %fusion.76), kind=kCustom, calls=%fused_computation.6.clone.1 | custom fusion | flops 1114112 | bytes 13369616 | tf_op jit(solution)/shard_map/while/body/eval_jaxpr/scatter-add | solution.py:27
  653.3 10.6 %scatter_fusion.3 = f32[128,32,128]{2,0,1:T(8,128)S(1)} fusion(f32[128,32,128]{2,0,1:T(8,128)S(1)} %scatter_fusion.2, s32[68]{0:T(128)S(1)} %get-tuple-element.490, f32[68,128,128]{2,1,0:T(8,128)} %fusion.77), kind=kCustom, calls=%fused_computation.7.clone.1 | custom fusion | flops 1114112 | bytes 13369616 | tf_op jit(solution)/shard_map/while/body/eval_jaxpr/scatter-add | solution.py:27
  672.5 10.6 %scatter_fusion.2 = f32[128,32,128]{2,0,1:T(8,128)S(1)} fusion(f32[128,32,128]{2,0,1:T(8,128)S(1)} %get-tuple-element.530, s32[68]{0:T(128)S(1)} %get-tuple-element.487, f32[68,128,128]{2,1,0:T(8,128)} %fusion.76), kind=kCustom, calls=%fused_computation.6.clone.1 | custom fusion | flops 1114112 | bytes 13369616 | tf_op jit(solution)/shard_map/while/body/eval_jaxpr/scatter-add | solution.py:27
  711.9 10.6 %scatter_fusion.2 = f32[128,32,128]{2,0,1:T(8,128)S(1)} fusion(f32[128,32,128]{2,0,1:T(8,128)S(1)} %get-tuple-element.530, s32[68]{0:T(128)S(1)} %get-tuple-element.487, f32[68,128,128]{2,1,0:T(8,128)} %fusion.76), kind=kCustom, calls=%fused_computation.6.clone.1 | custom fusion | flops 1114112 | bytes 13369616 | tf_op jit(solution)/shard_map/while/body/eval_jaxpr/scatter-add | solution.py:27
  751.3 10.6 %scatter_fusion.2 = f32[128,32,128]{2,0,1:T(8,128)S(1)} fusion(f32[128,32,128]{2,0,1:T(8,128)S(1)} %get-tuple-element.530, s32[68]{0:T(128)S(1)} %get-tuple-element.487, f32[68,128,128]{2,1,0:T(8,128)} %fusion.76), kind=kCustom, calls=%fused_computation.6.clone.1 | custom fusion | flops 1114112 | bytes 13369616 | tf_op jit(solution)/shard_map/while/body/eval_jaxpr/scatter-add | solution.py:27
  790.7 10.6 %scatter_fusion.2 = f32[128,32,128]{2,0,1:T(8,128)S(1)} fusion(f32[128,32,128]{2,0,1:T(8,128)S(1)} %get-tuple-element.530, s32[68]{0:T(128)S(1)} %get-tuple-element.487, f32[68,128,128]{2,1,0:T(8,128)} %fusion.76), kind=kCustom, calls=%fused_computation.6.clone.1 | custom fusion | flops 1114112 | bytes 13369616 | tf_op jit(solution)/shard_map/while/body/eval_jaxpr/scatter-add | solution.py:27
  830.1 10.6 %scatter_fusion.2 = f32[128,32,128]{2,0,1:T(8,128)S(1)} fusion(f32[128,32,128]{2,0,1:T(8,128)S(1)} %get-tuple-element.530, s32[68]{0:T(128)S(1)} %get-tuple-element.487, f32[68,128,128]{2,1,0:T(8,128)} %fusion.76), kind=kCustom, calls=%fused_computation.6.clone.1 | custom fusion | flops 1114112 | bytes 13369616 | tf_op jit(solution)/shard_map/while/body/eval_jaxpr/scatter-add | solution.py:27
  863.9 29.1 %reduce-scatter.2.cloned.1.call-done = f32[32,4096]{1,0:T(8,128)} async-done(((f32[128,4096]{1,0:T(8,128)}), f32[32,4096]{1,0:T(8,128)}) %reduce-scatter.2.cloned.1.call-update) | async-done | bytes 524304 | tf_op jit(solution)/shard_map/reduce_scatter | solution.py:88
  (172 shorter events, 365.6 us)
Async XLA Ops:
  7.2 29.0 %all-gather.8.cloned.1.call-start = ((), (), s32[]{:S(2)}) async-start(), calls=%async_computation.1 | async-start | bytes 1310720 | tf_op jit(solution)/shard_map/all_gather | solution.py:32
  7.9 107.1 %all-gather.10.cloned.1.call-start = ((), (), s32[]{:S(2)}) async-start(), calls=%async_computation.3 | async-start | bytes 18382848 | tf_op jit(solution)/shard_map/all_gather | solution.py:42
  8.6 183.0 %all-gather.12.cloned.1.call-start = ((), (), s32[]{:S(2)}) async-start(), calls=%async_computation.4 | async-start | bytes 18382848 | tf_op jit(solution)/shard_map/all_gather | solution.py:44
  9.4 883.6 %reduce-scatter.2.cloned.1.call-start = ((), (), s32[]{:S(2)}) async-start(), calls=%async_computation.2 | async-start | bytes 2621440 | tf_op jit(solution)/shard_map/reduce_scatter | solution.py:88
  535.2 2.9 copy-start
  535.2 2.9 copy-start.1
  542.2 1.7 copy-start.3
  861.0 1.6 copy-start.2
Sparse Core Ops, SparseCore 0:
  9.7 26.4 all-gather.7
  38.4 76.5 all-gather.9
  117.3 74.3 all-gather.11
  862.7 30.2 reduce-scatter.1
where the time goes:
time: 908 us; the launch traced here: 901 us
  other arithmetic  393 us (43%)
  waiting for transfers between devices  191 us (21%)
  matrix products  180 us (20%)
  local copies, waits for them, and re-layouts  107 us (12%)
  blocking collectives  14.7 us (2%)
  between operations  14.5 us (2%)
    scatter-add x16, other arithmetic, forward_group(): return total.at[:, col_target].add(product, mode='drop')  218 us
    scatter-add x16, other arithmetic, backward_group(): return total.at[:, row_target].add(product, mode='drop')  169 us
    dot_general x16, matrix products, backward_group(): jnp.einsum('tsn,skn->tsk', chosen, blocks, preferred_element_type=jnp.flo...  97.2 us
    dot_general x16, matrix products, forward_group(): jnp.einsum('tsk,skn->tsn', picked, blocks, preferred_element_type=jnp.flo...  82.6 us
    all_gather x1, waiting for transfers between devices, shards(): lax.all_gather(own_up, 'fsdp', axis=0, tiled=True)  76.6 us
    all_gather x1, waiting for transfers between devices, shards(): lax.all_gather(own_gate, 'fsdp', axis=0, tiled=True)  76.5 us
    gather x16, local copies, waits for them, and re-layouts, backward_group(): chosen = jnp.take(grad_split, col_of, axis=1)  48.5 us
    gather x16, local copies, waits for them, and re-layouts, forward_group(): picked = jnp.take(rows_split, row_of, axis=1)  39 us
  transfers between devices with their start and end apart: 4, of which 4 were waited for; matrix products, arithmetic and copies ran while one was open for 1% of the time, Pallas kernels for 0%

commit v1 on v0

v1 whole, which is shorter than its diff:
```python
import jax
import jax.numpy as jnp
from jax import lax
from jax.experimental import pallas as pl
from jax.experimental.pallas import tpu as pltpu
from jax.sharding import Mesh, PartitionSpec as P

F32 = jnp.float32
BF16 = jnp.bfloat16
BLK = 128
CHIPS = 16
NCB = 28
CAP = 17
SURE = 11
LIVE = 28
HID = NCB * BLK
WIDTH = CHIPS * 2 * BLK
DEAD = 32 * NCB
SWAP = [(0, 1), (1, 0)]
ANY = pl.BlockSpec(memory_space=pl.ANY)


def params(mib=56):
    return pltpu.CompilerParams(vmem_limit_bytes=mib << 20)


def pack_kernel(scal, mine, theirs, out, sem):
    core, n0 = scal[0], scal[1]

    def copies(first, second):
        made = [
            pltpu.make_async_copy(first.at[pl.ds(0, SURE)], out.at[pl.ds(0, SURE)], sem.at[0]),
            pltpu.make_async_copy(second.at[pl.ds(0, SURE)], out.at[pl.ds(n0, SURE)], sem.at[1]),
        ]
        for j in range(SURE, CAP):
            made.append((j < n0, pltpu.make_async_copy(first.at[j], out.at[j], sem.at[2 + j - SURE])))
            made.append((j < LIVE - n0, pltpu.make_async_copy(second.at[j], out.at[jnp.minimum(n0 + j, LIVE - 1)], sem.at[8 + j - SURE])))
        for verb in ("start", "wait"):
            for m in made:
                if isinstance(m, tuple):
                    pl.when(m[0])(getattr(m[1], verb))
                else:
                    getattr(m, verb)()

    @pl.when(core == 0)
    def _():
        copies(mine, theirs)

    @pl.when(core != 0)
    def _():
        copies(theirs, mine)


def pack(scal, mine, theirs):
    return pl.pallas_call(
        pack_kernel,
        out_shape=jax.ShapeDtypeStruct((LIVE, BLK, BLK), BF16),
        in_specs=[pl.BlockSpec(memory_space=pltpu.SMEM), ANY, ANY],
        out_specs=ANY,
        scratch_shapes=[pltpu.SemaphoreType.DMA((14,))],
        name="pack",
    )(scal, mine, theirs)


def fwd_kernel(table, blocks, x_own, x_other, acc_own, acc_other, panel):
    q = pl.program_id(0)

    @pl.when(q == 0)
    def _():
        acc_own[...] = jnp.zeros_like(acc_own)
        acc_other[...] = jnp.zeros_like(acc_other)

    panel[...] = jnp.zeros_like(panel)
    n0 = jnp.int32(SURE)
    for j in range(SURE, CAP):
        n0 += (table[q, j] < DEAD).astype(jnp.int32)
    base = q * 2 * NCB
    for j in range(LIVE):
        pos = table[q, jnp.where(j < n0, j, CAP + j - n0)] - base
        low = (pos >= NCB).astype(jnp.int32)
        panel[0, pos - low * NCB, pl.ds(pl.multiple_of(low * BLK, BLK), BLK), :] = blocks[j]
    x = jnp.concatenate([x_own[...], x_other[...]], axis=0)
    for c in range(NCB // 2):
        w = jnp.concatenate([panel[0, 2 * c], panel[0, 2 * c + 1]], axis=1)
        r = jnp.dot(x, w, preferred_element_type=F32)
        cols = pl.ds(c * 2 * BLK, 2 * BLK)
        acc_own[:, cols] += r[:BLK]
        acc_other[:, cols] += r[BLK:]


def forward(table, blocks, x_own, x_other):
    return pl.pallas_call(
        fwd_kernel,
        out_shape=(
            jax.ShapeDtypeStruct((BLK, HID), F32),
            jax.ShapeDtypeStruct((BLK, HID), F32),
            jax.ShapeDtypeStruct((CHIPS, NCB, 2 * BLK, BLK), BF16),
        ),
        grid_spec=pltpu.PrefetchScalarGridSpec(
            num_scalar_prefetch=1,
            grid=(CHIPS,),
            in_specs=[
                pl.BlockSpec((LIVE, BLK, BLK), lambda q, t: (q, 0, 0)),
                pl.BlockSpec((BLK, 2 * BLK), lambda q, t: (0, q)),
                pl.BlockSpec((BLK, 2 * BLK), lambda q, t: (0, q)),
            ],
            out_specs=[
                pl.BlockSpec((BLK, HID), lambda q, t: (0, 0)),
                pl.BlockSpec((BLK, HID), lambda q, t: (0, 0)),
                pl.BlockSpec((1, NCB, 2 * BLK, BLK), lambda q, t: (q, 0, 0, 0)),
            ],
        ),
        compiler_params=params(),
        name="forward",
    )(table, blocks, x_own, x_other)


def act_kernel(scal, mine, got, d_hidden, hidden, d_mine, d_send):
    first = scal[0] == 0
    a, b = mine[...], got[...]
    gate = jnp.where(first, a, b)
    up = jnp.where(first, b, a)
    d = d_hidden[...].astype(F32)
    sig = jax.nn.sigmoid(gate)
    active = gate * sig
    hidden[...] = (active * up).astype(BF16)
    d_gate = (d * up * sig * (1.0 + gate * (1.0 - sig))).astype(BF16)
    d_up = (d * active).astype(BF16)
    d_mine[...] = jnp.where(first, d_gate.astype(F32), d_up.astype(F32)).astype(BF16)
    d_send[...] = jnp.where(first, d_up.astype(F32), d_gate.astype(F32)).astype(BF16)


def activate(scal, mine, got, d_hidden):
    steps = 7
    spec = pl.BlockSpec((BLK, HID // steps), lambda i, s: (0, i))
    one = jax.ShapeDtypeStruct((BLK, HID), BF16)
    return pl.pallas_call(
        act_kernel,
        out_shape=(one, one, one),
        grid_spec=pltpu.PrefetchScalarGridSpec(
            num_scalar_prefetch=1, grid=(steps,), in_specs=[spec] * 3, out_specs=[spec] * 3
        ),
        compiler_params=params(),
        name="activate",
    )(scal, mine, got, d_hidden)


def bwd_kernel(d_own, d_other, panel, out_own, out_other, both):
    @pl.when(pl.program_id(0) == 0)
    def _():
        both[:BLK] = d_own[...]
        both[BLK:] = d_other[...]

    w = jnp.concatenate([panel[0, c] for c in range(NCB)], axis=1)
    r = lax.dot_general(both[...], w, (((1,), (1,)), ((), ())), preferred_element_type=F32)
    out_own[...] = r[:BLK]
    out_other[...] = r[BLK:].astype(BF16)


def backward(d_own, d_other, panels):
    whole = pl.BlockSpec((BLK, HID), lambda q: (0, 0))
    return pl.pallas_call(
        bwd_kernel,
        out_shape=(jax.ShapeDtypeStruct((BLK, WIDTH), F32), jax.ShapeDtypeStruct((BLK, WIDTH), BF16)),
        grid=(CHIPS,),
        in_specs=[whole, whole, pl.BlockSpec((1, NCB, 2 * BLK, BLK), lambda q: (q, 0, 0, 0))],
        out_specs=[pl.BlockSpec((BLK, 2 * BLK), lambda q: (0, q))] * 2,
        scratch_shapes=[pltpu.VMEM((2 * BLK, HID), BF16)],
        compiler_params=params(),
        name="backward",
    )(d_own, d_other, panels)


def join_kernel(scal, own, got, keep, *sends):
    z = scal[1]
    rows = BLK // 4
    total = [None] * 4
    for k in range(4):
        at = pl.ds(pl.multiple_of(((z + k) % 4) * rows, rows), rows)
        total[k] = own[at, :] + got[at, :].astype(F32)
    keep[...] = total[0]
    for k in range(3):
        sends[k][...] = total[k + 1].astype(BF16)


def join(scal, own, got):
    rows, steps = BLK // 4, 4
    cols = own.shape[1]
    wide = pl.BlockSpec((BLK, cols // steps), lambda i, s: (0, i))
    thin = pl.BlockSpec((rows, cols // steps), lambda i, s: (0, i))
    return pl.pallas_call(
        join_kernel,
        out_shape=(jax.ShapeDtypeStruct((rows, cols), F32),) + (jax.ShapeDtypeStruct((rows, cols), BF16),) * 3,
        grid_spec=pltpu.PrefetchScalarGridSpec(
            num_scalar_prefetch=1, grid=(steps,), in_specs=[wide, wide], out_specs=[thin] * 4
        ),
        compiler_params=params(),
        name="join",
    )(scal, own, got)


def shards(tokens, gate_blocks, gate_index, up_blocks, up_index, d_hidden):
    core, z = lax.axis_index("c"), lax.axis_index("z")
    first = core == 0
    gate_i, up_i = gate_index[0], up_index[0]
    both_index = lax.all_gather(jnp.stack([gate_i, up_i]), ("x", "y", "c"), axis=0)
    mine = jnp.where(first, gate_blocks[0], up_blocks[0])
    theirs = lax.ppermute(jnp.where(first, up_blocks[0], gate_blocks[0]), "c", SWAP)
    mine_i = jnp.where(first, gate_i, up_i)
    theirs_i = lax.ppermute(jnp.where(first, up_i, gate_i), "c", SWAP)
    n0 = jnp.sum((jnp.where(first, mine_i, theirs_i) < DEAD).astype(jnp.int32))
    payload = pack(jnp.stack([core, n0]), mine, theirs)
    blocks = lax.all_gather(payload, ("x", "y"), axis=0, tiled=True)
    table = jnp.where(first, both_index[:, 0], both_index[:, 1]).reshape(CHIPS, 2 * CAP)
    x_own = lax.all_gather(tokens, "z", axis=0, tiled=True)
    x_other = lax.ppermute(x_own, "c", SWAP)
    acc_own, acc_other, panels = forward(table, blocks, x_own, x_other)
    got = lax.ppermute(acc_other, "c", SWAP)
    scal = jnp.stack([core, z])
    hidden, d_mine, d_send = activate(scal, acc_own, got, d_hidden)
    d_other = lax.ppermute(d_send, "c", SWAP)
    part_own, part_other = backward(d_mine, d_other, panels)
    part_got = lax.ppermute(part_other, "c", SWAP)
    keep, *sends = join(scal, part_own, part_got)
    for k, s in enumerate(sends):
        keep = keep + lax.ppermute(s, "z", [(i, (i + k + 1) % 4) for i in range(4)]).astype(F32)
    return hidden, keep.astype(BF16)


def solution(mesh):
    fine = Mesh(mesh.devices.reshape(4, 4, 2, 4), ("x", "y", "c", "z"))
    fsdp = ("x", "y", "c")
    every = P((*fsdp, "z"), None)
    in_specs = (every, P("z", fsdp, None, None), P("z", fsdp), P("z", fsdp, None, None), P("z", fsdp), P(fsdp, "z"))
    return jax.shard_map(shards, mesh=fine, in_specs=in_specs, out_specs=(P(fsdp, "z"), every), check_vma=False)
```

time: 908 us -> 246 us (0.27)
  other arithmetic: 393 us -> 6.51 us
  matrix products: 180 us -> 0 us
  local copies, waits for them, and re-layouts: 107 us -> 4.65 us
  waiting for transfers between devices: 191 us -> 97.8 us
  Pallas kernels: 0 us -> 88.2 us
  blocking collectives: 14.7 us -> 24.5 us
    scatter-add x32 -> x0, other arithmetic: 387 us -> none  [the longest x16 218 us: forward_group(): return total.at[:, col_target].add(product, mode='drop')]
    dot_general x32 -> x0, matrix products: 180 us -> none  [the longest x16 97.2 us: backward_group(): jnp.einsum('tsn,skn->tsk', chosen, blocks, preferred_element_type=jnp.flo...]
    pallas_call x0 -> x5, Pallas kernels: none -> 88.2 us  [the longest x1 29.7 us: pack(): pl.pallas_call(pack_kernel, out_shape=jax.ShapeDtypeStruct((LIVE, BLK, BL...]
    gather x32 -> x0, local copies, waits for them, and re-layouts: 87.5 us -> none  [the longest x16 48.5 us: backward_group(): chosen = jnp.take(grad_split, col_of, axis=1)]
    all_gather x3 -> x2, waiting for transfers between devices: 159 us -> 77 us  [the longest x1 77 us: shards(): blocks = lax.all_gather(payload, ('x', 'y'), axis=0, tiled=True)]
    reduce_scatter x1 -> x0, waiting for transfers between devices: 29.1 us -> none  [shards(): lax.psum_scatter(partial_grad, 'tensor', scatter_dimension=0, tiled=True)]
    all_gather x0 -> x1, blocking collectives: none -> 24.5 us  [shards(): lax.all_gather(jnp.stack([gate_i, up_i]), ('x', 'y', 'c'), axis=0)]
    ppermute x0 -> x9, waiting for transfers between devices: none -> 20.1 us  [the longest x3 10.8 us: shards(): lax.ppermute(s, 'z', [(i, (i + k + 1) % 4) for i in range(4)]).astype(F32)]
  transfers between devices with their start and end apart: 4 -> 11, of which waited for: 4 -> 7; matrix products, arithmetic and copies ran while one was open for 1% -> 2% of each run, Pallas kernels for 0% -> 12%
where the time goes in v1:
time: 246 us; the launch traced here: 244 us
  waiting for transfers between devices  97.8 us (40%)
  Pallas kernels  88.2 us (36%)
  blocking collectives  24.5 us (10%)
  between operations  14.1 us (6%)
  starting transfers between devices  8.43 us (3%)
  other arithmetic  6.51 us (3%)
  local copies, waits for them, and re-layouts  4.65 us (2%)
    all_gather x1, waiting for transfers between devices, shards(): blocks = lax.all_gather(payload, ('x', 'y'), axis=0, tiled=True)  77 us
    pallas_call x1, Pallas kernels, pack(): pl.pallas_call(pack_kernel, out_shape=jax.ShapeDtypeStruct((LIVE, BLK, BL...  29.7 us
    pallas_call x1, Pallas kernels, forward(): pl.pallas_call(fwd_kernel, out_shape=(jax.ShapeDtypeStruct((BLK, HID), F3...  26.4 us
    all_gather x1, blocking collectives, shards(): lax.all_gather(jnp.stack([gate_i, up_i]), ('x', 'y', 'c'), axis=0)  24.5 us
    pallas_call x1, Pallas kernels, backward(): pl.pallas_call(bwd_kernel, out_shape=(jax.ShapeDtypeStruct((BLK, WIDTH),...  20.7 us
    ppermute x3, waiting for transfers between devices, shards(): lax.ppermute(s, 'z', [(i, (i + k + 1) % 4) for i in range(4)]).astype(F32)  10.8 us
    pallas_call x1, Pallas kernels, activate(): pl.pallas_call(act_kernel, out_shape=(one, one, one), grid_spec=pltpu.Pre...  7.01 us
    ppermute x3, starting transfers between devices, shards(): lax.ppermute(s, 'z', [(i, (i + k + 1) % 4) for i in range(4)]).astype(F32)  4.98 us
  transfers between devices with their start and end apart: 11, of which 7 were waited for; matrix products, arithmetic and copies ran while one was open for 2% of the time, Pallas kernels for 12%

profile of v1, /device:TPU:1, one launch (start us, length us, event | category | flops | bytes accessed | tf_op | source)
XLA Modules:
  0.0 244.3 jit_solution(9901508252434872468)
XLA Ops:
  7.2 0.7 all-gather.7.cloned.1.call-update
  8.0 2.1 select_bitcast_fusion
  10.1 1.4 collective-permute-start.1
  11.6 1.5 collective-permute-done
  13.1 0.6 fusion.3
  13.7 1.3 pad_add_fusion.1.scal
  15.0 0.8 copy-done.4
  15.8 29.7 %pack.1 = bf16[28,128,128]{2,1,0:T(8,128)(2,1)} custom-call(s32[2]{0:T(128)} %pad_add_fusion.1.scal, bf16[17,128,128]{2,1,0:T(8,128)(2,1)} %get-tuple-element.27.mine, bf16[17,128,128]{2,1,0:T(8,128)(2,1)} %copy-done.4), custom_call_target="tpu_custom_call" | custom-call | tf_op jit(solution)/shard_map/pack/pallas_call | solution.py:55
  45.6 0.4 collective-permute-start.2
  46.0 24.5 %all-gather.1 = s32[32,2,17]{2,1,0:T(2,128)S(1)} all-gather(s32[1,2,17]{2,1,0:T(2,128)S(1)} %add_bitcast_fusion), channel_id=2, replica_groups=mesh['x'=4,'y'=4,'c'=2,'z'=4] {'x','y','c'}, dimensions={0}, use_global_device_ids=true | all-gather | bytes 4488 | tf_op jit(solution)/shard_map/all_gather | solution.py:206
  70.6 0.7 select_n.55.table
  71.3 77.0 %all-gather.5.cloned.1.call-done.blocks = bf16[448,128,128]{2,1,0:T(8,128)(2,1)} async-done(((bf16[28,128,128]{2,1,0:T(8,128)(2,1)}), bf16[448,128,128]{2,1,0:T(8,128)(2,1)}) %all-gather.5.cloned.1.call-update) | async-done | bytes 14680080 | tf_op jit(solution)/shard_map/all_gather | solution.py:213
  148.3 26.4 %forward.1 = (f32[128,3584]{1,0:T(8,128)}, f32[128,3584]{1,0:T(8,128)}, bf16[16,28,256,128]{3,2,1,0:T(8,128)(2,1)}) custom-call(s32[16,34]{1,0:T(8,128)} %select_n.55.table, bf16[448,128,128]{2,1,0:T(8,128)(2,1)} %all-gather.5.cloned.1.call-done.blocks, bf16[128,4096]{1,0:T(8,128)(2,1)} %all-gather.7.cloned.1.call-done.x_own, bf16[128,4096]{1,0:T(8,128)(2,1)} %copy-done.2), custom_call_target="tpu_custom_call" | custom-call | tf_op jit(solution)/shard_map/forward/pallas_call | solution.py:92
  174.6 0.7 collective-permute-start.3
  175.3 0.6 pad_add_fusion.scal
  175.9 3.0 %collective-permute-done.3.got = f32[128,3584]{1,0:T(8,128)S(1)} collective-permute-done((f32[128,3584]{1,0:T(8,128)}, f32[128,3584]{1,0:T(8,128)S(1)}, u32[]{:S(2)}, u32[]{:S(2)}) %collective-permute-start.3) | collective-permute-done | bytes 1835040 | tf_op jit(solution)/shard_map/ppermute | solution.py:218
  179.0 1.2 copy-done
  180.2 7.0 %activate.1 = (bf16[128,3584]{1,0:T(8,128)(2,1)}, bf16[128,3584]{1,0:T(8,128)(2,1)}, bf16[128,3584]{1,0:T(8,128)(2,1)}) custom-call(s32[2]{0:T(128)} %pad_add_fusion.scal, f32[128,3584]{1,0:T(8,128)} %get-tuple-element.14.mine, f32[128,3584]{1,0:T(8,128)} %copy-done, bf16[128,3584]{1,0:T(8,128)(2,1)} %d_hidden.1), custom_call_target="tpu_custom_call" | custom-call | tf_op jit(solution)/shard_map/activate/pallas_call | solution.py:137
  187.2 0.4 collective-permute-start.4
  187.6 2.3 collective-permute-done.4.d_other
  189.9 0.9 copy-done.3
  190.8 20.7 %backward.1 = (f32[128,4096]{1,0:T(8,128)}, bf16[128,4096]{1,0:T(8,128)(2,1)}) custom-call(bf16[128,3584]{1,0:T(8,128)(2,1)} %get-tuple-element.17.d_own, bf16[128,3584]{1,0:T(8,128)(2,1)} %copy-done.3, bf16[16,28,256,128]{3,2,1,0:T(8,128)(2,1)} %get-tuple-element.19.panel), custom_call_target="tpu_custom_call" | custom-call | tf_op jit(solution)/shard_map/backward/pallas_call | solution.py:162
  211.5 0.4 collective-permute-start.5
  211.9 2.5 %collective-permute-done.5.got = bf16[128,4096]{1,0:T(8,128)(2,1)S(1)} collective-permute-done((bf16[128,4096]{1,0:T(8,128)(2,1)}, bf16[128,4096]{1,0:T(8,128)(2,1)S(1)}, u32[]{:S(2)}, u32[]{:S(2)}) %collective-permute-start.5) | collective-permute-done | bytes 1048608 | tf_op jit(solution)/shard_map/ppermute | solution.py:223
  214.4 1.0 copy-done.1
  215.4 4.4 %join.1 = (f32[32,4096]{1,0:T(8,128)}, bf16[32,4096]{1,0:T(8,128)(2,1)}, bf16[32,4096]{1,0:T(8,128)(2,1)}, bf16[32,4096]{1,0:T(8,128)(2,1)}) custom-call(s32[2]{0:T(128)} %pad_add_fusion.scal, f32[128,4096]{1,0:T(8,128)} %get-tuple-element.20.own, bf16[128,4096]{1,0:T(8,128)(2,1)} %copy-done.1), custom_call_target="tpu_custom_call" | custom-call | tf_op jit(solution)/shard_map/join/pallas_call | solution.py:191
  219.8 1.3 collective-permute-start.6
  221.1 2.6 %collective-permute-start.7 = (bf16[32,4096]{1,0:T(8,128)(2,1)}, bf16[32,4096]{1,0:T(8,128)(2,1)S(1)}, u32[]{:S(2)}, u32[]{:S(2)}) collective-permute-start(bf16[32,4096]{1,0:T(8,128)(2,1)} %get-tuple-element.24), channel_id=1, source_target_pairs={{0,2},{1,3},{2,0},{3,1},{4,6},{5,7},{6,4},{7,5},{8,10},{9,11},{10,... | collective-permute-start | bytes 786440 | tf_op jit(solution)/shard_map/ppermute | solution.py:226
  223.7 1.1 collective-permute-start.8
  224.8 4.0 %collective-permute-done.6 = bf16[32,4096]{1,0:T(8,128)(2,1)S(1)} collective-permute-done((bf16[32,4096]{1,0:T(8,128)(2,1)}, bf16[32,4096]{1,0:T(8,128)(2,1)S(1)}, u32[]{:S(2)}, u32[]{:S(2)}) %collective-permute-start.6) | collective-permute-done | bytes 262176 | tf_op jit(solution)/shard_map/ppermute | solution.py:226
  228.8 6.8 %collective-permute-done.7 = bf16[32,4096]{1,0:T(8,128)(2,1)S(1)} collective-permute-done((bf16[32,4096]{1,0:T(8,128)(2,1)}, bf16[32,4096]{1,0:T(8,128)(2,1)S(1)}, u32[]{:S(2)}, u32[]{:S(2)}) %collective-permute-start.7) | collective-permute-done | bytes 262176 | tf_op jit(solution)/shard_map/ppermute | solution.py:226
  235.6 1.9 add_convert_fusion
  (21 shorter events, 0.3 us)
Async XLA Ops:
  7.2 4.3 %copy-start.5 = (s32[1,17]{1,0:T(1,128)S(1)}, s32[1,17]{1,0:T(1,128)}, u32[]{:S(2)}) copy-start(s32[1,17]{1,0:T(1,128)} %param.10) | copy-start | bytes 208
  7.2 4.3 %copy-start.6 = (s32[1,17]{1,0:T(1,128)S(1)}, s32[1,17]{1,0:T(1,128)}, u32[]{:S(2)}) copy-start(s32[1,17]{1,0:T(1,128)} %param.8) | copy-start | bytes 208
  7.2 38.4 %all-gather.7.cloned.1.call-start = ((), (), s32[]{:S(2)}) async-start(), calls=%async_computation.1 | async-start | bytes 1310720 | tf_op jit(solution)/shard_map/all_gather | solution.py:215
  7.9 140.3 %all-gather.5.cloned.1.call-start = ((), (), s32[]{:S(2)}) async-start(), calls=%async_computation | async-start | bytes 15597568 | tf_op jit(solution)/shard_map/all_gather | solution.py:213
  10.1 4.9 %collective-permute-start.1 = (bf16[17,128,128]{2,1,0:T(8,128)(2,1)S(1)}, bf16[17,128,128]{2,1,0:T(8,128)(2,1)S(1)}, u32[]{:S(2)}, u32[]{:S(2)}) collective-permute-start(bf16[17,128,128]{2,1,0:T(8,128)(2,1)S(1)} %get-tuple-element.26), channel_id=1, source_target_pairs={{0,4},{4,0},{1,5},{5,1},{2,6},{6,2},{3,7},{7,3},{8,12},{12,8},{9,1... | collective-permute-start | bytes 1671176 | tf_op jit(solution)/shard_map/ppermute | solution.py:208
  11.5 1.6 collective-permute-start
  15.0 0.8 copy-start.4
  45.6 25.7 %collective-permute-start.2 = (bf16[128,4096]{1,0:T(8,128)(2,1)}, bf16[128,4096]{1,0:T(8,128)(2,1)S(1)}, u32[]{:S(2)}, u32[]{:S(2)}) collective-permute-start(bf16[128,4096]{1,0:T(8,128)(2,1)} %all-gather.7.cloned.1.call-done.x_own), channel_id=1, source_target_pairs={{0,4},{4,0},{1,5},{5,1},{2,6},{6,2},{3,7},{7,3},{8,12},{12,8},{9,1... | collective-permute-start | bytes 3145736 | tf_op jit(solution)/shard_map/ppermute | solution.py:216
  71.3 77.0 %copy-start.2 = (bf16[128,4096]{1,0:T(8,128)(2,1)}, bf16[128,4096]{1,0:T(8,128)(2,1)S(1)}, u32[]{:S(2)}) copy-start(bf16[128,4096]{1,0:T(8,128)(2,1)S(1)} %collective-permute-done.2.x_other) | copy-start | bytes 3145732
  174.6 4.3 %collective-permute-start.3 = (f32[128,3584]{1,0:T(8,128)}, f32[128,3584]{1,0:T(8,128)S(1)}, u32[]{:S(2)}, u32[]{:S(2)}) collective-permute-start(f32[128,3584]{1,0:T(8,128)} %get-tuple-element.15), channel_id=1, source_target_pairs={{0,4},{4,0},{1,5},{5,1},{2,6},{6,2},{3,7},{7,3},{8,12},{12,8},{9,1... | collective-permute-start | bytes 5505032 | tf_op jit(solution)/shard_map/ppermute | solution.py:218
  179.0 1.2 copy-start
  187.2 2.7 %collective-permute-start.4 = (bf16[128,3584]{1,0:T(8,128)(2,1)}, bf16[128,3584]{1,0:T(8,128)(2,1)S(1)}, u32[]{:S(2)}, u32[]{:S(2)}) collective-permute-start(bf16[128,3584]{1,0:T(8,128)(2,1)} %get-tuple-element.18), channel_id=1, source_target_pairs={{0,4},{4,0},{1,5},{5,1},{2,6},{6,2},{3,7},{7,3},{8,12},{12,8},{9,1... | collective-permute-start | bytes 2752520 | tf_op jit(solution)/shard_map/ppermute | solution.py:221
  189.9 0.9 copy-start.3
  211.5 2.9 %collective-permute-start.5 = (bf16[128,4096]{1,0:T(8,128)(2,1)}, bf16[128,4096]{1,0:T(8,128)(2,1)S(1)}, u32[]{:S(2)}, u32[]{:S(2)}) collective-permute-start(bf16[128,4096]{1,0:T(8,128)(2,1)} %get-tuple-element.21), channel_id=1, source_target_pairs={{0,4},{4,0},{1,5},{5,1},{2,6},{6,2},{3,7},{7,3},{8,12},{12,8},{9,1... | collective-permute-start | bytes 3145736 | tf_op jit(solution)/shard_map/ppermute | solution.py:223
  214.4 1.0 copy-start.1
  219.8 9.0 %collective-permute-start.6 = (bf16[32,4096]{1,0:T(8,128)(2,1)}, bf16[32,4096]{1,0:T(8,128)(2,1)S(1)}, u32[]{:S(2)}, u32[]{:S(2)}) collective-permute-start(bf16[32,4096]{1,0:T(8,128)(2,1)} %get-tuple-element.23), channel_id=1, source_target_pairs={{0,1},{1,2},{2,3},{3,0},{4,5},{5,6},{6,7},{7,4},{8,9},{9,10},{10,1... | collective-permute-start | bytes 786440 | tf_op jit(solution)/shard_map/ppermute | solution.py:226
  221.1 14.5 %collective-permute-start.7 = (bf16[32,4096]{1,0:T(8,128)(2,1)}, bf16[32,4096]{1,0:T(8,128)(2,1)S(1)}, u32[]{:S(2)}, u32[]{:S(2)}) collective-permute-start(bf16[32,4096]{1,0:T(8,128)(2,1)} %get-tuple-element.24), channel_id=1, source_target_pairs={{0,2},{1,3},{2,0},{3,1},{4,6},{5,7},{6,4},{7,5},{8,10},{9,11},{10,... | collective-permute-start | bytes 786440 | tf_op jit(solution)/shard_map/ppermute | solution.py:226
  223.7 11.9 %collective-permute-start.8 = (bf16[32,4096]{1,0:T(8,128)(2,1)}, bf16[32,4096]{1,0:T(8,128)(2,1)S(1)}, u32[]{:S(2)}, u32[]{:S(2)}) collective-permute-start(bf16[32,4096]{1,0:T(8,128)(2,1)} %get-tuple-element.25), channel_id=1, source_target_pairs={{0,3},{1,0},{2,1},{3,2},{4,7},{5,4},{6,5},{7,6},{8,11},{9,8},{10,9... | collective-permute-start | bytes 786440 | tf_op jit(solution)/shard_map/ppermute | solution.py:226
Sparse Core Ops, SparseCore 0:
  9.7 26.4 all-gather.6
  45.7 102.5 all-gather.4

commit v2 on v1

v2 whole, which is shorter than its diff:
```python
import jax
import jax.numpy as jnp
from jax import lax
from jax.experimental import pallas as pl
from jax.experimental.pallas import tpu as pltpu
from jax.sharding import Mesh, PartitionSpec as P

F32 = jnp.float32
BF16 = jnp.bfloat16
BLK = 128
CHIPS = 16
NCB = 28
CAP = 17
SURE = 11
LIVE = 28
HID = NCB * BLK
WIDTH = CHIPS * 2 * BLK
DEAD = 32 * NCB
SWAP = [(0, 1), (1, 0)]
HALF = LIVE // 2
UNIT = HALF * BLK + 16
CUT = HALF // 2 * BLK
MARK = HALF * BLK
ROWS = BLK // 4
ANY = pl.BlockSpec(memory_space=pl.ANY)
VMEM = pl.BlockSpec(memory_space=pltpu.VMEM)
SMEM = pl.BlockSpec(memory_space=pltpu.SMEM)


def params(mib=56):
    return pltpu.CompilerParams(vmem_limit_bytes=mib << 20)


def pack_kernel(scal, mine_i, theirs_i, mine, theirs, out_a, out_b):
    core, base = scal[0], scal[1]
    lane = lax.broadcasted_iota(jnp.int32, (16, BLK), 1)

    def place(j, block):
        out, at = (out_a, j) if j < HALF else (out_b, j - HALF)
        out[at * BLK : (at + 1) * BLK] = block

    def fill(first, first_i, second, second_i):
        n0 = jnp.int32(SURE)
        for j in range(SURE, CAP):
            n0 += (first_i[j] < DEAD).astype(jnp.int32)
        marks = [jnp.zeros((16, BLK), jnp.int32)] * 2
        for j in range(LIVE):
            if j < SURE:
                spot = first_i[j]
                place(j, first[j])
            elif j < CAP:
                spot = jnp.where(j < n0, first_i[j], second_i[jnp.maximum(j - n0, 0)])
                pl.when(j < n0)(lambda j=j: place(j, first[j]))
                pl.when(j >= n0)(lambda j=j: place(j, second[jnp.maximum(j - n0, 0)]))
            else:
                spot = second_i[j - n0]
                place(j, second[j - n0])
            half = j // HALF
            marks[half] = jnp.where(lane == j % HALF, spot - base, marks[half])
        out_a[MARK:UNIT] = marks[0].astype(F32).astype(BF16)
        out_b[MARK:UNIT] = marks[1].astype(F32).astype(BF16)

    pl.when(core == 0)(lambda: fill(mine, mine_i, theirs, theirs_i))
    pl.when(core != 0)(lambda: fill(theirs, theirs_i, mine, mine_i))


def pack(scal, mine_i, theirs_i, mine, theirs):
    one = jax.ShapeDtypeStruct((UNIT, BLK), BF16)
    return pl.pallas_call(
        pack_kernel,
        out_shape=(one, one),
        in_specs=[SMEM, SMEM, SMEM, VMEM, VMEM],
        out_specs=(VMEM, VMEM),
        compiler_params=params(),
        name="pack",
    )(scal, mine_i, theirs_i, mine, theirs)


def forward(units, chips, x_own, x_other, pieces, carry=None, room=None):
    count, given = len(units), len(pieces)
    room = room or count
    resumed = carry is not None

    def kernel(chip_of, xo, xt, *refs):
        parts, refs = refs[:given], refs[given:]
        if resumed:
            before, refs = refs[:2], refs[2:]
        acc_own, acc_other, panels, buf, tiles, ints, marks, panel, sem_t, sem_b, sem_m, sem_p, sem_a = refs
        moved = []
        for t, pair in enumerate(units):
            for h, source in enumerate(pair):
                part, row, rows, at = source[-1]
                mark = row + MARK - at
                tile = pltpu.make_async_copy(parts[part].at[pl.ds(mark, 16)], tiles.at[2 * t + h], sem_t.at[2 * t + h])
                tile.start()
                moved.append(tile)
        for t, pair in enumerate(units):
            for h, source in enumerate(pair):
                for part, row, rows, at in source:
                    pltpu.make_async_copy(
                        parts[part].at[pl.ds(row, rows)], buf.at[t, h, pl.ds(at, rows)], sem_b.at[t, h]
                    ).start()
        if resumed:
            loads = [pltpu.make_async_copy(b, a, sem_a.at[i]) for i, (b, a) in enumerate(zip(before, (acc_own, acc_other)))]
            for m in loads:
                m.start()
        else:
            acc_own[...] = jnp.zeros_like(acc_own)
            acc_other[...] = jnp.zeros_like(acc_other)
        for i, m in enumerate(moved):
            m.wait()
            ints[pl.ds(i, 1), :] = tiles[i].astype(F32)[0:1].astype(jnp.int32)
        load = pltpu.make_async_copy(ints, marks, sem_m)
        load.start()
        load.wait()
        if resumed:
            for m in loads:
                m.wait()

        def stored(slot):
            return pltpu.make_async_copy(panel.at[slot], panels.at[0], sem_p.at[slot])

        def step(t, _):
            slot = t % 2
            for h in range(2):
                pltpu.make_async_copy(buf.at[t, h], buf.at[t, h], sem_b.at[t, h]).wait()
            pl.when(t >= 2)(lambda: stored(slot).wait())
            panel[slot] = jnp.zeros((NCB, 2 * BLK, BLK), BF16)
            for j in range(LIVE):
                h, k = divmod(j, HALF)
                pos = marks[2 * t + h, k]
                low = (pos >= NCB).astype(jnp.int32)
                panel[slot, pos - low * NCB, pl.ds(pl.multiple_of(low * BLK, BLK), BLK), :] = buf[t, h, k * BLK : (k + 1) * BLK]
            pltpu.make_async_copy(panel.at[slot], panels.at[room - count + t], sem_p.at[slot]).start()
            cols = pl.ds(pl.multiple_of(chip_of[t] * 2 * BLK, 2 * BLK), 2 * BLK)
            x = jnp.concatenate([xo[:, cols], xt[:, cols]], axis=0)
            for c in range(NCB // 2):
                w = jnp.concatenate([panel[slot, 2 * c], panel[slot, 2 * c + 1]], axis=1)
                r = jnp.dot(x, w, preferred_element_type=F32)
                at = pl.ds(c * 2 * BLK, 2 * BLK)
                acc_own[:, at] += r[:BLK]
                acc_other[:, at] += r[BLK:]
            return 0

        lax.fori_loop(0, count, step, 0)
        for t in range(max(0, count - 2), count):
            stored(t % 2).wait()

    extra = list(carry) if resumed else []
    alias = {3 + given + 2: 2} if resumed and len(extra) == 3 else {}
    acc = jax.ShapeDtypeStruct((BLK, HID), F32)
    wrapped = kernel
    if alias:
        def wrapped(*refs):
            kernel(*refs[: 3 + given + 2], *refs[3 + given + 3 :])
    return pl.pallas_call(
        wrapped,
        out_shape=(acc, acc, jax.ShapeDtypeStruct((room, NCB, 2 * BLK, BLK), BF16)),
        in_specs=[SMEM, VMEM, VMEM] + [ANY] * (given + len(extra)),
        out_specs=(VMEM, VMEM, ANY),
        scratch_shapes=[
            pltpu.VMEM((count, 2, UNIT, BLK), BF16),
            pltpu.VMEM((2 * count, 16, BLK), BF16),
            pltpu.VMEM((2 * count, BLK), jnp.int32),
            pltpu.SMEM((2 * count, BLK), jnp.int32),
            pltpu.VMEM((2, NCB, 2 * BLK, BLK), BF16),
            pltpu.SemaphoreType.DMA((2 * count,)),
            pltpu.SemaphoreType.DMA((count, 2)),
            pltpu.SemaphoreType.DMA,
            pltpu.SemaphoreType.DMA((2,)),
            pltpu.SemaphoreType.DMA((2,)),
        ],
        input_output_aliases=alias,
        compiler_params=params(),
        name="forward",
    )(chips, x_own, x_other, *pieces, *extra)


def act_kernel(scal, mine, got, d_hidden, hidden, d_mine, d_send):
    def work(gate_ref, up_ref, d_gate, d_up):
        for k in range(4):
            rel = pl.ds(k * ROWS, ROWS)
            real = pl.ds(pl.multiple_of((scal[1] - k + 4) % 4 * ROWS, ROWS), ROWS)
            gate, up = gate_ref[rel, :], up_ref[rel, :]
            d = d_hidden[real, :].astype(F32)
            sig = jax.nn.sigmoid(gate)
            active = gate * sig
            hidden[real, :] = (active * up).astype(BF16)
            d_gate[rel, :] = (d * up * sig * (1.0 + gate * (1.0 - sig))).astype(BF16)
            d_up[rel, :] = (d * active).astype(BF16)

    pl.when(scal[0] == 0)(lambda: work(mine, got, d_mine, d_send))
    pl.when(scal[0] != 0)(lambda: work(got, mine, d_send, d_mine))


def activate(scal, mine, got, d_hidden):
    steps = 7
    spec = pl.BlockSpec((BLK, HID // steps), lambda i, s: (0, i))
    one = jax.ShapeDtypeStruct((BLK, HID), BF16)
    return pl.pallas_call(
        act_kernel,
        out_shape=(one, one, one),
        grid_spec=pltpu.PrefetchScalarGridSpec(
            num_scalar_prefetch=1, grid=(steps,), in_specs=[spec] * 3, out_specs=[spec] * 3
        ),
        compiler_params=params(),
        name="activate",
    )(scal, mine, got, d_hidden)


def bwd_kernel(d_own, d_other, panel, out_own, out_other, both):
    @pl.when(pl.program_id(0) == 0)
    def _():
        both[:BLK] = d_own[...]
        both[BLK:] = d_other[...]

    w = jnp.concatenate([panel[0, c] for c in range(NCB)], axis=1)
    r = lax.dot_general(both[...], w, (((1,), (1,)), ((), ())), preferred_element_type=F32)
    out_own[...] = r[:BLK]
    out_other[...] = r[BLK:].astype(BF16)


def backward(d_own, d_other, panels):
    whole = pl.BlockSpec((BLK, HID), lambda q: (0, 0))
    count = panels.shape[0]
    width = count * 2 * BLK
    return pl.pallas_call(
        bwd_kernel,
        out_shape=(jax.ShapeDtypeStruct((BLK, width), F32), jax.ShapeDtypeStruct((BLK, width), BF16)),
        grid=(count,),
        in_specs=[whole, whole, pl.BlockSpec((1, NCB, 2 * BLK, BLK), lambda q: (q, 0, 0, 0))],
        out_specs=[pl.BlockSpec((BLK, 2 * BLK), lambda q: (0, q))] * 2,
        scratch_shapes=[pltpu.VMEM((2 * BLK, HID), BF16)],
        compiler_params=params(),
        name="backward",
    )(d_own, d_other, panels)


def join_kernel(own, got, keep, *sends):
    for k in range(4):
        at = slice(k * ROWS, (k + 1) * ROWS)
        total = own[at, :] + got[at, :].astype(F32)
        if k:
            sends[k - 1][...] = total.astype(BF16)
        else:
            keep[...] = total


def join(own, got):
    cols = own.shape[1]
    return pl.pallas_call(
        join_kernel,
        out_shape=(jax.ShapeDtypeStruct((ROWS, cols), F32),) + (jax.ShapeDtypeStruct((ROWS, cols), BF16),) * 3,
        in_specs=[VMEM, VMEM],
        out_specs=(VMEM,) * 4,
        compiler_params=params(),
        name="join",
    )(own, got)


def finish(chips, groups):
    def kernel(chip_of, *refs):
        out, t = refs[-1], 0
        for g in range(len(groups)):
            parts = refs[4 * g : 4 * g + 4]
            for i in range(parts[0].shape[1] // (2 * BLK)):
                at = slice(i * 2 * BLK, (i + 1) * 2 * BLK)
                total = parts[0][:, at]
                for p in parts[1:]:
                    total += p[:, at].astype(F32)
                out[:, pl.ds(pl.multiple_of(chip_of[t] * 2 * BLK, 2 * BLK), 2 * BLK)] = total.astype(BF16)
                t += 1

    flat = [a for g in groups for a in g]
    return pl.pallas_call(
        kernel,
        out_shape=jax.ShapeDtypeStruct((ROWS, WIDTH), BF16),
        in_specs=[SMEM] + [VMEM] * len(flat),
        out_specs=VMEM,
        compiler_params=params(),
        name="finish",
    )(chips, *flat)


def shift(a, axis, by):
    return lax.ppermute(a, axis, [(i, (i + by) % 4) for i in range(4)])


def shards(tokens, gate_blocks, gate_index, up_blocks, up_index, d_hidden):
    x, y, core, z = (lax.axis_index(n) for n in ("x", "y", "c", "z"))
    first = core == 0
    gate_i, up_i = gate_index[0], up_index[0]
    theirs = lax.ppermute(jnp.where(first, up_blocks[0], gate_blocks[0]), "c", SWAP)
    theirs_i = lax.ppermute(jnp.where(first, up_i, gate_i), "c", SWAP)
    mine = jnp.where(first, gate_blocks[0], up_blocks[0])
    mine_i = jnp.where(first, gate_i, up_i)
    scal = jnp.stack([core, z, (x * 4 + y) * 2 * NCB])
    a, b = pack(scal[0::2], mine_i, theirs_i, mine, theirs)

    line = {}
    for name, unit, near in (("a", a, "x"), ("b", b, "y")):
        line[name] = [unit, shift(unit, near, 1), shift(unit, near, -1), shift(unit, near, 2)]
    x_own = jnp.concatenate([tokens] + [shift(tokens, "z", k) for k in (1, 2, 3)], axis=0)
    x_other = lax.ppermute(x_own, "c", SWAP)
    three, far = {}, {}
    for name, across in (("a", "y"), ("b", "x")):
        u = line[name]
        own3 = jnp.concatenate(u[:3], axis=0)
        three[name] = [None, shift(own3, across, 1), shift(own3, across, -1)]
        far[name] = [u[3], shift(u[3], across, 1), shift(u[3], across, -1)]
    middle = UNIT + CUT
    three2, far2 = {}, {}
    for name, across in (("a", "y"), ("b", "x")):
        t, f = three[name], far[name]
        three2[name] = (shift(t[1][:middle], across, 1), shift(t[2][middle:], across, -1))
        far2[name] = (shift(f[1][:CUT], across, 1), shift(f[2][CUT:], across, -1))

    def source(name, near, across):
        if across == 0:
            return [(line[name][near], 0, UNIT, 0)]
        if across < 3 and near < 3:
            return [(three[name][across], near * UNIT, UNIT, 0)]
        if across < 3:
            return [(far[name][across], 0, UNIT, 0)]
        if near == 3:
            low, high = far2[name]
            return [(low, 0, CUT, 0), (high, 0, UNIT - CUT, CUT)]
        low, high = three2[name]
        if near == 0:
            return [(low, 0, UNIT, 0)]
        if near == 2:
            return [(high, UNIT - CUT, UNIT, 0)]
        return [(low, UNIT, CUT, 0), (high, 0, UNIT - CUT, CUT)]

    step = (0, -1, 1, 2)
    near9 = [(i, j) for i in range(3) for j in range(3)]
    last6 = [(3, 0), (3, 1), (3, 2), (0, 3), (1, 3), (2, 3)]
    order = near9 + last6 + [(3, 3)]
    chips = jnp.stack([(x + step[i]) % 4 * 4 + (y + step[j]) % 4 for i, j in order])

    def stage(which, at, carry=None, room=None):
        pieces, units = [], []
        for i, j in which:
            pair = []
            for src in (source("a", i, j), source("b", j, i)):
                row = []
                for piece, r, n, d in src:
                    k = next((m for m, p in enumerate(pieces) if p is piece), None)
                    if k is None:
                        k = len(pieces)
                        pieces.append(piece)
                    row.append((k, r, n, d))
                pair.append(row)
            units.append(pair)
        return forward(units, chips[at : at + len(which)], x_own, x_other, pieces, carry, room)

    acc_own, acc_other, panels9 = stage(near9, 0)
    acc_own, acc_other, panels7 = stage(last6, 9, (acc_own, acc_other), None)
    acc_own, acc_other, panels1 = stage([(3, 3)], 15, (acc_own, acc_other), None)
    got = lax.ppermute(acc_other, "c", SWAP)
    hidden, d_mine, d_send = activate(scal[:2], acc_own, got, d_hidden)
    d_other = lax.ppermute(d_send, "c", SWAP)
    groups = []
    for panels in (panels9, panels7, panels1):
        part_own, part_other = backward(d_mine, d_other, panels)
        keep, *sends = join(part_own, lax.ppermute(part_other, "c", SWAP))
        groups.append([keep] + [shift(s, "z", -k - 1) for k, s in enumerate(sends)])
    return hidden, finish(chips, groups)

def solution(mesh):
    fine = Mesh(mesh.devices.reshape(4, 4, 2, 4), ("x", "y", "c", "z"))
    fsdp = ("x", "y", "c")
    every = P((*fsdp, "z"), None)
    in_specs = (every, P("z", fsdp, None, None), P("z", fsdp), P("z", fsdp, None, None), P("z", fsdp), P(fsdp, "z"))
    return jax.shard_map(shards, mesh=fine, in_specs=in_specs, out_specs=(P(fsdp, "z"), every), check_vma=False)
```

time: 246 us -> 247 us (level)
  starting transfers between devices: 8.43 us -> 46.1 us
  blocking collectives: 24.5 us -> 0 us
  between operations: 14.1 us -> 1.19 us
  local copies, waits for them, and re-layouts: 4.65 us -> 15.6 us
  Pallas kernels: 88.2 us -> 80.4 us
  other arithmetic: 6.51 us -> 3.28 us
    ppermute x4 -> x37, waiting for transfers between devices: 13.3 us -> 91.6 us  [the longest x34 91.6 us: shift(): return lax.ppermute(a, axis, [(i, (i + by) % 4) for i in range(4)])]
    all_gather x2 -> x0, waiting for transfers between devices: 77 us -> none  [the longest x1 77 us: shards(): blocks = lax.all_gather(payload, ('x', 'y'), axis=0, tiled=True)]
    ppermute x4 -> x37, starting transfers between devices: 5.35 us -> 39.4 us  [the longest x34 38.5 us: shift(): return lax.ppermute(a, axis, [(i, (i + by) % 4) for i in range(4)])]
    all_gather x1 -> x0, blocking collectives: 24.5 us -> none  [shards(): lax.all_gather(jnp.stack([gate_i, up_i]), ('x', 'y', 'c'), axis=0)]
    pallas_call x4 -> x11, Pallas kernels: 81.2 us -> 73.4 us  [the longest x3 38.3 us: forward(): pl.pallas_call(wrapped, out_shape=(acc, acc, jax.ShapeDtypeStruct((room,...]
    unnamed x14 -> x97, local copies, waits for them, and re-layouts: 3.98 us -> 9.84 us
    slice x0 -> x9, local copies, waits for them, and re-layouts: none -> 3.67 us  [the longest x4 2.89 us: shards(): far2[name] = (shift(f[1][:CUT], across, 1), shift(f[2][CUT:], across, -1))]
  transfers between devices with their start and end apart: 11 -> 42, of which waited for: 7 -> 13; matrix products, arithmetic and copies ran while one was open for 2% -> 5% of each run, Pallas kernels for 12% -> 21%
where the time goes in v2:
time: 247 us; the launch traced here: 243 us
  waiting for transfers between devices  96.9 us (39%)
  Pallas kernels  80.4 us (33%)
  starting transfers between devices  46.1 us (19%)
  local copies, waits for them, and re-layouts  15.6 us (6%)
  other arithmetic  3.28 us (1%)
    ppermute x34, waiting for transfers between devices, shift(): return lax.ppermute(a, axis, [(i, (i + by) % 4) for i in range(4)])  91.6 us
    ppermute x34, starting transfers between devices, shift(): return lax.ppermute(a, axis, [(i, (i + by) % 4) for i in range(4)])  38.5 us
    pallas_call x3, Pallas kernels, forward(): pl.pallas_call(wrapped, out_shape=(acc, acc, jax.ShapeDtypeStruct((room,...  38.3 us
    pallas_call x3, Pallas kernels, backward(): pl.pallas_call(bwd_kernel, out_shape=(jax.ShapeDtypeStruct((BLK, width),...  24.8 us
    unnamed x97, local copies, waits for them, and re-layouts  9.84 us
    pallas_call x1, Pallas kernels, activate(): pl.pallas_call(act_kernel, out_shape=(one, one, one), grid_spec=pltpu.Pre...  7.03 us
    pallas_call x3, Pallas kernels, join(): pl.pallas_call(join_kernel, out_shape=(jax.ShapeDtypeStruct((ROWS, cols),...  5.86 us
  transfers between devices with their start and end apart: 42, of which 13 were waited for; matrix products, arithmetic and copies ran while one was open for 5% of the time, Pallas kernels for 21%

profile of v2, /device:TPU:1, one launch (start us, length us, event | category | flops | bytes accessed | tf_op | source)
XLA Modules:
  0.0 243.5 jit_solution(199022078415890332)
XLA Ops:
  0.7 2.5 %collective-permute-start = (bf16[32,4096]{1,0:T(8,128)(2,1)}, bf16[32,4096]{1,0:T(8,128)(2,1)S(1)}, u32[]{:S(2)}, u32[]{:S(2)}) collective-permute-start(bf16[32,4096]{1,0:T(8,128)(2,1)} %param.6), channel_id=1, source_target_pairs={{0,1},{1,2},{2,3},{3,0},{4,5},{5,6},{6,7},{7,4},{8,9},{9,10},{10,1... | collective-permute-start | bytes 786440 | tf_op jit(solution)/shard_map/ppermute | solution.py:286
  3.2 3.3 %collective-permute-start.1 = (bf16[32,4096]{1,0:T(8,128)(2,1)}, bf16[32,4096]{1,0:T(8,128)(2,1)S(1)}, u32[]{:S(2)}, u32[]{:S(2)}) collective-permute-start(bf16[32,4096]{1,0:T(8,128)(2,1)} %param.6), channel_id=1, source_target_pairs={{0,2},{1,3},{2,0},{3,1},{4,6},{5,7},{6,4},{7,5},{8,10},{9,11},{10,... | collective-permute-start | bytes 786440 | tf_op jit(solution)/shard_map/ppermute | solution.py:286
  7.2 2.1 select_bitcast_fusion
  12.1 5.9 %collective-permute-done.1 = bf16[32,4096]{1,0:T(8,128)(2,1)S(1)} collective-permute-done((bf16[32,4096]{1,0:T(8,128)(2,1)}, bf16[32,4096]{1,0:T(8,128)(2,1)S(1)}, u32[]{:S(2)}, u32[]{:S(2)}) %collective-permute-start.1) | collective-permute-done | bytes 262176 | tf_op jit(solution)/shard_map/ppermute | solution.py:286
  20.5 2.3 pack.1
  30.4 6.1 %collective-permute-done.16.refs_3_ = bf16[1808,128]{1,0:T(8,128)(2,1)S(1)} collective-permute-done((bf16[1808,128]{1,0:T(8,128)(2,1)}, bf16[1808,128]{1,0:T(8,128)(2,1)S(1)}, u32[]{:S(2)}, u32[]{:S(2)}) %collective-permute-start.16) | collective-permute-done | bytes 462880 | tf_op jit(solution)/shard_map/ppermute | solution.py:286
  38.1 2.8 %collective-permute-start.6 = (bf16[1808,128]{1,0:T(8,128)(2,1)S(1)}, bf16[1808,128]{1,0:T(8,128)(2,1)S(1)}, u32[]{:S(2)}, u32[]{:S(2)}) collective-permute-start(bf16[1808,128]{1,0:T(8,128)(2,1)S(1)} %copy-done.7), channel_id=1, source_target_pairs={{0,64},{32,96},{64,0},{96,32},{1,65},{33,97},{65,1},{97,33},{2,66}... | collective-permute-start | bytes 1388552 | tf_op jit(solution)/shard_map/ppermute | solution.py:286
  41.4 2.4 collective-permute-start.20
  43.9 5.4 %collective-permute-done.11.refs_6_ = bf16[1808,128]{1,0:T(8,128)(2,1)S(1)} collective-permute-done((bf16[1808,128]{1,0:T(8,128)(2,1)S(1)}, bf16[1808,128]{1,0:T(8,128)(2,1)S(1)}, u32[]{:S(2)}, u32[]{:S(2)}) %collective-permute-start.11) | collective-permute-done | bytes 462880 | tf_op jit(solution)/shard_map/ppermute | solution.py:286
  53.3 28.6 %collective-permute-done.18.refs_7_ = bf16[5424,128]{1,0:T(8,128)(2,1)S(1)} collective-permute-done((bf16[5424,128]{1,0:T(8,128)(2,1)S(1)}, bf16[5424,128]{1,0:T(8,128)(2,1)S(1)}, u32[]{:S(2)}, u32[]{:S(2)}) %collective-permute-start.18) | collective-permute-done | bytes 1388576 | tf_op jit(solution)/shard_map/ppermute | solution.py:286
  83.3 8.5 %collective-permute-done.12.refs_8_ = bf16[1808,128]{1,0:T(8,128)(2,1)S(1)} collective-permute-done((bf16[1808,128]{1,0:T(8,128)(2,1)S(1)}, bf16[1808,128]{1,0:T(8,128)(2,1)S(1)}, u32[]{:S(2)}, u32[]{:S(2)}) %collective-permute-start.12) | collective-permute-done | bytes 462880 | tf_op jit(solution)/shard_map/ppermute | solution.py:286
  93.9 2.3 collective-permute-start.27
  97.8 22.8 %collective-permute-done.7.refs_2_ = bf16[1808,128]{1,0:T(8,128)(2,1)S(1)} collective-permute-done((bf16[1808,128]{1,0:T(8,128)(2,1)S(1)}, bf16[1808,128]{1,0:T(8,128)(2,1)S(1)}, u32[]{:S(2)}, u32[]{:S(2)}) %collective-permute-start.7) | collective-permute-done | bytes 462880 | tf_op jit(solution)/shard_map/ppermute | solution.py:286
  126.6 16.9 %forward.3 = (f32[128,3584]{1,0:T(8,128)}, f32[128,3584]{1,0:T(8,128)}, bf16[9,28,256,128]{3,2,1,0:T(8,128)(2,1)}) custom-call(s32[9]{0:T(128)} %stack.91.chip_of, bf16[128,4096]{1,0:T(8,128)(2,1)} %copy-done, bf16[128,4096]{1,0:T(8,128)(2,1)} %copy-done.1, bf16[1808,128]{1,0:T(8,128)(2,1)} %get-tuple-element.34.refs_0_, ...), custom_call_target="tpu_custom_call" | custom-call | tf_op jit(solution)/shard_map/forward/pallas_call | solution.py:156
  144.4 13.8 %forward.4 = (f32[128,3584]{1,0:T(8,128)}, f32[128,3584]{1,0:T(8,128)}, bf16[6,28,256,128]{3,2,1,0:T(8,128)(2,1)}) custom-call(s32[6]{0:T(128)} %stack.81.chip_of, bf16[128,4096]{1,0:T(8,128)(2,1)} %copy-done, bf16[128,4096]{1,0:T(8,128)(2,1)} %copy-done.1, bf16[1808,128]{1,0:T(8,128)(2,1)} %copy-done.25, bf16[2704,128]{1,0:T(8,128)(2,1)} %copy-done.20, ...), custom_call_target="tpu_custom_call" | custom-call | tf_op jit(solution)/shard_map/forward/pallas_call | solution.py:156
  158.3 7.6 %forward.5 = (f32[128,3584]{1,0:T(8,128)}, f32[128,3584]{1,0:T(8,128)}, bf16[1,28,256,128]{3,2,1,0:T(8,128)(2,1)}) custom-call(s32[1]{0:T(128)} %bitcast.2.chip_of, bf16[128,4096]{1,0:T(8,128)(2,1)} %copy-done, bf16[128,4096]{1,0:T(8,128)(2,1)} %copy-done.1, bf16[896,128]{1,0:T(8,128)(2,1)} %collective-permute-done.8.refs_0_, ...), custom_call_target="tpu_custom_call" | custom-call | tf_op jit(solution)/shard_map/forward/pallas_call | solution.py:156
  165.9 3.1 %collective-permute-start.28 = (f32[128,3584]{1,0:T(8,128)}, f32[128,3584]{1,0:T(8,128)S(1)}, u32[]{:S(2)}, u32[]{:S(2)}) collective-permute-start(f32[128,3584]{1,0:T(8,128)} %get-tuple-element.41), channel_id=1, source_target_pairs={{0,4},{4,0},{1,5},{5,1},{2,6},{6,2},{3,7},{7,3},{8,12},{12,8},{9,1... | collective-permute-start | bytes 5505032 | tf_op jit(solution)/shard_map/ppermute | solution.py:360
  169.6 3.0 %collective-permute-done.28.got = f32[128,3584]{1,0:T(8,128)S(1)} collective-permute-done((f32[128,3584]{1,0:T(8,128)}, f32[128,3584]{1,0:T(8,128)S(1)}, u32[]{:S(2)}, u32[]{:S(2)}) %collective-permute-start.28) | collective-permute-done | bytes 1835040 | tf_op jit(solution)/shard_map/ppermute | solution.py:360
  173.9 7.0 %activate.1 = (bf16[128,3584]{1,0:T(8,128)(2,1)}, bf16[128,3584]{1,0:T(8,128)(2,1)}, bf16[128,3584]{1,0:T(8,128)(2,1)}) custom-call(s32[2]{0:T(128)} %pad_add_fusion.scal, f32[128,3584]{1,0:T(8,128)} %get-tuple-element.40.mine, f32[128,3584]{1,0:T(8,128)} %copy-done.13, bf16[128,3584]{1,0:T(8,128)(2,1)} %d_hidden.1), custom_call_target="tpu_custom_call" | custom-call | tf_op jit(solution)/shard_map/activate/pallas_call | solution.py:200
  181.3 2.3 collective-permute-done.29.d_other
  184.6 12.5 %backward.3 = (f32[128,2304]{1,0:T(8,128)}, bf16[128,2304]{1,0:T(8,128)(2,1)}) custom-call(bf16[128,3584]{1,0:T(8,128)(2,1)} %get-tuple-element.43.d_own, bf16[128,3584]{1,0:T(8,128)(2,1)} %copy-done.2, bf16[9,28,256,128]{3,2,1,0:T(8,128)(2,1)} %get-tuple-element.45.panel), custom_call_target="tpu_custom_call" | custom-call | tf_op jit(solution)/shard_map/backward/pallas_call | solution.py:227
  197.5 8.9 %backward.4 = (f32[128,1536]{1,0:T(8,128)}, bf16[128,1536]{1,0:T(8,128)(2,1)}) custom-call(bf16[128,3584]{1,0:T(8,128)(2,1)} %get-tuple-element.43.d_own, bf16[128,3584]{1,0:T(8,128)(2,1)} %copy-done.2, bf16[6,28,256,128]{3,2,1,0:T(8,128)(2,1)} %get-tuple-element.52.panel), custom_call_target="tpu_custom_call" | custom-call | tf_op jit(solution)/shard_map/backward/pallas_call | solution.py:227
  206.5 3.4 %backward.5 = (f32[128,256]{1,0:T(8,128)}, bf16[128,256]{1,0:T(8,128)(2,1)}) custom-call(bf16[128,3584]{1,0:T(8,128)(2,1)} %get-tuple-element.43.d_own, bf16[128,3584]{1,0:T(8,128)(2,1)} %copy-done.2, bf16[1,28,256,128]{3,2,1,0:T(8,128)(2,1)} %get-tuple-element.59.panel), custom_call_target="tpu_custom_call" | custom-call | tf_op jit(solution)/shard_map/backward/pallas_call | solution.py:227
  211.0 2.0 join.4
  213.0 1.9 collective-permute-start.35
  218.3 2.3 join.3
  221.4 2.1 collective-permute-start.32
  223.5 2.2 collective-permute-start.40
  225.7 4.9 %collective-permute-done.40.refs_10_ = bf16[32,256]{1,0:T(8,128)(2,1)S(1)} collective-permute-done((bf16[32,256]{1,0:T(8,128)(2,1)S(1)}, bf16[32,256]{1,0:T(8,128)(2,1)S(1)}, u32[]{:S(2)}, u32[]{:S(2)}) %collective-permute-start.40) | collective-permute-done | bytes 16416 | tf_op jit(solution)/shard_map/ppermute | solution.py:286
  230.7 3.8 %collective-permute-done.41.refs_11_ = bf16[32,256]{1,0:T(8,128)(2,1)S(1)} collective-permute-done((bf16[32,256]{1,0:T(8,128)(2,1)S(1)}, bf16[32,256]{1,0:T(8,128)(2,1)S(1)}, u32[]{:S(2)}, u32[]{:S(2)}) %collective-permute-start.41) | collective-permute-done | bytes 16416 | tf_op jit(solution)/shard_map/ppermute | solution.py:286
  236.2 3.3 %collective-permute-done.36.refs_6_ = bf16[32,1536]{1,0:T(8,128)(2,1)S(1)} collective-permute-done((bf16[32,1536]{1,0:T(8,128)(2,1)S(1)}, bf16[32,1536]{1,0:T(8,128)(2,1)S(1)}, u32[]{:S(2)}, u32[]{:S(2)}) %collective-permute-start.36) | collective-permute-done | bytes 98336 | tf_op jit(solution)/shard_map/ppermute | solution.py:286
  241.3 2.2 finish.1
  (180 shorter events, 43.8 us)
Async XLA Ops:
  0.7 11.4 %collective-permute-start = (bf16[32,4096]{1,0:T(8,128)(2,1)}, bf16[32,4096]{1,0:T(8,128)(2,1)S(1)}, u32[]{:S(2)}, u32[]{:S(2)}) collective-permute-start(bf16[32,4096]{1,0:T(8,128)(2,1)} %param.6), channel_id=1, source_target_pairs={{0,1},{1,2},{2,3},{3,0},{4,5},{5,6},{6,7},{7,4},{8,9},{9,10},{10,1... | collective-permute-start | bytes 786440 | tf_op jit(solution)/shard_map/ppermute | solution.py:286
  3.2 14.8 %collective-permute-start.1 = (bf16[32,4096]{1,0:T(8,128)(2,1)}, bf16[32,4096]{1,0:T(8,128)(2,1)S(1)}, u32[]{:S(2)}, u32[]{:S(2)}) collective-permute-start(bf16[32,4096]{1,0:T(8,128)(2,1)} %param.6), channel_id=1, source_target_pairs={{0,2},{1,3},{2,0},{3,1},{4,6},{5,7},{6,4},{7,5},{8,10},{9,11},{10,... | collective-permute-start | bytes 786440 | tf_op jit(solution)/shard_map/ppermute | solution.py:286
  6.5 11.6 %collective-permute-start.2 = (bf16[32,4096]{1,0:T(8,128)(2,1)}, bf16[32,4096]{1,0:T(8,128)(2,1)S(1)}, u32[]{:S(2)}, u32[]{:S(2)}) collective-permute-start(bf16[32,4096]{1,0:T(8,128)(2,1)} %param.6), channel_id=1, source_target_pairs={{0,3},{1,0},{2,1},{3,2},{4,7},{5,4},{6,5},{7,6},{8,11},{9,8},{10,9... | collective-permute-start | bytes 786440 | tf_op jit(solution)/shard_map/ppermute | solution.py:286
  9.3 10.4 %collective-permute-start.5 = (bf16[17,128,128]{2,1,0:T(8,128)(2,1)S(1)}, bf16[17,128,128]{2,1,0:T(8,128)(2,1)S(1)}, u32[]{:S(2)}, u32[]{:S(2)}) collective-permute-start(bf16[17,128,128]{2,1,0:T(8,128)(2,1)S(1)} %get-tuple-element.66), channel_id=1, source_target_pairs={{0,4},{4,0},{1,5},{5,1},{2,6},{6,2},{3,7},{7,3},{8,12},{12,8},{9,1... | collective-permute-start | bytes 1671176 | tf_op jit(solution)/shard_map/ppermute | solution.py:293
  18.1 34.0 %collective-permute-start.3 = (bf16[128,4096]{1,0:T(8,128)(2,1)S(1)}, bf16[128,4096]{1,0:T(8,128)(2,1)S(1)}, u32[]{:S(2)}, u32[]{:S(2)}) collective-permute-start(bf16[128,4096]{1,0:T(8,128)(2,1)S(1)} %constant_dynamic-update-slice_fusion.xo), channel_id=1, source_target_pairs={{0,4},{4,0},{1,5},{5,1},{2,6},{6,2},{3,7},{7,3},{8,12},{12,8},{9,1... | collective-permute-start | bytes 3145736 | tf_op jit(solution)/shard_map/ppermute | solution.py:304
  22.8 13.7 %collective-permute-start.16 = (bf16[1808,128]{1,0:T(8,128)(2,1)}, bf16[1808,128]{1,0:T(8,128)(2,1)S(1)}, u32[]{:S(2)}, u32[]{:S(2)}) collective-permute-start(bf16[1808,128]{1,0:T(8,128)(2,1)} %get-tuple-element.35.refs_1_), channel_id=1, source_target_pairs={{0,8},{8,16},{16,24},{24,0},{1,9},{9,17},{17,25},{25,1},{2,10},{10... | collective-permute-start | bytes 1388552 | tf_op jit(solution)/shard_map/ppermute | solution.py:286
  24.1 13.9 %collective-permute-start.17 = (bf16[1808,128]{1,0:T(8,128)(2,1)}, bf16[1808,128]{1,0:T(8,128)(2,1)S(1)}, u32[]{:S(2)}, u32[]{:S(2)}) collective-permute-start(bf16[1808,128]{1,0:T(8,128)(2,1)} %get-tuple-element.35.refs_1_), channel_id=1, source_target_pairs={{0,24},{8,0},{16,8},{24,16},{1,25},{9,1},{17,9},{25,17},{2,26},{10... | collective-permute-start | bytes 1388552 | tf_op jit(solution)/shard_map/ppermute | solution.py:286
  25.6 15.3 %collective-permute-start.22 = (bf16[1808,128]{1,0:T(8,128)(2,1)}, bf16[1808,128]{1,0:T(8,128)(2,1)S(1)}, u32[]{:S(2)}, u32[]{:S(2)}) collective-permute-start(bf16[1808,128]{1,0:T(8,128)(2,1)} %get-tuple-element.34.refs_0_), channel_id=1, source_target_pairs={{0,32},{32,64},{64,96},{96,0},{1,33},{33,65},{65,97},{97,1},{2,34}... | collective-permute-start | bytes 1388552 | tf_op jit(solution)/shard_map/ppermute | solution.py:286
  26.8 14.6 %collective-permute-start.23 = (bf16[1808,128]{1,0:T(8,128)(2,1)}, bf16[1808,128]{1,0:T(8,128)(2,1)S(1)}, u32[]{:S(2)}, u32[]{:S(2)}) collective-permute-start(bf16[1808,128]{1,0:T(8,128)(2,1)} %get-tuple-element.34.refs_0_), channel_id=1, source_target_pairs={{0,96},{32,0},{64,32},{96,64},{1,97},{33,1},{65,33},{97,65},{2,98}... | collective-permute-start | bytes 1388552 | tf_op jit(solution)/shard_map/ppermute | solution.py:286
  36.5 12.8 %collective-permute-start.11 = (bf16[1808,128]{1,0:T(8,128)(2,1)S(1)}, bf16[1808,128]{1,0:T(8,128)(2,1)S(1)}, u32[]{:S(2)}, u32[]{:S(2)}) collective-permute-start(bf16[1808,128]{1,0:T(8,128)(2,1)S(1)} %copy-done.8), channel_id=1, source_target_pairs={{0,16},{8,24},{16,0},{24,8},{1,17},{9,25},{17,1},{25,9},{2,18},{10... | collective-permute-start | bytes 1388552 | tf_op jit(solution)/shard_map/ppermute | solution.py:286
  38.1 12.4 %collective-permute-start.6 = (bf16[1808,128]{1,0:T(8,128)(2,1)S(1)}, bf16[1808,128]{1,0:T(8,128)(2,1)S(1)}, u32[]{:S(2)}, u32[]{:S(2)}) collective-permute-start(bf16[1808,128]{1,0:T(8,128)(2,1)S(1)} %copy-done.7), channel_id=1, source_target_pairs={{0,64},{32,96},{64,0},{96,32},{1,65},{33,97},{65,1},{97,33},{2,66}... | collective-permute-start | bytes 1388552 | tf_op jit(solution)/shard_map/ppermute | solution.py:286
  41.0 41.0 %collective-permute-start.18 = (bf16[5424,128]{1,0:T(8,128)(2,1)S(1)}, bf16[5424,128]{1,0:T(8,128)(2,1)S(1)}, u32[]{:S(2)}, u32[]{:S(2)}) collective-permute-start(bf16[5424,128]{1,0:T(8,128)(2,1)S(1)} %constant_dynamic-update-slice_fusion.4), channel_id=1, source_target_pairs={{0,32},{32,64},{64,96},{96,0},{1,33},{33,65},{65,97},{97,1},{2,34}... | collective-permute-start | bytes 4165640 | tf_op jit(solution)/shard_map/ppermute | solution.py:286
  41.4 40.5 %collective-permute-start.20 = (bf16[5424,128]{1,0:T(8,128)(2,1)S(1)}, bf16[5424,128]{1,0:T(8,128)(2,1)S(1)}, u32[]{:S(2)}, u32[]{:S(2)}) collective-permute-start(bf16[5424,128]{1,0:T(8,128)(2,1)S(1)} %constant_dynamic-update-slice_fusion.4), channel_id=1, source_target_pairs={{0,96},{32,0},{64,32},{96,64},{1,97},{33,1},{65,33},{97,65},{2,98}... | collective-permute-start | bytes 4165640 | tf_op jit(solution)/shard_map/ppermute | solution.py:286
  49.3 42.5 %collective-permute-start.24 = (bf16[5424,128]{1,0:T(8,128)(2,1)S(1)}, bf16[5424,128]{1,0:T(8,128)(2,1)S(1)}, u32[]{:S(2)}, u32[]{:S(2)}) collective-permute-start(bf16[5424,128]{1,0:T(8,128)(2,1)S(1)} %constant_dynamic-update-slice_fusion.7), channel_id=1, source_target_pairs={{0,8},{8,16},{16,24},{24,0},{1,9},{9,17},{17,25},{25,1},{2,10},{10... | collective-permute-start | bytes 4165640 | tf_op jit(solution)/shard_map/ppermute | solution.py:286
  50.5 42.9 %collective-permute-start.26 = (bf16[5424,128]{1,0:T(8,128)(2,1)S(1)}, bf16[5424,128]{1,0:T(8,128)(2,1)S(1)}, u32[]{:S(2)}, u32[]{:S(2)}) collective-permute-start(bf16[5424,128]{1,0:T(8,128)(2,1)S(1)} %constant_dynamic-update-slice_fusion.7), channel_id=1, source_target_pairs={{0,24},{8,0},{16,8},{24,16},{1,25},{9,1},{17,9},{25,17},{2,26},{10... | collective-permute-start | bytes 4165640 | tf_op jit(solution)/shard_map/ppermute | solution.py:286
  52.1 39.8 %collective-permute-start.12 = (bf16[1808,128]{1,0:T(8,128)(2,1)S(1)}, bf16[1808,128]{1,0:T(8,128)(2,1)S(1)}, u32[]{:S(2)}, u32[]{:S(2)}) collective-permute-start(bf16[1808,128]{1,0:T(8,128)(2,1)S(1)} %collective-permute-done.11.refs_6_), channel_id=1, source_target_pairs={{0,32},{32,64},{64,96},{96,0},{1,33},{33,65},{65,97},{97,1},{2,34}... | collective-permute-start | bytes 1388552 | tf_op jit(solution)/shard_map/ppermute | solution.py:286
  81.9 12.0 %collective-permute-start.14 = (bf16[1808,128]{1,0:T(8,128)(2,1)S(1)}, bf16[1808,128]{1,0:T(8,128)(2,1)S(1)}, u32[]{:S(2)}, u32[]{:S(2)}) collective-permute-start(bf16[1808,128]{1,0:T(8,128)(2,1)S(1)} %collective-permute-done.11.refs_6_), channel_id=1, source_target_pairs={{0,96},{32,0},{64,32},{96,64},{1,97},{33,1},{65,33},{97,65},{2,98}... | collective-permute-start | bytes 1388552 | tf_op jit(solution)/shard_map/ppermute | solution.py:286
  81.9 14.3 %collective-permute-start.9 = (bf16[1808,128]{1,0:T(8,128)(2,1)S(1)}, bf16[1808,128]{1,0:T(8,128)(2,1)S(1)}, u32[]{:S(2)}, u32[]{:S(2)}) collective-permute-start(bf16[1808,128]{1,0:T(8,128)(2,1)S(1)} %collective-permute-done.6.refs_0_), channel_id=1, source_target_pairs={{0,24},{8,0},{16,8},{24,16},{1,25},{9,1},{17,9},{25,17},{2,26},{10... | collective-permute-start | bytes 1388552 | tf_op jit(solution)/shard_map/ppermute | solution.py:286
  91.8 31.8 %collective-permute-start.21 = (bf16[2720,128]{1,0:T(8,128)(2,1)S(1)}, bf16[2720,128]{1,0:T(8,128)(2,1)S(1)}, u32[]{:S(2)}, u32[]{:S(2)}) collective-permute-start(bf16[2720,128]{1,0:T(8,128)(2,1)S(1)} %slice.47), channel_id=1, source_target_pairs={{0,96},{32,0},{64,32},{96,64},{1,97},{33,1},{65,33},{97,65},{2,98}... | collective-permute-start | bytes 2088968 | tf_op jit(solution)/shard_map/ppermute | solution.py:286
  91.9 28.7 %collective-permute-start.19 = (bf16[2704,128]{1,0:T(8,128)(2,1)S(1)}, bf16[2704,128]{1,0:T(8,128)(2,1)S(1)}, u32[]{:S(2)}, u32[]{:S(2)}) collective-permute-start(bf16[2704,128]{1,0:T(8,128)(2,1)S(1)} %slice.46), channel_id=1, source_target_pairs={{0,32},{32,64},{64,96},{96,0},{1,33},{33,65},{65,97},{97,1},{2,34}... | collective-permute-start | bytes 2076680 | tf_op jit(solution)/shard_map/ppermute | solution.py:286
  93.4 29.7 %collective-permute-start.25 = (bf16[2704,128]{1,0:T(8,128)(2,1)S(1)}, bf16[2704,128]{1,0:T(8,128)(2,1)S(1)}, u32[]{:S(2)}, u32[]{:S(2)}) collective-permute-start(bf16[2704,128]{1,0:T(8,128)(2,1)S(1)} %slice.48), channel_id=1, source_target_pairs={{0,8},{8,16},{16,24},{24,0},{1,9},{9,17},{17,25},{25,1},{2,10},{10... | collective-permute-start | bytes 2076680 | tf_op jit(solution)/shard_map/ppermute | solution.py:286
  93.9 49.6 %collective-permute-start.27 = (bf16[2720,128]{1,0:T(8,128)(2,1)S(1)}, bf16[2720,128]{1,0:T(8,128)(2,1)S(1)}, u32[]{:S(2)}, u32[]{:S(2)}) collective-permute-start(bf16[2720,128]{1,0:T(8,128)(2,1)S(1)} %slice.49), channel_id=1, source_target_pairs={{0,24},{8,0},{16,8},{24,16},{1,25},{9,1},{17,9},{25,17},{2,26},{10... | collective-permute-start | bytes 2088968 | tf_op jit(solution)/shard_map/ppermute | solution.py:286
  96.3 24.3 %collective-permute-start.7 = (bf16[1808,128]{1,0:T(8,128)(2,1)S(1)}, bf16[1808,128]{1,0:T(8,128)(2,1)S(1)}, u32[]{:S(2)}, u32[]{:S(2)}) collective-permute-start(bf16[1808,128]{1,0:T(8,128)(2,1)S(1)} %collective-permute-done.6.refs_0_), channel_id=1, source_target_pairs={{0,8},{8,16},{16,24},{24,0},{1,9},{9,17},{17,25},{25,1},{2,10},{10... | collective-permute-start | bytes 1388552 | tf_op jit(solution)/shard_map/ppermute | solution.py:286
  120.5 37.7 %collective-permute-start.10 = (bf16[912,128]{1,0:T(8,128)(2,1)}, bf16[912,128]{1,0:T(8,128)(2,1)}, u32[]{:S(2)}, u32[]{:S(2)}) collective-permute-start(bf16[912,128]{1,0:T(8,128)(2,1)} %slice.43), channel_id=1, source_target_pairs={{0,24},{8,0},{16,8},{24,16},{1,25},{9,1},{17,9},{25,17},{2,26},{10... | collective-permute-start | bytes 700424 | tf_op jit(solution)/shard_map/ppermute | solution.py:286
  120.6 37.7 %collective-permute-start.15 = (bf16[912,128]{1,0:T(8,128)(2,1)}, bf16[912,128]{1,0:T(8,128)(2,1)}, u32[]{:S(2)}, u32[]{:S(2)}) collective-permute-start(bf16[912,128]{1,0:T(8,128)(2,1)} %slice.45), channel_id=1, source_target_pairs={{0,96},{32,0},{64,32},{96,64},{1,97},{33,1},{65,33},{97,65},{2,98}... | collective-permute-start | bytes 700424 | tf_op jit(solution)/shard_map/ppermute | solution.py:286
  123.1 35.2 %collective-permute-start.13 = (bf16[896,128]{1,0:T(8,128)(2,1)}, bf16[896,128]{1,0:T(8,128)(2,1)}, u32[]{:S(2)}, u32[]{:S(2)}) collective-permute-start(bf16[896,128]{1,0:T(8,128)(2,1)} %slice.44), channel_id=1, source_target_pairs={{0,32},{32,64},{64,96},{96,0},{1,33},{33,65},{65,97},{97,1},{2,34}... | collective-permute-start | bytes 688136 | tf_op jit(solution)/shard_map/ppermute | solution.py:286
  123.9 34.3 %collective-permute-start.8 = (bf16[896,128]{1,0:T(8,128)(2,1)}, bf16[896,128]{1,0:T(8,128)(2,1)}, u32[]{:S(2)}, u32[]{:S(2)}) collective-permute-start(bf16[896,128]{1,0:T(8,128)(2,1)} %slice.42), channel_id=1, source_target_pairs={{0,8},{8,16},{16,24},{24,0},{1,9},{9,17},{17,25},{25,1},{2,10},{10... | collective-permute-start | bytes 688136 | tf_op jit(solution)/shard_map/ppermute | solution.py:286
  197.1 20.4 %collective-permute-start.30 = (bf16[128,2304]{1,0:T(8,128)(2,1)}, bf16[128,2304]{1,0:T(8,128)(2,1)S(1)}, u32[]{:S(2)}, u32[]{:S(2)}) collective-permute-start(bf16[128,2304]{1,0:T(8,128)(2,1)} %get-tuple-element.47), channel_id=1, source_target_pairs={{0,4},{4,0},{1,5},{5,1},{2,6},{6,2},{3,7},{7,3},{8,12},{12,8},{9,1... | collective-permute-start | bytes 1769480 | tf_op jit(solution)/shard_map/ppermute | solution.py:366
  213.0 22.5 %collective-permute-start.35 = (bf16[32,1536]{1,0:T(8,128)(2,1)}, bf16[32,1536]{1,0:T(8,128)(2,1)S(1)}, u32[]{:S(2)}, u32[]{:S(2)}) collective-permute-start(bf16[32,1536]{1,0:T(8,128)(2,1)} %get-tuple-element.56), channel_id=1, source_target_pairs={{0,3},{1,0},{2,1},{3,2},{4,7},{5,4},{6,5},{7,6},{8,11},{9,8},{10,9... | collective-permute-start | bytes 294920 | tf_op jit(solution)/shard_map/ppermute | solution.py:286
  220.6 19.9 %collective-permute-start.31 = (bf16[32,2304]{1,0:T(8,128)(2,1)}, bf16[32,2304]{1,0:T(8,128)(2,1)S(1)}, u32[]{:S(2)}, u32[]{:S(2)}) collective-permute-start(bf16[32,2304]{1,0:T(8,128)(2,1)} %get-tuple-element.49), channel_id=1, source_target_pairs={{0,3},{1,0},{2,1},{3,2},{4,7},{5,4},{6,5},{7,6},{8,11},{9,8},{10,9... | collective-permute-start | bytes 442376 | tf_op jit(solution)/shard_map/ppermute | solution.py:286
  221.4 19.1 %collective-permute-start.32 = (bf16[32,2304]{1,0:T(8,128)(2,1)}, bf16[32,2304]{1,0:T(8,128)(2,1)S(1)}, u32[]{:S(2)}, u32[]{:S(2)}) collective-permute-start(bf16[32,2304]{1,0:T(8,128)(2,1)} %get-tuple-element.50), channel_id=1, source_target_pairs={{0,2},{1,3},{2,0},{3,1},{4,6},{5,7},{6,4},{7,5},{8,10},{9,11},{10,... | collective-permute-start | bytes 442376 | tf_op jit(solution)/shard_map/ppermute | solution.py:286
  223.5 17.0 %collective-permute-start.33 = (bf16[32,2304]{1,0:T(8,128)(2,1)}, bf16[32,2304]{1,0:T(8,128)(2,1)S(1)}, u32[]{:S(2)}, u32[]{:S(2)}) collective-permute-start(bf16[32,2304]{1,0:T(8,128)(2,1)} %get-tuple-element.51), channel_id=1, source_target_pairs={{0,1},{1,2},{2,3},{3,0},{4,5},{5,6},{6,7},{7,4},{8,9},{9,10},{10,1... | collective-permute-start | bytes 442376 | tf_op jit(solution)/shard_map/ppermute | solution.py:286
  (55 other events, 700.1 us)

commit v3 on v2

v3 whole, which is shorter than its diff:
```python
import jax
import jax.numpy as jnp
from jax import lax
from jax.experimental import pallas as pl
from jax.experimental.pallas import tpu as pltpu
from jax.sharding import Mesh, PartitionSpec as P

F32 = jnp.float32
BF16 = jnp.bfloat16
BLK = 128
CHIPS = 16
NCB = 28
CAP = 17
SURE = 11
LIVE = 28
HID = NCB * BLK
WIDTH = CHIPS * 2 * BLK
DEAD = 32 * NCB
SWAP = [(0, 1), (1, 0)]
HALF = LIVE // 2
UNIT = HALF * BLK + 16
MARK = HALF * BLK
ROWS = BLK // 4
HBM = pl.BlockSpec(memory_space=pltpu.HBM)
VMEM = pl.BlockSpec(memory_space=pltpu.VMEM)
SMEM = pl.BlockSpec(memory_space=pltpu.SMEM)


def params(mib=56):
    return pltpu.CompilerParams(vmem_limit_bytes=mib << 20)


def pack_kernel(scal, mine_i, theirs_i, mine, theirs, out_a, out_b):
    core, base = scal[0], scal[1]
    lane = lax.broadcasted_iota(jnp.int32, (16, BLK), 1)

    def place(j, block):
        out, at = (out_a, j) if j < HALF else (out_b, j - HALF)
        out[at * BLK : (at + 1) * BLK] = block

    def fill(first, first_i, second, second_i):
        n0 = jnp.int32(SURE)
        for j in range(SURE, CAP):
            n0 += (first_i[j] < DEAD).astype(jnp.int32)
        marks = [jnp.zeros((16, BLK), jnp.int32)] * 2
        for j in range(LIVE):
            if j < SURE:
                spot = first_i[j]
                place(j, first[j])
            elif j < CAP:
                spot = jnp.where(j < n0, first_i[j], second_i[jnp.maximum(j - n0, 0)])
                pl.when(j < n0)(lambda j=j: place(j, first[j]))
                pl.when(j >= n0)(lambda j=j: place(j, second[jnp.maximum(j - n0, 0)]))
            else:
                spot = second_i[j - n0]
                place(j, second[j - n0])
            half = j // HALF
            marks[half] = jnp.where(lane == j % HALF, spot - base, marks[half])
        out_a[MARK:UNIT] = marks[0].astype(F32).astype(BF16)
        out_b[MARK:UNIT] = marks[1].astype(F32).astype(BF16)

    pl.when(core == 0)(lambda: fill(mine, mine_i, theirs, theirs_i))
    pl.when(core != 0)(lambda: fill(theirs, theirs_i, mine, mine_i))


def pack(scal, mine_i, theirs_i, mine, theirs):
    one = jax.ShapeDtypeStruct((UNIT, BLK), BF16)
    return pl.pallas_call(
        pack_kernel,
        out_shape=(one, one),
        in_specs=[SMEM, SMEM, SMEM, VMEM, VMEM],
        out_specs=(VMEM, VMEM),
        compiler_params=params(8),
        cost_estimate=cost(2),
        name="pack",
    )(scal, mine_i, theirs_i, mine, theirs)


def stack_kernel(a, b, c, d, first, second):
    first[:UNIT] = a[...]
    first[UNIT:] = b[...]
    second[:UNIT] = c[...]
    second[UNIT:] = d[...]


def stack_pairs(a, b, c, d):
    two = pltpu.VMEM((2 * UNIT, BLK), BF16)
    return pl.pallas_call(
        stack_kernel,
        out_shape=(two, two),
        in_specs=[VMEM] * 4,
        out_specs=(VMEM, VMEM),
        compiler_params=params(4),
        cost_estimate=cost(1),
        name="stack_pairs",
    )(a, b, c, d)


def forward(units, chips, x_own, x_other, pieces, carry=None):
    count, given = len(units), len(pieces)
    carry = list(carry) if carry else []

    def kernel(chip_of, xo, xt, *refs):
        parts, refs = refs[:given], refs[given + len(carry) :]
        acc_own, acc_other, panels, buf, tiles, ints, marks, sem_t, sem_b, sem_m = refs
        moved = []
        for t, pair in enumerate(units):
            for h, source in enumerate(pair):
                part, row, rows, at = source[-1]
                mark = row + MARK - at
                tile = pltpu.make_async_copy(parts[part].at[pl.ds(mark, 16)], tiles.at[2 * t + h], sem_t.at[2 * t + h])
                tile.start()
                moved.append(tile)
        for t, pair in enumerate(units):
            for h, source in enumerate(pair):
                for part, row, rows, at in source:
                    pltpu.make_async_copy(
                        parts[part].at[pl.ds(row, rows)], buf.at[t, h, pl.ds(at, rows)], sem_b.at[t, h]
                    ).start()
        if not carry:
            acc_own[...] = jnp.zeros_like(acc_own)
            acc_other[...] = jnp.zeros_like(acc_other)
        for i, m in enumerate(moved):
            m.wait()
            ints[pl.ds(i, 1), :] = tiles[i].astype(F32)[0:1].astype(jnp.int32)
        load = pltpu.make_async_copy(ints, marks, sem_m)
        load.start()
        load.wait()

        def step(t, _):
            for h in range(2):
                pltpu.make_async_copy(buf.at[t, h], buf.at[t, h], sem_b.at[t, h]).wait()
            panels[t] = jnp.zeros((NCB, 2 * BLK, BLK), BF16)
            for j in range(LIVE):
                h, k = divmod(j, HALF)
                pos = marks[2 * t + h, k]
                low = (pos >= NCB).astype(jnp.int32)
                panels[t, pos - low * NCB, pl.ds(pl.multiple_of(low * BLK, BLK), BLK), :] = buf[t, h, k * BLK : (k + 1) * BLK]
            cols = pl.ds(pl.multiple_of(chip_of[t] * 2 * BLK, 2 * BLK), 2 * BLK)
            x = jnp.concatenate([xo[:, cols], xt[:, cols]], axis=0)
            for c in range(NCB // 2):
                w = jnp.concatenate([panels[t, 2 * c], panels[t, 2 * c + 1]], axis=1)
                r = jnp.dot(x, w, preferred_element_type=F32)
                at = pl.ds(c * 2 * BLK, 2 * BLK)
                acc_own[:, at] += r[:BLK]
                acc_other[:, at] += r[BLK:]
            return 0

        lax.fori_loop(0, count, step, 0)

    acc = pltpu.VMEM((BLK, HID), F32)
    return pl.pallas_call(
        kernel,
        out_shape=(acc, acc, pltpu.VMEM((count, NCB, 2 * BLK, BLK), BF16)),
        in_specs=[SMEM, VMEM, VMEM] + [HBM] * given + [VMEM] * len(carry),
        out_specs=(VMEM, VMEM, VMEM),
        scratch_shapes=[
            pltpu.VMEM((count, 2, UNIT, BLK), BF16),
            pltpu.VMEM((2 * count, 16, BLK), BF16),
            pltpu.VMEM((2 * count, BLK), jnp.int32),
            pltpu.SMEM((2 * count, BLK), jnp.int32),
            pltpu.SemaphoreType.DMA((2 * count,)),
            pltpu.SemaphoreType.DMA((count, 2)),
            pltpu.SemaphoreType.DMA,
        ],
        input_output_aliases={3 + given + i: i for i in range(len(carry))},
        compiler_params=params(count + 3),
        cost_estimate=cost(1.6 * count + 2),
        name="forward",
    )(chips, x_own, x_other, *[pltpu.with_memory_space_constraint(p, pltpu.HBM) for p in pieces], *carry)


def act_kernel(scal, mine, got, d_hidden, hidden, d_mine, d_send):
    def work(gate_ref, up_ref, d_gate, d_up):
        for k in range(4):
            rel = pl.ds(k * ROWS, ROWS)
            real = pl.ds(pl.multiple_of((scal[1] - k + 4) % 4 * ROWS, ROWS), ROWS)
            gate, up = gate_ref[rel, :], up_ref[rel, :]
            d = d_hidden[real, :].astype(F32)
            sig = jax.nn.sigmoid(gate)
            active = gate * sig
            hidden[real, :] = (active * up).astype(BF16)
            d_gate[rel, :] = (d * up * sig * (1.0 + gate * (1.0 - sig))).astype(BF16)
            d_up[rel, :] = (d * active).astype(BF16)

    pl.when(scal[0] == 0)(lambda: work(mine, got, d_mine, d_send))
    pl.when(scal[0] != 0)(lambda: work(got, mine, d_send, d_mine))


def activate(scal, mine, got, d_hidden):
    one = pltpu.VMEM((BLK, HID), BF16)
    return pl.pallas_call(
        act_kernel,
        out_shape=(jax.ShapeDtypeStruct((BLK, HID), BF16), one, one),
        in_specs=[SMEM, VMEM, VMEM, VMEM],
        out_specs=(VMEM, VMEM, VMEM),
        compiler_params=params(8),
        cost_estimate=cost(4),
        name="activate",
    )(scal, mine, got, d_hidden)


def backward(d_own, d_other, panels):
    count = [p.shape[0] for p in panels]
    width = sum(count) * 2 * BLK

    def kernel(own, other, *refs):
        parts, (out_own, out_other, both) = refs[:-3], refs[-3:]
        both[:BLK] = own[...]
        both[BLK:] = other[...]
        done = 0
        for part, n in zip(parts, count):

            def step(t, _, part=part, done=done):
                w = jnp.concatenate([part[t, c] for c in range(NCB)], axis=1)
                r = lax.dot_general(both[...], w, (((1,), (1,)), ((), ())), preferred_element_type=F32)
                cols = pl.ds(pl.multiple_of((t + done) * 2 * BLK, 2 * BLK), 2 * BLK)
                out_own[:, cols] = r[:BLK]
                out_other[:, cols] = r[BLK:].astype(BF16)
                return 0

            lax.fori_loop(0, n, step, 0)
            done += n

    return pl.pallas_call(
        kernel,
        out_shape=(pltpu.VMEM((BLK, width), F32), pltpu.VMEM((BLK, width), BF16)),
        in_specs=[VMEM] * (2 + len(panels)),
        out_specs=(VMEM, VMEM),
        scratch_shapes=[pltpu.VMEM((2 * BLK, HID), BF16)],
        compiler_params=params(8),
        cost_estimate=cost(0.85 * sum(count) + 1),
        name="backward",
    )(d_own, d_other, *panels)


def join(owns, gots):
    cols = [p.shape[1] for p in owns]

    def kernel(*refs):
        n, outs = len(cols), refs[-4:]
        for k in range(4):
            at, start = slice(k * ROWS, (k + 1) * ROWS), 0
            for own, got, wide in zip(refs[:n], refs[n : 2 * n], cols):
                total = own[at, :] + got[at, :].astype(F32)
                outs[k][:, start : start + wide] = total.astype(outs[k].dtype)
                start += wide

    return pl.pallas_call(
        kernel,
        out_shape=(pltpu.VMEM((ROWS, sum(cols)), F32),) + (pltpu.VMEM((ROWS, sum(cols)), BF16),) * 3,
        in_specs=[VMEM] * (2 * len(cols)),
        out_specs=(VMEM,) * 4,
        compiler_params=params(4),
        cost_estimate=cost(1.5),
        name="join",
    )(*owns, *gots)


def finish(chips, groups):
    def kernel(chip_of, *refs):
        out, t = refs[-1], 0
        for g in range(len(groups)):
            parts = refs[4 * g : 4 * g + 4]
            for i in range(parts[0].shape[1] // (2 * BLK)):
                at = slice(i * 2 * BLK, (i + 1) * 2 * BLK)
                total = parts[0][:, at]
                for p in parts[1:]:
                    total += p[:, at].astype(F32)
                out[:, pl.ds(pl.multiple_of(chip_of[t] * 2 * BLK, 2 * BLK), 2 * BLK)] = total.astype(BF16)
                t += 1

    flat = [a for g in groups for a in g]
    return pl.pallas_call(
        kernel,
        out_shape=jax.ShapeDtypeStruct((ROWS, WIDTH), BF16),
        in_specs=[SMEM] + [VMEM] * len(flat),
        out_specs=VMEM,
        compiler_params=params(4),
        cost_estimate=cost(2),
        name="finish",
    )(chips, *flat)


def cost(us):
    return pl.CostEstimate(flops=int(us * 1.0e9), bytes_accessed=int(us * 3.0e6), transcendentals=0)


def shift(a, axis, by, name="near"):
    with jax.named_scope(name):
        return lax.ppermute(a, axis, [(i, (i + by) % 4) for i in range(4)])


def swap(a, name="swap"):
    with jax.named_scope(name):
        return lax.ppermute(a, "c", SWAP)


def together(*arrays):
    return lax.optimization_barrier(arrays)


def shards(tokens, gate_blocks, gate_index, up_blocks, up_index, d_hidden):
    x, y, core, z = (lax.axis_index(n) for n in ("x", "y", "c", "z"))
    first = core == 0
    gate_i, up_i = gate_index[0], up_index[0]
    theirs = swap(jnp.where(first, up_blocks[0], gate_blocks[0]), "swap_blocks")
    theirs_i = swap(jnp.where(first, up_i, gate_i), "swap_index")
    mine = jnp.where(first, gate_blocks[0], up_blocks[0])
    mine_i = jnp.where(first, gate_i, up_i)
    scal = jnp.stack([core, z, (x * 4 + y) * 2 * NCB])
    a, b = pack(scal[0::2], mine_i, theirs_i, mine, theirs)
    a, b, tokens = together(a, b, tokens)

    a1, b2, a2, b1 = shift(a, "x", 1, "a1"), shift(b, "y", -1, "b2"), shift(a, "x", -1, "a2"), shift(b, "y", 1, "b1")
    a1, b2 = together(a1, b2)
    a3, b3 = shift(a1, "x", 1, "a3"), shift(b2, "y", -1, "b3")
    pa, pb = stack_pairs(a, a1, b, b2)
    qa, qb = stack_pairs(a2, a3, b1, b3)
    t1 = shift(tokens, "z", 1, "tokens")
    near_tokens, t1 = together(tokens, t1)
    t3 = shift(near_tokens, "z", -1, "tokens")
    t1, t3 = together(t1, t3)
    t2 = shift(t1, "z", 1, "tokens")
    x_own = jnp.concatenate([tokens, t1, t2, t3], axis=0)
    x_other = swap(x_own, "swap_tokens")
    pa1, pb2 = together(shift(pa, "y", 1, "pa1"), shift(pb, "x", -1, "pb2"))
    qa2, qb1 = together(shift(qa, "y", -1, "qa2"), shift(qb, "x", 1, "qb1"))
    late_qa, late_qb, pa1, pb2 = together(qa, qb, pa1, pb2)
    qa1, qb2 = together(shift(late_qa, "y", 1, "qa1"), shift(late_qb, "x", -1, "qb2"))
    late_pa, late_pb, qa2, qb1 = together(pa, pb, qa2, qb1)
    pa2, pb1 = together(shift(late_pa, "y", -1, "pa2"), shift(late_pb, "x", 1, "pb1"))
    step = (0, -1, 1, 2)
    stages = (
        [(0, 0), (0, 1), (1, 1), (2, 0), (2, 2)],
        [(1, 0), (2, 1), (0, 2), (1, 2)],
        [(0, 3), (1, 3), (3, 0), (3, 2)],
        [(2, 3), (3, 1), (3, 3)],
    )
    order = [c for which in stages for c in which]
    chips = jnp.stack([(x + step[i]) % 4 * 4 + (y + step[j]) % 4 for i, j in order])
    held = {
        "a": [(a, a1, a2, a3), (pa1, None), (None, qa2), None, (0, 1, 2, 3)],
        "b": [(b, b1, b2, b3), (None, qb1), (pb2, None), None, (0, 2, 1, 3)],
    }

    def source(name, near, across):
        if across == 0:
            return [(held[name][0][near], 0, UNIT, 0)]
        half, row = divmod(held[name][4].index(near), 2)
        return [(held[name][across][half], row * UNIT, UNIT, 0)]

    def stage(which, at, carry=None):
        pieces, units = [], []
        for i, j in which:
            pair = []
            for src in (source("a", i, j), source("b", j, i)):
                row = []
                for piece, r, n, d in src:
                    k = next((m for m, p in enumerate(pieces) if p is piece), None)
                    if k is None:
                        k = len(pieces)
                        pieces.append(piece)
                    row.append((k, r, n, d))
                pair.append(row)
            units.append(pair)
        *carry, panels = forward(units, chips[at : at + len(which)], x_own, x_other, pieces, carry)
        return carry, panels

    carry, first_panels = stage(stages[0], 0)
    held_pa, held_pb, *carry = together(pa1, pb2, *carry)
    fpa, fpb = together(shift(held_pa, "y", 1, "fpa"), shift(held_pb, "x", -1, "fpb"))
    held_qa, held_qb, pa2, pb1 = together(qa2, qb1, pa2, pb1)
    fqa, fqb = together(shift(held_qa, "y", -1, "fqa"), shift(held_qb, "x", 1, "fqb"))
    held["a"][1:4] = (pa1, qa1), (pa2, qa2), (fpa, fqa)
    held["b"][1:4] = (pb1, qb1), (pb2, qb2), (fpb, fqb)
    panels, at = [first_panels], len(stages[0])
    for which in stages[1:]:
        carry, panel = stage(which, at, carry)
        panels.append(panel)
        at += len(which)
    acc_own, acc_other = carry
    got = swap(acc_other, "swap_gate_up")
    hidden, d_mine, d_send = activate(scal[:2], acc_own, got, d_hidden)
    d_other = swap(d_send, "swap_d")
    parts = []
    for some in (panels[2:], panels[:2]):
        part_own, part_other = backward(d_mine, d_other, some)
        parts.append((part_own, swap(part_other, "swap_part")))
    keep, *sends = join([p[0] for p in reversed(parts)], [p[1] for p in reversed(parts)])
    groups = [[keep] + [shift(s, "z", -k - 1, "send_back") for k, s in enumerate(sends)]]
    return hidden, finish(chips, groups)


def solution(mesh):
    fine = Mesh(mesh.devices.reshape(4, 4, 2, 4), ("x", "y", "c", "z"))
    fsdp = ("x", "y", "c")
    every = P((*fsdp, "z"), None)
    in_specs = (every, P("z", fsdp, None, None), P("z", fsdp), P("z", fsdp, None, None), P("z", fsdp), P(fsdp, "z"))
    return jax.shard_map(shards, mesh=fine, in_specs=in_specs, out_specs=(P(fsdp, "z"), every), check_vma=False)
```

time: 247 us -> 164 us (0.66); the launches traced: 243 us -> 164 us
  waiting for transfers between devices: 96.9 us -> 63.2 us
  Pallas kernels: 80.4 us -> 46.9 us
  starting transfers between devices: 46.1 us -> 36.4 us
    ppermute x34 -> x24, waiting for transfers between devices: 91.6 us -> 54.8 us  [shift(): return lax.ppermute(a, axis, [(i, (i + by) % 4) for i in range(4)])]
    pallas_call x10, Pallas kernels: 76 us -> 44.9 us  [the longest x4 28.1 us: forward(): pl.pallas_call(kernel, out_shape=(acc, acc, pltpu.VMEM((count, NCB, 2 * B...]
    ppermute x34 -> x24, starting transfers between devices: 38.5 us -> 28 us  [shift(): return lax.ppermute(a, axis, [(i, (i + by) % 4) for i in range(4)])]
    unnamed x97 -> x57, local copies, waits for them, and re-layouts: 9.84 us -> 14.1 us
    slice x8 -> x0, local copies, waits for them, and re-layouts: 3.07 us -> none  [the longest x4 2.89 us: shards(): far2[name] = (shift(f[1][:CUT], across, 1), shift(f[2][CUT:], across, -1))]
    ppermute x8 -> x7, waiting for transfers between devices: 5.36 us -> 8.41 us  [swap(): return lax.ppermute(a, 'c', SWAP)]
    ppermute x8 -> x7, starting transfers between devices: 7.58 us -> 8.47 us  [swap(): return lax.ppermute(a, 'c', SWAP)]
  transfers between devices with their start and end apart: 42 -> 31, of which waited for: 13 -> 18; matrix products, arithmetic and copies ran while one was open for 5% -> 0% of each run, Pallas kernels for 21% -> 18%
where the time goes in v3:
time: 164 us
  waiting for transfers between devices  63.2 us (39%)
  Pallas kernels  46.9 us (29%)
  starting transfers between devices  36.4 us (22%)
  local copies, waits for them, and re-layouts  14.4 us (9%)
  other arithmetic  1.68 us (1%)
    ppermute x24, waiting for transfers between devices, shift(): return lax.ppermute(a, axis, [(i, (i + by) % 4) for i in range(4)])  54.8 us
    pallas_call x4, Pallas kernels, forward(): pl.pallas_call(kernel, out_shape=(acc, acc, pltpu.VMEM((count, NCB, 2 * B...  28.1 us
    ppermute x24, starting transfers between devices, shift(): return lax.ppermute(a, axis, [(i, (i + by) % 4) for i in range(4)])  28 us
    unnamed x57, local copies, waits for them, and re-layouts  14.1 us
    pallas_call x2, Pallas kernels, backward(): pl.pallas_call(kernel, out_shape=(pltpu.VMEM((BLK, width), F32), pltpu.VM...  11.1 us
    ppermute x7, starting transfers between devices, swap(): return lax.ppermute(a, 'c', SWAP)  8.47 us
    ppermute x7, waiting for transfers between devices, swap(): return lax.ppermute(a, 'c', SWAP)  8.41 us
  transfers between devices with their start and end apart: 31, of which 18 were waited for; matrix products, arithmetic and copies ran while one was open for 0% of the time, Pallas kernels for 18%

profile of v3, /device:TPU:1, one launch (start us, length us, event | category | flops | bytes accessed | tf_op | source)
XLA Modules:
  0.0 163.6 jit_solution(943088796692246547)
XLA Ops:
  2.0 1.5 collective-permute-start.1
  6.0 1.7 %collective-permute-start.2 = (bf16[32,4096]{1,0:T(8,128)(2,1)S(1)}, bf16[32,4096]{1,0:T(8,128)(2,1)S(1)}, u32[]{:S(2)}, u32[]{:S(2)}) collective-permute-start(bf16[32,4096]{1,0:T(8,128)(2,1)S(1)} %copy-done.18), channel_id=1, source_target_pairs={{0,1},{1,2},{2,3},{3,0},{4,5},{5,6},{6,7},{7,4},{8,9},{9,10},{10,1... | collective-permute-start | bytes 786440 | tf_op jit(solution)/shard_map/tokens/ppermute | solution.py:291
  8.9 2.7 %collective-permute-start.7 = (bf16[1808,128]{1,0:T(8,128)(2,1)S(1)}, bf16[1808,128]{1,0:T(8,128)(2,1)S(1)}, u32[]{:S(2)}, u32[]{:S(2)}) collective-permute-start(bf16[1808,128]{1,0:T(8,128)(2,1)S(1)} %get-tuple-element.76.c.refs_1_), channel_id=1, source_target_pairs={{0,24},{8,0},{16,8},{24,16},{1,25},{9,1},{17,9},{25,17},{2,26},{10... | collective-permute-start | bytes 1388552 | tf_op jit(solution)/shard_map/b2/ppermute | solution.py:291
  13.1 3.1 %collective-permute-done.2 = bf16[32,4096]{1,0:T(8,128)(2,1)S(1)} collective-permute-done((bf16[32,4096]{1,0:T(8,128)(2,1)S(1)}, bf16[32,4096]{1,0:T(8,128)(2,1)S(1)}, u32[]{:S(2)}, u32[]{:S(2)}) %collective-permute-start.2) | collective-permute-done | bytes 262176 | tf_op jit(solution)/shard_map/tokens/ppermute | solution.py:291
  17.4 3.1 %collective-permute-done.6.b.refs_0_ = bf16[1808,128]{1,0:T(8,128)(2,1)S(1)} collective-permute-done((bf16[1808,128]{1,0:T(8,128)(2,1)S(1)}, bf16[1808,128]{1,0:T(8,128)(2,1)S(1)}, u32[]{:S(2)}, u32[]{:S(2)}) %collective-permute-start.6) | collective-permute-done | bytes 462880 | tf_op jit(solution)/shard_map/a1/ppermute | solution.py:291
  21.9 3.4 %collective-permute-start.11 = (bf16[1808,128]{1,0:T(8,128)(2,1)S(1)}, bf16[1808,128]{1,0:T(8,128)(2,1)S(1)}, u32[]{:S(2)}, u32[]{:S(2)}) collective-permute-start(bf16[1808,128]{1,0:T(8,128)(2,1)S(1)} %collective-permute-done.7.d.refs_5_), channel_id=1, source_target_pairs={{0,24},{8,0},{16,8},{24,16},{1,25},{9,1},{17,9},{25,17},{2,26},{10... | collective-permute-start | bytes 1388552 | tf_op jit(solution)/shard_map/b3/ppermute | solution.py:291
  25.3 1.6 %collective-permute-start.4 = (bf16[32,4096]{1,0:T(8,128)(2,1)S(1)}, bf16[32,4096]{1,0:T(8,128)(2,1)S(1)}, u32[]{:S(2)}, u32[]{:S(2)}) collective-permute-start(bf16[32,4096]{1,0:T(8,128)(2,1)S(1)} %collective-permute-done.2), channel_id=1, source_target_pairs={{0,1},{1,2},{2,3},{3,0},{4,5},{5,6},{6,7},{7,4},{8,9},{9,10},{10,1... | collective-permute-start | bytes 786440 | tf_op jit(solution)/shard_map/tokens/ppermute | solution.py:291
  26.9 5.1 %collective-permute-done.4 = bf16[32,4096]{1,0:T(8,128)(2,1)S(1)} collective-permute-done((bf16[32,4096]{1,0:T(8,128)(2,1)S(1)}, bf16[32,4096]{1,0:T(8,128)(2,1)S(1)}, u32[]{:S(2)}, u32[]{:S(2)}) %collective-permute-start.4) | collective-permute-done | bytes 262176 | tf_op jit(solution)/shard_map/tokens/ppermute | solution.py:291
  32.1 3.3 %collective-permute-start.5 = (bf16[128,4096]{1,0:T(8,128)(2,1)S(1)}, bf16[128,4096]{1,0:T(8,128)(2,1)S(1)}, u32[]{:S(2)}, u32[]{:S(2)}) collective-permute-start(bf16[128,4096]{1,0:T(8,128)(2,1)S(1)} %constant_dynamic-update-slice_fusion.xo), channel_id=1, source_target_pairs={{0,4},{4,0},{1,5},{5,1},{2,6},{6,2},{3,7},{7,3},{8,12},{12,8},{9,1... | collective-permute-start | bytes 3145736 | tf_op jit(solution)/shard_map/swap_tokens/ppermute | solution.py:296
  36.9 1.6 collective-permute-start.19
  38.5 1.5 stack_pairs.3
  40.1 2.6 %collective-permute-start.12 = (bf16[3616,128]{1,0:T(8,128)(2,1)}, bf16[3616,128]{1,0:T(8,128)(2,1)}, u32[]{:S(2)}, u32[]{:S(2)}) collective-permute-start(bf16[3616,128]{1,0:T(8,128)(2,1)} %get-tuple-element.96), channel_id=1, source_target_pairs={{0,24},{8,0},{16,8},{24,16},{1,25},{9,1},{17,9},{25,17},{2,26},{10... | collective-permute-start | bytes 2777096 | tf_op jit(solution)/shard_map/qa2/ppermute | solution.py:291
  42.8 17.7 %collective-permute-done.18.refs_2_ = bf16[3616,128]{1,0:T(8,128)(2,1)} collective-permute-done((bf16[3616,128]{1,0:T(8,128)(2,1)}, bf16[3616,128]{1,0:T(8,128)(2,1)}, u32[]{:S(2)}, u32[]{:S(2)}) %collective-permute-start.18) | collective-permute-done | bytes 925728 | tf_op jit(solution)/shard_map/pa1/ppermute | solution.py:291
  60.6 2.6 %collective-permute-start.21 = (bf16[3616,128]{1,0:T(8,128)(2,1)}, bf16[3616,128]{1,0:T(8,128)(2,1)}, u32[]{:S(2)}, u32[]{:S(2)}) collective-permute-start(bf16[3616,128]{1,0:T(8,128)(2,1)} %get-tuple-element.97), channel_id=1, source_target_pairs={{0,96},{32,0},{64,32},{96,64},{1,97},{33,1},{65,33},{97,65},{2,98}... | collective-permute-start | bytes 2777096 | tf_op jit(solution)/shard_map/qb2/ppermute | solution.py:291
  63.2 2.2 %collective-permute-done.13.refs_4_.refs_2_ = bf16[3616,128]{1,0:T(8,128)(2,1)} collective-permute-done((bf16[3616,128]{1,0:T(8,128)(2,1)}, bf16[3616,128]{1,0:T(8,128)(2,1)}, u32[]{:S(2)}, u32[]{:S(2)}) %collective-permute-start.13) | collective-permute-done | bytes 925728 | tf_op jit(solution)/shard_map/qb1/ppermute | solution.py:291
  68.0 8.3 %forward.4 = (f32[128,3584]{1,0:T(8,128)S(1)}, f32[128,3584]{1,0:T(8,128)S(1)}, bf16[5,28,256,128]{3,2,1,0:T(8,128)(2,1)S(1)}) custom-call(s32[5]{0:T(128)S(1)} %stack.92.chip_of, bf16[128,4096]{1,0:T(8,128)(2,1)S(1)} %constant_dynamic-update-slice_fusion.xo, bf16[128,4096]{1,0:T(8,128)(2,1)S(1)} %copy-done.1, bf16[1808,128]{1,0:T(8,128)(2,1)} %copy-done.9, ...), custom_call_target="tpu_custom_call" | custom-call | flops 10000000000 | bytes 30000000 | tf_op jit(solution)/shard_map/forward/pallas_call | solution.py:152
  76.3 3.6 %copy-done.13 = bf16[5,28,256,128]{3,2,1,0:T(8,128)(2,1)} copy-done((bf16[5,28,256,128]{3,2,1,0:T(8,128)(2,1)}, bf16[5,28,256,128]{3,2,1,0:T(8,128)(2,1)S(1)}, u32[]{:S(2)}) %copy-start.13) | copy-done | bytes 9175064
  83.4 1.5 collective-permute-start.23
  90.6 6.9 %forward.5 = (f32[128,3584]{1,0:T(8,128)S(1)}, f32[128,3584]{1,0:T(8,128)S(1)}, bf16[4,28,256,128]{3,2,1,0:T(8,128)(2,1)S(1)}) custom-call(s32[4]{0:T(128)S(1)} %pad_add_fusion.4.chip_of, bf16[128,4096]{1,0:T(8,128)(2,1)S(1)} %constant_dynamic-update-slice_fusion.xo, bf16[128,4096]{1,0:T(8,128)(2,1)S(1)} %copy-done.2, ...), custom_call_target="tpu_custom_call", output_to_operand_aliasing={{0}: (9, {}), {1}: (10, {})} | custom-call | flops 8400000000 | bytes 25200000 | tf_op jit(solution)/shard_map/forward/pallas_call | solution.py:152
  97.5 5.1 %collective-permute-done.22.refs_0_ = bf16[3616,128]{1,0:T(8,128)(2,1)} collective-permute-done((bf16[3616,128]{1,0:T(8,128)(2,1)}, bf16[3616,128]{1,0:T(8,128)(2,1)}, u32[]{:S(2)}, u32[]{:S(2)}) %collective-permute-start.22) | collective-permute-done | bytes 925728 | tf_op jit(solution)/shard_map/fpa/ppermute | solution.py:291
  104.1 6.9 %forward.6 = (f32[128,3584]{1,0:T(8,128)S(1)}, f32[128,3584]{1,0:T(8,128)S(1)}, bf16[4,28,256,128]{3,2,1,0:T(8,128)(2,1)S(1)}) custom-call(s32[4]{0:T(128)S(1)} %pad_add_fusion.3.chip_of, bf16[128,4096]{1,0:T(8,128)(2,1)S(1)} %constant_dynamic-update-slice_fusion.xo, bf16[128,4096]{1,0:T(8,128)(2,1)S(1)} %copy-done.2, ...), custom_call_target="tpu_custom_call", output_to_operand_aliasing={{0}: (9, {}), {1}: (10, {})} | custom-call | flops 8400000000 | bytes 25200000 | tf_op jit(solution)/shard_map/forward/pallas_call | solution.py:152
  112.4 5.9 %forward.7 = (f32[128,3584]{1,0:T(8,128)S(1)}, f32[128,3584]{1,0:T(8,128)S(1)}, bf16[3,28,256,128]{3,2,1,0:T(8,128)(2,1)S(1)}) custom-call(s32[3]{0:T(128)S(1)} %pad_add_fusion.1.chip_of, bf16[128,4096]{1,0:T(8,128)(2,1)S(1)} %constant_dynamic-update-slice_fusion.xo, bf16[128,4096]{1,0:T(8,128)(2,1)S(1)} %copy-done.3, ...), custom_call_target="tpu_custom_call", output_to_operand_aliasing={{0}: (7, {}), {1}: (8, {})} | custom-call | flops 6800000000 | bytes 20400000 | tf_op jit(solution)/shard_map/forward/pallas_call | solution.py:152
  119.5 2.5 %collective-permute-start.24 = (f32[128,3584]{1,0:T(8,128)S(1)}, f32[128,3584]{1,0:T(8,128)S(1)}, u32[]{:S(2)}, u32[]{:S(2)}) collective-permute-start(f32[128,3584]{1,0:T(8,128)S(1)} %get-tuple-element.118), channel_id=1, source_target_pairs={{0,4},{4,0},{1,5},{5,1},{2,6},{6,2},{3,7},{7,3},{8,12},{12,8},{9,1... | collective-permute-start | bytes 5505032 | tf_op jit(solution)/shard_map/swap_gate_up/ppermute | solution.py:296
  122.0 3.3 %collective-permute-done.24.got = f32[128,3584]{1,0:T(8,128)S(1)} collective-permute-done((f32[128,3584]{1,0:T(8,128)S(1)}, f32[128,3584]{1,0:T(8,128)S(1)}, u32[]{:S(2)}, u32[]{:S(2)}) %collective-permute-start.24) | collective-permute-done | bytes 1835040 | tf_op jit(solution)/shard_map/swap_gate_up/ppermute | solution.py:296
  126.9 2.7 %activate.1 = (bf16[128,3584]{1,0:T(8,128)(2,1)}, bf16[128,3584]{1,0:T(8,128)(2,1)S(1)}, bf16[128,3584]{1,0:T(8,128)(2,1)S(1)}) custom-call(s32[2]{0:T(128)S(1)} %pad_add_fusion.scal, f32[128,3584]{1,0:T(8,128)S(1)} %copy-done.17, f32[128,3584]{1,0:T(8,128)S(1)} %collective-permute-done.24.got, bf16[128,3584]{1,0:T(8,128)(2,1)S(1)} %copy-done.4), custom_call_target="tpu_custom_call" | custom-call | flops 4000000000 | bytes 12000000 | tf_op jit(solution)/shard_map/activate/pallas_call | solution.py:192
  129.9 2.1 %collective-permute-done.25.other = bf16[128,3584]{1,0:T(8,128)(2,1)S(1)} collective-permute-done((bf16[128,3584]{1,0:T(8,128)(2,1)S(1)}, bf16[128,3584]{1,0:T(8,128)(2,1)S(1)}, u32[]{:S(2)}, u32[]{:S(2)}) %collective-permute-start.25) | collective-permute-done | bytes 917536 | tf_op jit(solution)/shard_map/swap_d/ppermute | solution.py:296
  132.1 6.2 %backward.2 = (f32[128,2304]{1,0:T(8,128)S(1)}, bf16[128,2304]{1,0:T(8,128)(2,1)S(1)}) custom-call(bf16[128,3584]{1,0:T(8,128)(2,1)S(1)} %get-tuple-element.120.own, bf16[128,3584]{1,0:T(8,128)(2,1)S(1)} %collective-permute-done.25.other, bf16[5,28,256,128]{3,2,1,0:T(8,128)(2,1)S(1)} %bitcast.28, bf16[4,28,256,128]{3,2,1,0:T(8,128)(2,1)S(1)} %get-tuple-element.123.refs_1_), custom_call_target="tpu_custom_call" | custom-call | flops 8650000384 | bytes 25950000 | tf_op jit(solution)/shard_map/backward/pallas_call | solution.py:225
  138.7 4.8 %backward.3 = (f32[128,1792]{1,0:T(8,128)S(1)}, bf16[128,1792]{1,0:T(8,128)(2,1)S(1)}) custom-call(bf16[128,3584]{1,0:T(8,128)(2,1)S(1)} %get-tuple-element.120.own, bf16[128,3584]{1,0:T(8,128)(2,1)S(1)} %collective-permute-done.25.other, bf16[4,28,256,128]{3,2,1,0:T(8,128)(2,1)S(1)} %get-tuple-element.125.refs_0_, ...), custom_call_target="tpu_custom_call" | custom-call | flops 6950000128 | bytes 20850000 | tf_op jit(solution)/shard_map/backward/pallas_call | solution.py:225
  143.8 1.7 %collective-permute-done.27.refs_3_ = bf16[128,1792]{1,0:T(8,128)(2,1)S(1)} collective-permute-done((bf16[128,1792]{1,0:T(8,128)(2,1)S(1)}, bf16[128,1792]{1,0:T(8,128)(2,1)S(1)}, u32[]{:S(2)}, u32[]{:S(2)}) %collective-permute-start.27) | collective-permute-done | bytes 458784 | tf_op jit(solution)/shard_map/swap_part/ppermute | solution.py:296
  148.8 4.7 %collective-permute-done.28.refs_1_ = bf16[32,4096]{1,0:T(8,128)(2,1)S(1)} collective-permute-done((bf16[32,4096]{1,0:T(8,128)(2,1)S(1)}, bf16[32,4096]{1,0:T(8,128)(2,1)S(1)}, u32[]{:S(2)}, u32[]{:S(2)}) %collective-permute-start.28) | collective-permute-done | bytes 262176 | tf_op jit(solution)/shard_map/send_back/ppermute | solution.py:291
  153.5 2.4 %collective-permute-done.29.refs_2_ = bf16[32,4096]{1,0:T(8,128)(2,1)S(1)} collective-permute-done((bf16[32,4096]{1,0:T(8,128)(2,1)S(1)}, bf16[32,4096]{1,0:T(8,128)(2,1)S(1)}, u32[]{:S(2)}, u32[]{:S(2)}) %collective-permute-start.29) | collective-permute-done | bytes 262176 | tf_op jit(solution)/shard_map/send_back/ppermute | solution.py:291
  155.9 6.4 %collective-permute-done.30.refs_3_ = bf16[32,4096]{1,0:T(8,128)(2,1)S(1)} collective-permute-done((bf16[32,4096]{1,0:T(8,128)(2,1)S(1)}, bf16[32,4096]{1,0:T(8,128)(2,1)S(1)}, u32[]{:S(2)}, u32[]{:S(2)}) %collective-permute-start.30) | collective-permute-done | bytes 262176 | tf_op jit(solution)/shard_map/send_back/ppermute | solution.py:291
  (111 shorter events, 33.8 us)
Async XLA Ops:
  2.0 3.1 %collective-permute-start.1 = (bf16[17,128,128]{2,1,0:T(8,128)(2,1)S(1)}, bf16[17,128,128]{2,1,0:T(8,128)(2,1)S(1)}, u32[]{:S(2)}, u32[]{:S(2)}) collective-permute-start(bf16[17,128,128]{2,1,0:T(8,128)(2,1)S(1)} %get-tuple-element.134), channel_id=1, source_target_pairs={{0,4},{4,0},{1,5},{5,1},{2,6},{6,2},{3,7},{7,3},{8,12},{12,8},{9,1... | collective-permute-start | bytes 1671176 | tf_op jit(solution)/shard_map/swap_blocks/ppermute | solution.py:296
  3.5 1.6 collective-permute-start
  5.7 31.1 %copy-start.9 = (bf16[1808,128]{1,0:T(8,128)(2,1)}, bf16[1808,128]{1,0:T(8,128)(2,1)S(1)}, u32[]{:S(2)}) copy-start(bf16[1808,128]{1,0:T(8,128)(2,1)S(1)} %get-tuple-element.75.a.refs_0_) | copy-start | bytes 1388548
  6.0 10.2 %collective-permute-start.2 = (bf16[32,4096]{1,0:T(8,128)(2,1)S(1)}, bf16[32,4096]{1,0:T(8,128)(2,1)S(1)}, u32[]{:S(2)}, u32[]{:S(2)}) collective-permute-start(bf16[32,4096]{1,0:T(8,128)(2,1)S(1)} %copy-done.18), channel_id=1, source_target_pairs={{0,1},{1,2},{2,3},{3,0},{4,5},{5,6},{6,7},{7,4},{8,9},{9,10},{10,1... | collective-permute-start | bytes 786440 | tf_op jit(solution)/shard_map/tokens/ppermute | solution.py:291
  7.7 12.7 %collective-permute-start.6 = (bf16[1808,128]{1,0:T(8,128)(2,1)S(1)}, bf16[1808,128]{1,0:T(8,128)(2,1)S(1)}, u32[]{:S(2)}, u32[]{:S(2)}) collective-permute-start(bf16[1808,128]{1,0:T(8,128)(2,1)S(1)} %get-tuple-element.75.a.refs_0_), channel_id=1, source_target_pairs={{0,32},{32,64},{64,96},{96,0},{1,33},{33,65},{65,97},{97,1},{2,34}... | collective-permute-start | bytes 1388552 | tf_op jit(solution)/shard_map/a1/ppermute | solution.py:291
  8.9 11.7 %collective-permute-start.7 = (bf16[1808,128]{1,0:T(8,128)(2,1)S(1)}, bf16[1808,128]{1,0:T(8,128)(2,1)S(1)}, u32[]{:S(2)}, u32[]{:S(2)}) collective-permute-start(bf16[1808,128]{1,0:T(8,128)(2,1)S(1)} %get-tuple-element.76.c.refs_1_), channel_id=1, source_target_pairs={{0,24},{8,0},{16,8},{24,16},{1,25},{9,1},{17,9},{25,17},{2,26},{10... | collective-permute-start | bytes 1388552 | tf_op jit(solution)/shard_map/b2/ppermute | solution.py:291
  11.7 25.1 %collective-permute-start.8 = (bf16[1808,128]{1,0:T(8,128)(2,1)S(1)}, bf16[1808,128]{1,0:T(8,128)(2,1)S(1)}, u32[]{:S(2)}, u32[]{:S(2)}) collective-permute-start(bf16[1808,128]{1,0:T(8,128)(2,1)S(1)} %get-tuple-element.75.a.refs_0_), channel_id=1, source_target_pairs={{0,96},{32,0},{64,32},{96,64},{1,97},{33,1},{65,33},{97,65},{2,98}... | collective-permute-start | bytes 1388552 | tf_op jit(solution)/shard_map/a2/ppermute | solution.py:291
  13.1 23.8 %collective-permute-start.10 = (bf16[1808,128]{1,0:T(8,128)(2,1)S(1)}, bf16[1808,128]{1,0:T(8,128)(2,1)S(1)}, u32[]{:S(2)}, u32[]{:S(2)}) collective-permute-start(bf16[1808,128]{1,0:T(8,128)(2,1)S(1)} %get-tuple-element.76.c.refs_1_), channel_id=1, source_target_pairs={{0,8},{8,16},{16,24},{24,0},{1,9},{9,17},{17,25},{25,1},{2,10},{10... | collective-permute-start | bytes 1388552 | tf_op jit(solution)/shard_map/b1/ppermute | solution.py:291
  16.2 9.1 %collective-permute-start.3 = (bf16[32,4096]{1,0:T(8,128)(2,1)S(1)}, bf16[32,4096]{1,0:T(8,128)(2,1)S(1)}, u32[]{:S(2)}, u32[]{:S(2)}) collective-permute-start(bf16[32,4096]{1,0:T(8,128)(2,1)S(1)} %copy-done.18), channel_id=1, source_target_pairs={{0,3},{1,0},{2,1},{3,2},{4,7},{5,4},{6,5},{7,6},{8,11},{9,8},{10,9... | collective-permute-start | bytes 786440 | tf_op jit(solution)/shard_map/tokens/ppermute | solution.py:291
  20.7 17.9 %collective-permute-start.9 = (bf16[1808,128]{1,0:T(8,128)(2,1)S(1)}, bf16[1808,128]{1,0:T(8,128)(2,1)S(1)}, u32[]{:S(2)}, u32[]{:S(2)}) collective-permute-start(bf16[1808,128]{1,0:T(8,128)(2,1)S(1)} %collective-permute-done.6.b.refs_0_), channel_id=1, source_target_pairs={{0,32},{32,64},{64,96},{96,0},{1,33},{33,65},{65,97},{97,1},{2,34}... | collective-permute-start | bytes 1388552 | tf_op jit(solution)/shard_map/a3/ppermute | solution.py:291
  21.9 16.7 %collective-permute-start.11 = (bf16[1808,128]{1,0:T(8,128)(2,1)S(1)}, bf16[1808,128]{1,0:T(8,128)(2,1)S(1)}, u32[]{:S(2)}, u32[]{:S(2)}) collective-permute-start(bf16[1808,128]{1,0:T(8,128)(2,1)S(1)} %collective-permute-done.7.d.refs_5_), channel_id=1, source_target_pairs={{0,24},{8,0},{16,8},{24,16},{1,25},{9,1},{17,9},{25,17},{2,26},{10... | collective-permute-start | bytes 1388552 | tf_op jit(solution)/shard_map/b3/ppermute | solution.py:291
  25.3 6.7 %collective-permute-start.4 = (bf16[32,4096]{1,0:T(8,128)(2,1)S(1)}, bf16[32,4096]{1,0:T(8,128)(2,1)S(1)}, u32[]{:S(2)}, u32[]{:S(2)}) collective-permute-start(bf16[32,4096]{1,0:T(8,128)(2,1)S(1)} %collective-permute-done.2), channel_id=1, source_target_pairs={{0,1},{1,2},{2,3},{3,0},{4,5},{5,6},{6,7},{7,4},{8,9},{9,10},{10,1... | collective-permute-start | bytes 786440 | tf_op jit(solution)/shard_map/tokens/ppermute | solution.py:291
  32.1 33.7 %collective-permute-start.5 = (bf16[128,4096]{1,0:T(8,128)(2,1)S(1)}, bf16[128,4096]{1,0:T(8,128)(2,1)S(1)}, u32[]{:S(2)}, u32[]{:S(2)}) collective-permute-start(bf16[128,4096]{1,0:T(8,128)(2,1)S(1)} %constant_dynamic-update-slice_fusion.xo), channel_id=1, source_target_pairs={{0,4},{4,0},{1,5},{5,1},{2,6},{6,2},{3,7},{7,3},{8,12},{12,8},{9,1... | collective-permute-start | bytes 3145736 | tf_op jit(solution)/shard_map/swap_tokens/ppermute | solution.py:296
  36.8 23.7 %collective-permute-start.18 = (bf16[3616,128]{1,0:T(8,128)(2,1)}, bf16[3616,128]{1,0:T(8,128)(2,1)}, u32[]{:S(2)}, u32[]{:S(2)}) collective-permute-start(bf16[3616,128]{1,0:T(8,128)(2,1)} %get-tuple-element.87), channel_id=1, source_target_pairs={{0,8},{8,16},{16,24},{24,0},{1,9},{9,17},{17,25},{25,1},{2,10},{10... | collective-permute-start | bytes 2777096 | tf_op jit(solution)/shard_map/pa1/ppermute | solution.py:291
  36.9 23.6 %collective-permute-start.19 = (bf16[3616,128]{1,0:T(8,128)(2,1)}, bf16[3616,128]{1,0:T(8,128)(2,1)}, u32[]{:S(2)}, u32[]{:S(2)}) collective-permute-start(bf16[3616,128]{1,0:T(8,128)(2,1)} %get-tuple-element.88), channel_id=1, source_target_pairs={{0,96},{32,0},{64,32},{96,64},{1,97},{33,1},{65,33},{97,65},{2,98}... | collective-permute-start | bytes 2777096 | tf_op jit(solution)/shard_map/pb2/ppermute | solution.py:291
  40.1 23.1 %collective-permute-start.12 = (bf16[3616,128]{1,0:T(8,128)(2,1)}, bf16[3616,128]{1,0:T(8,128)(2,1)}, u32[]{:S(2)}, u32[]{:S(2)}) collective-permute-start(bf16[3616,128]{1,0:T(8,128)(2,1)} %get-tuple-element.96), channel_id=1, source_target_pairs={{0,24},{8,0},{16,8},{24,16},{1,25},{9,1},{17,9},{25,17},{2,26},{10... | collective-permute-start | bytes 2777096 | tf_op jit(solution)/shard_map/qa2/ppermute | solution.py:291
  42.7 22.7 %collective-permute-start.13 = (bf16[3616,128]{1,0:T(8,128)(2,1)}, bf16[3616,128]{1,0:T(8,128)(2,1)}, u32[]{:S(2)}, u32[]{:S(2)}) collective-permute-start(bf16[3616,128]{1,0:T(8,128)(2,1)} %get-tuple-element.97), channel_id=1, source_target_pairs={{0,32},{32,64},{64,96},{96,0},{1,33},{33,65},{65,97},{97,1},{2,34}... | collective-permute-start | bytes 2777096 | tf_op jit(solution)/shard_map/qb1/ppermute | solution.py:291
  60.6 22.8 %collective-permute-start.20 = (bf16[3616,128]{1,0:T(8,128)(2,1)}, bf16[3616,128]{1,0:T(8,128)(2,1)S(1)}, u32[]{:S(2)}, u32[]{:S(2)}) collective-permute-start(bf16[3616,128]{1,0:T(8,128)(2,1)} %get-tuple-element.96), channel_id=1, source_target_pairs={{0,8},{8,16},{16,24},{24,0},{1,9},{9,17},{17,25},{25,1},{2,10},{10... | collective-permute-start | bytes 2777096 | tf_op jit(solution)/shard_map/qa1/ppermute | solution.py:291
  60.6 24.5 %collective-permute-start.21 = (bf16[3616,128]{1,0:T(8,128)(2,1)}, bf16[3616,128]{1,0:T(8,128)(2,1)}, u32[]{:S(2)}, u32[]{:S(2)}) collective-permute-start(bf16[3616,128]{1,0:T(8,128)(2,1)} %get-tuple-element.97), channel_id=1, source_target_pairs={{0,96},{32,0},{64,32},{96,64},{1,97},{33,1},{65,33},{97,65},{2,98}... | collective-permute-start | bytes 2777096 | tf_op jit(solution)/shard_map/qb2/ppermute | solution.py:291
  65.4 20.6 %collective-permute-start.14 = (bf16[3616,128]{1,0:T(8,128)(2,1)}, bf16[3616,128]{1,0:T(8,128)(2,1)}, u32[]{:S(2)}, u32[]{:S(2)}) collective-permute-start(bf16[3616,128]{1,0:T(8,128)(2,1)} %get-tuple-element.87), channel_id=1, source_target_pairs={{0,24},{8,0},{16,8},{24,16},{1,25},{9,1},{17,9},{25,17},{2,26},{10... | collective-permute-start | bytes 2777096 | tf_op jit(solution)/shard_map/pa2/ppermute | solution.py:291
  65.8 21.5 %collective-permute-start.15 = (bf16[3616,128]{1,0:T(8,128)(2,1)}, bf16[3616,128]{1,0:T(8,128)(2,1)}, u32[]{:S(2)}, u32[]{:S(2)}) collective-permute-start(bf16[3616,128]{1,0:T(8,128)(2,1)} %get-tuple-element.88), channel_id=1, source_target_pairs={{0,32},{32,64},{64,96},{96,0},{1,33},{33,65},{65,97},{97,1},{2,34}... | collective-permute-start | bytes 2777096 | tf_op jit(solution)/shard_map/pb1/ppermute | solution.py:291
  81.1 21.5 %collective-permute-start.22 = (bf16[3616,128]{1,0:T(8,128)(2,1)}, bf16[3616,128]{1,0:T(8,128)(2,1)}, u32[]{:S(2)}, u32[]{:S(2)}) collective-permute-start(bf16[3616,128]{1,0:T(8,128)(2,1)} %collective-permute-done.18.refs_2_), channel_id=1, source_target_pairs={{0,8},{8,16},{16,24},{24,0},{1,9},{9,17},{17,25},{25,1},{2,10},{10... | collective-permute-start | bytes 2777096 | tf_op jit(solution)/shard_map/fpa/ppermute | solution.py:291
  83.4 20.8 %collective-permute-start.23 = (bf16[3616,128]{1,0:T(8,128)(2,1)}, bf16[3616,128]{1,0:T(8,128)(2,1)}, u32[]{:S(2)}, u32[]{:S(2)}) collective-permute-start(bf16[3616,128]{1,0:T(8,128)(2,1)} %collective-permute-done.19.refs_6_), channel_id=1, source_target_pairs={{0,96},{32,0},{64,32},{96,64},{1,97},{33,1},{65,33},{97,65},{2,98}... | collective-permute-start | bytes 2777096 | tf_op jit(solution)/shard_map/fpb/ppermute | solution.py:291
  87.3 23.8 %collective-permute-start.16 = (bf16[3616,128]{1,0:T(8,128)(2,1)}, bf16[3616,128]{1,0:T(8,128)(2,1)S(1)}, u32[]{:S(2)}, u32[]{:S(2)}) collective-permute-start(bf16[3616,128]{1,0:T(8,128)(2,1)} %collective-permute-done.12.refs_7_.refs_5_), channel_id=1, source_target_pairs={{0,24},{8,0},{16,8},{24,16},{1,25},{9,1},{17,9},{25,17},{2,26},{10... | collective-permute-start | bytes 2777096 | tf_op jit(solution)/shard_map/fqa/ppermute | solution.py:291
  87.7 23.4 %collective-permute-start.17 = (bf16[3616,128]{1,0:T(8,128)(2,1)}, bf16[3616,128]{1,0:T(8,128)(2,1)S(1)}, u32[]{:S(2)}, u32[]{:S(2)}) collective-permute-start(bf16[3616,128]{1,0:T(8,128)(2,1)} %collective-permute-done.13.refs_4_.refs_2_), channel_id=1, source_target_pairs={{0,32},{32,64},{64,96},{96,0},{1,33},{33,65},{65,97},{97,1},{2,34}... | collective-permute-start | bytes 2777096 | tf_op jit(solution)/shard_map/fqb/ppermute | solution.py:291
  119.5 5.9 %collective-permute-start.24 = (f32[128,3584]{1,0:T(8,128)S(1)}, f32[128,3584]{1,0:T(8,128)S(1)}, u32[]{:S(2)}, u32[]{:S(2)}) collective-permute-start(f32[128,3584]{1,0:T(8,128)S(1)} %get-tuple-element.118), channel_id=1, source_target_pairs={{0,4},{4,0},{1,5},{5,1},{2,6},{6,2},{3,7},{7,3},{8,12},{12,8},{9,1... | collective-permute-start | bytes 5505032 | tf_op jit(solution)/shard_map/swap_gate_up/ppermute | solution.py:296
  129.6 2.5 %collective-permute-start.25 = (bf16[128,3584]{1,0:T(8,128)(2,1)S(1)}, bf16[128,3584]{1,0:T(8,128)(2,1)S(1)}, u32[]{:S(2)}, u32[]{:S(2)}) collective-permute-start(bf16[128,3584]{1,0:T(8,128)(2,1)S(1)} %get-tuple-element.121), channel_id=1, source_target_pairs={{0,4},{4,0},{1,5},{5,1},{2,6},{6,2},{3,7},{7,3},{8,12},{12,8},{9,1... | collective-permute-start | bytes 2752520 | tf_op jit(solution)/shard_map/swap_d/ppermute | solution.py:296
  138.3 7.2 %collective-permute-start.26 = (bf16[128,2304]{1,0:T(8,128)(2,1)S(1)}, bf16[128,2304]{1,0:T(8,128)(2,1)S(1)}, u32[]{:S(2)}, u32[]{:S(2)}) collective-permute-start(bf16[128,2304]{1,0:T(8,128)(2,1)S(1)} %get-tuple-element.128), channel_id=1, source_target_pairs={{0,4},{4,0},{1,5},{5,1},{2,6},{6,2},{3,7},{7,3},{8,12},{12,8},{9,1... | collective-permute-start | bytes 1769480 | tf_op jit(solution)/shard_map/swap_part/ppermute | solution.py:296
  143.6 1.9 %collective-permute-start.27 = (bf16[128,1792]{1,0:T(8,128)(2,1)S(1)}, bf16[128,1792]{1,0:T(8,128)(2,1)S(1)}, u32[]{:S(2)}, u32[]{:S(2)}) collective-permute-start(bf16[128,1792]{1,0:T(8,128)(2,1)S(1)} %get-tuple-element.129), channel_id=1, source_target_pairs={{0,4},{4,0},{1,5},{5,1},{2,6},{6,2},{3,7},{7,3},{8,12},{12,8},{9,1... | collective-permute-start | bytes 1376264 | tf_op jit(solution)/shard_map/swap_part/ppermute | solution.py:296
  145.6 7.8 %collective-permute-start.28 = (bf16[32,4096]{1,0:T(8,128)(2,1)S(1)}, bf16[32,4096]{1,0:T(8,128)(2,1)S(1)}, u32[]{:S(2)}, u32[]{:S(2)}) collective-permute-start(bf16[32,4096]{1,0:T(8,128)(2,1)S(1)} %get-tuple-element.131), channel_id=1, source_target_pairs={{0,3},{1,0},{2,1},{3,2},{4,7},{5,4},{6,5},{7,6},{8,11},{9,8},{10,9... | collective-permute-start | bytes 786440 | tf_op jit(solution)/shard_map/send_back/ppermute | solution.py:291
  146.9 9.0 %collective-permute-start.29 = (bf16[32,4096]{1,0:T(8,128)(2,1)S(1)}, bf16[32,4096]{1,0:T(8,128)(2,1)S(1)}, u32[]{:S(2)}, u32[]{:S(2)}) collective-permute-start(bf16[32,4096]{1,0:T(8,128)(2,1)S(1)} %get-tuple-element.132), channel_id=1, source_target_pairs={{0,2},{1,3},{2,0},{3,1},{4,6},{5,7},{6,4},{7,5},{8,10},{9,11},{10,... | collective-permute-start | bytes 786440 | tf_op jit(solution)/shard_map/send_back/ppermute | solution.py:291
  147.9 14.3 %collective-permute-start.30 = (bf16[32,4096]{1,0:T(8,128)(2,1)S(1)}, bf16[32,4096]{1,0:T(8,128)(2,1)S(1)}, u32[]{:S(2)}, u32[]{:S(2)}) collective-permute-start(bf16[32,4096]{1,0:T(8,128)(2,1)S(1)} %get-tuple-element.133), channel_id=1, source_target_pairs={{0,1},{1,2},{2,3},{3,0},{4,5},{5,6},{6,7},{7,4},{8,9},{9,10},{10,1... | collective-permute-start | bytes 786440 | tf_op jit(solution)/shard_map/send_back/ppermute | solution.py:291
  (26 other events, 161.6 us)

commit v4 on v3

--- a/solution.py
+++ b/solution.py
@@ -31,7 +31,7 @@
 
 
 def pack_kernel(scal, mine_i, theirs_i, mine, theirs, out_a, out_b):
-    core, base = scal[0], scal[1]
+    core, base = scal[0], scal[2]
     lane = lax.broadcasted_iota(jnp.int32, (16, BLK), 1)
 
     def place(j, block):
@@ -96,63 +96,81 @@
     )(a, b, c, d)
 
 
-def forward(units, chips, x_own, x_other, pieces, carry=None):
+def forward(units, at, chips, x_own, x_other, pieces, inside, carry=None):
     count, given = len(units), len(pieces)
     carry = list(carry) if carry else []
 
     def kernel(chip_of, xo, xt, *refs):
         parts, refs = refs[:given], refs[given + len(carry) :]
         acc_own, acc_other, panels, buf, tiles, ints, marks, sem_t, sem_b, sem_m = refs
-        moved = []
-        for t, pair in enumerate(units):
-            for h, source in enumerate(pair):
-                part, row, rows, at = source[-1]
-                mark = row + MARK - at
-                tile = pltpu.make_async_copy(parts[part].at[pl.ds(mark, 16)], tiles.at[2 * t + h], sem_t.at[2 * t + h])
-                tile.start()
-                moved.append(tile)
-        for t, pair in enumerate(units):
-            for h, source in enumerate(pair):
-                for part, row, rows, at in source:
-                    pltpu.make_async_copy(
-                        parts[part].at[pl.ds(row, rows)], buf.at[t, h, pl.ds(at, rows)], sem_b.at[t, h]
-                    ).start()
+        direct = all(inside)
+        if not direct:
+            moved = []
+            for t, pair in enumerate(units):
+                for h, source in enumerate(pair):
+                    part, row, rows, to = source[-1]
+                    mark = row + MARK - to
+                    tile = pltpu.make_async_copy(parts[part].at[pl.ds(mark, 16)], tiles.at[2 * t + h], sem_t.at[2 * t + h])
+                    tile.start()
+                    moved.append(tile)
+            for t, pair in enumerate(units):
+                for h, source in enumerate(pair):
+                    for part, row, rows, to in source:
+                        pltpu.make_async_copy(
+                            parts[part].at[pl.ds(row, rows)], buf.at[t, h, pl.ds(to, rows)], sem_b.at[t, h]
+                        ).start()
         if not carry:
             acc_own[...] = jnp.zeros_like(acc_own)
             acc_other[...] = jnp.zeros_like(acc_other)
-        for i, m in enumerate(moved):
-            m.wait()
-            ints[pl.ds(i, 1), :] = tiles[i].astype(F32)[0:1].astype(jnp.int32)
+        for i in range(2 * count):
+            if direct:
+                part, row, rows, to = units[i // 2][i % 2][-1]
+                tile = parts[part][row + MARK - to : row + UNIT - to]
+            else:
+                moved[i].wait()
+                tile = tiles[i]
+            ints[pl.ds(i, 1), :] = tile.astype(F32)[0:1].astype(jnp.int32)
         load = pltpu.make_async_copy(ints, marks, sem_m)
         load.start()
         load.wait()
 
+        def block(t, h, k):
+            if direct:
+                part, row, rows, to = units[t][h][-1]
+                return parts[part][row + k * BLK : row + (k + 1) * BLK]
+            return buf[t, h, k * BLK : (k + 1) * BLK]
+
         def step(t, _):
-            for h in range(2):
-                pltpu.make_async_copy(buf.at[t, h], buf.at[t, h], sem_b.at[t, h]).wait()
+            if not direct:
+                for h in range(2):
+                    pltpu.make_async_copy(buf.at[t, h], buf.at[t, h], sem_b.at[t, h]).wait()
             panels[t] = jnp.zeros((NCB, 2 * BLK, BLK), BF16)
             for j in range(LIVE):
                 h, k = divmod(j, HALF)
                 pos = marks[2 * t + h, k]
                 low = (pos >= NCB).astype(jnp.int32)
-                panels[t, pos - low * NCB, pl.ds(pl.multiple_of(low * BLK, BLK), BLK), :] = buf[t, h, k * BLK : (k + 1) * BLK]
-            cols = pl.ds(pl.multiple_of(chip_of[t] * 2 * BLK, 2 * BLK), 2 * BLK)
+                panels[t, pos - low * NCB, pl.ds(pl.multiple_of(low * BLK, BLK), BLK), :] = block(t, h, k)
+            cols = pl.ds(pl.multiple_of(chip_of[at + t] * 2 * BLK, 2 * BLK), 2 * BLK)
             x = jnp.concatenate([xo[:, cols], xt[:, cols]], axis=0)
             for c in range(NCB // 2):
                 w = jnp.concatenate([panels[t, 2 * c], panels[t, 2 * c + 1]], axis=1)
                 r = jnp.dot(x, w, preferred_element_type=F32)
-                at = pl.ds(c * 2 * BLK, 2 * BLK)
-                acc_own[:, at] += r[:BLK]
-                acc_other[:, at] += r[BLK:]
+                span = pl.ds(c * 2 * BLK, 2 * BLK)
+                acc_own[:, span] += r[:BLK]
+                acc_other[:, span] += r[BLK:]
             return 0
 
-        lax.fori_loop(0, count, step, 0)
+        if direct:
+            for t in range(count):
+                step(t, 0)
+        else:
+            lax.fori_loop(0, count, step, 0)
 
     acc = pltpu.VMEM((BLK, HID), F32)
     return pl.pallas_call(
         kernel,
         out_shape=(acc, acc, pltpu.VMEM((count, NCB, 2 * BLK, BLK), BF16)),
-        in_specs=[SMEM, VMEM, VMEM] + [HBM] * given + [VMEM] * len(carry),
+        in_specs=[SMEM, VMEM, VMEM] + [VMEM if i else HBM for i in inside] + [VMEM] * len(carry),
         out_specs=(VMEM, VMEM, VMEM),
         scratch_shapes=[
             pltpu.VMEM((count, 2, UNIT, BLK), BF16),
@@ -167,7 +185,7 @@
         compiler_params=params(count + 3),
         cost_estimate=cost(1.6 * count + 2),
         name="forward",
-    )(chips, x_own, x_other, *[pltpu.with_memory_space_constraint(p, pltpu.HBM) for p in pieces], *carry)
+    )(chips, x_own, x_other, *[p if i else pltpu.with_memory_space_constraint(p, pltpu.HBM) for p, i in zip(pieces, inside)], *carry)
 
 
 def act_kernel(scal, mine, got, d_hidden, hidden, d_mine, d_send):
@@ -308,40 +326,39 @@
     theirs_i = swap(jnp.where(first, up_i, gate_i), "swap_index")
     mine = jnp.where(first, gate_blocks[0], up_blocks[0])
     mine_i = jnp.where(first, gate_i, up_i)
-    scal = jnp.stack([core, z, (x * 4 + y) * 2 * NCB])
-    a, b = pack(scal[0::2], mine_i, theirs_i, mine, theirs)
-    a, b, tokens = together(a, b, tokens)
-
-    a1, b2, a2, b1 = shift(a, "x", 1, "a1"), shift(b, "y", -1, "b2"), shift(a, "x", -1, "a2"), shift(b, "y", 1, "b1")
-    a1, b2 = together(a1, b2)
-    a3, b3 = shift(a1, "x", 1, "a3"), shift(b2, "y", -1, "b3")
-    pa, pb = stack_pairs(a, a1, b, b2)
-    qa, qb = stack_pairs(a2, a3, b1, b3)
-    t1 = shift(tokens, "z", 1, "tokens")
-    near_tokens, t1 = together(tokens, t1)
-    t3 = shift(near_tokens, "z", -1, "tokens")
-    t1, t3 = together(t1, t3)
-    t2 = shift(t1, "z", 1, "tokens")
-    x_own = jnp.concatenate([tokens, t1, t2, t3], axis=0)
-    x_other = swap(x_own, "swap_tokens")
-    pa1, pb2 = together(shift(pa, "y", 1, "pa1"), shift(pb, "x", -1, "pb2"))
-    qa2, qb1 = together(shift(qa, "y", -1, "qa2"), shift(qb, "x", 1, "qb1"))
-    late_qa, late_qb, pa1, pb2 = together(qa, qb, pa1, pb2)
-    qa1, qb2 = together(shift(late_qa, "y", 1, "qa1"), shift(late_qb, "x", -1, "qb2"))
-    late_pa, late_pb, qa2, qb1 = together(pa, pb, qa2, qb1)
-    pa2, pb1 = together(shift(late_pa, "y", -1, "pa2"), shift(late_pb, "x", 1, "pb1"))
     step = (0, -1, 1, 2)
     stages = (
         [(0, 0), (0, 1), (1, 1), (2, 0), (2, 2)],
-        [(1, 0), (2, 1), (0, 2), (1, 2)],
-        [(0, 3), (1, 3), (3, 0), (3, 2)],
-        [(2, 3), (3, 1), (3, 3)],
+        [(1, 0), (3, 0), (0, 2), (1, 2), (3, 2), (0, 3), (1, 3)],
+        [(2, 1), (3, 1), (2, 3), (3, 3)],
     )
     order = [c for which in stages for c in which]
     chips = jnp.stack([(x + step[i]) % 4 * 4 + (y + step[j]) % 4 for i, j in order])
+    scal = jnp.stack([core, z, (x * 4 + y) * 2 * NCB])
+    a, b = pack(scal, mine_i, theirs_i, mine, theirs)
+    a, b, chips, scal, near_tokens = together(a, b, chips, scal, tokens)
+
+    a1, b2, a2, b1 = shift(a, "x", 1, "a1"), shift(b, "y", -1, "b2"), shift(a, "x", -1, "a2"), shift(b, "y", 1, "b1")
+    t1 = shift(near_tokens, "z", 1, "tokens")
+    a1, b2 = together(a1, b2)
+    tokens, t1, a2, b1 = together(tokens, t1, a2, b1)
+    a3, b3 = shift(a1, "x", 1, "a3"), shift(b2, "y", -1, "b3")
+    t2, t3 = shift(t1, "z", 1, "tokens"), shift(tokens, "z", -1, "tokens")
+    t2, t3, a3, b3 = together(t2, t3, a3, b3)
+    qa, qb = stack_pairs(a2, a3, b1, b3)
+    qa, qb, a_late, b_late = together(qa, qb, a, b)
+    pa, pb = stack_pairs(a_late, a1, b_late, b2)
+    qa2, qb1 = shift(qa, "y", -1, "qa2"), shift(qb, "x", 1, "qb1")
+    pa1, pb2 = shift(pa, "y", 1, "pa1"), shift(pb, "x", -1, "pb2")
+    x_own = jnp.concatenate([tokens, t1, t2, t3], axis=0)
+    x_other = swap(x_own, "swap_tokens")
+    late_pa, qa2, pa1 = together(pa, qa2, pa1)
+    late_pb, qb1, pb2 = together(pb, qb1, pb2)
+    pa2, pb1 = shift(late_pa, "y", -1, "pa2"), shift(late_pb, "x", 1, "pb1")
+    fpa, fpb = shift(pa1, "y", 1, "fpa"), shift(pb2, "x", -1, "fpb")
     held = {
-        "a": [(a, a1, a2, a3), (pa1, None), (None, qa2), None, (0, 1, 2, 3)],
-        "b": [(b, b1, b2, b3), (None, qb1), (pb2, None), None, (0, 2, 1, 3)],
+        "a": [(a, a1, a2, a3), (pa1, None), (pa2, qa2), (fpa, None), (0, 1, 2, 3)],
+        "b": [(b, b1, b2, b3), (pb1, qb1), (pb2, None), (fpb, None), (0, 2, 1, 3)],
     }
 
     def source(name, near, across):
@@ -350,7 +367,7 @@
         half, row = divmod(held[name][4].index(near), 2)
         return [(held[name][across][half], row * UNIT, UNIT, 0)]
 
-    def stage(which, at, carry=None):
+    def stage(which, at, carry=None, fresh=()):
         pieces, units = [], []
         for i, j in which:
             pair = []
@@ -364,32 +381,35 @@
                     row.append((k, r, n, d))
                 pair.append(row)
             units.append(pair)
-        *carry, panels = forward(units, chips[at : at + len(which)], x_own, x_other, pieces, carry)
+        *carry, panels = forward(units, at, chips, x_own, x_other, pieces, [any(p is f for f in fresh) for p in pieces], carry)
         return carry, panels
 
     carry, first_panels = stage(stages[0], 0)
-    held_pa, held_pb, *carry = together(pa1, pb2, *carry)
-    fpa, fpb = together(shift(held_pa, "y", 1, "fpa"), shift(held_pb, "x", -1, "fpb"))
-    held_qa, held_qb, pa2, pb1 = together(qa2, qb1, pa2, pb1)
-    fqa, fqb = together(shift(held_qa, "y", -1, "fqa"), shift(held_qb, "x", 1, "fqb"))
+    late_qa, late_qb, held_qa, held_qb, *carry = together(qa, qb, qa2, qb1, *carry)
+    late_qa, held_qa, fpa, pa2 = together(late_qa, held_qa, fpa, pa2)
+    late_qb, held_qb, fpb, pb1 = together(late_qb, held_qb, fpb, pb1)
+    fqa, fqb = shift(held_qa, "y", -1, "fqa"), shift(held_qb, "x", 1, "fqb")
+    qa1, qb2 = shift(late_qa, "y", 1, "qa1"), shift(late_qb, "x", -1, "qb2")
     held["a"][1:4] = (pa1, qa1), (pa2, qa2), (fpa, fqa)
     held["b"][1:4] = (pb1, qb1), (pb2, qb2), (fpb, fqb)
     panels, at = [first_panels], len(stages[0])
     for which in stages[1:]:
-        carry, panel = stage(which, at, carry)
+        carry, panel = stage(which, at, carry, (qa1, qb2, fqa, fqb))
         panels.append(panel)
         at += len(which)
     acc_own, acc_other = carry
     got = swap(acc_other, "swap_gate_up")
-    hidden, d_mine, d_send = activate(scal[:2], acc_own, got, d_hidden)
+    hidden, d_mine, d_send = activate(scal, acc_own, got, d_hidden)
     d_other = swap(d_send, "swap_d")
     parts = []
-    for some in (panels[2:], panels[:2]):
+    for some in (panels[1:2], panels[0::2]):
         part_own, part_other = backward(d_mine, d_other, some)
         parts.append((part_own, swap(part_other, "swap_part")))
-    keep, *sends = join([p[0] for p in reversed(parts)], [p[1] for p in reversed(parts)])
+    keep, *sends = join([p[0] for p in parts], [p[1] for p in parts])
+    tail = [c for k in (1, 0, 2) for c in stages[k]]
+    tail = jnp.stack([(x + step[i]) % 4 * 4 + (y + step[j]) % 4 for i, j in tail])
     groups = [[keep] + [shift(s, "z", -k - 1, "send_back") for k, s in enumerate(sends)]]
-    return hidden, finish(chips, groups)
+    return hidden, finish(tail, groups)
 
 
 def solution(mesh):

time: 164 us -> 157 us (0.957)
  local copies, waits for them, and re-layouts: 14.4 us -> 0.34 us
  waiting for transfers between devices: 63.2 us -> 71 us
  Pallas kernels: 46.9 us -> 39.5 us
  starting transfers between devices: 36.4 us -> 43.7 us
    unnamed x57 -> x43, local copies, waits for them, and re-layouts: 14.1 us -> 0.13 us
    ppermute x24, waiting for transfers between devices: 54.8 us -> 62.5 us  [shift(): return lax.ppermute(a, axis, [(i, (i + by) % 4) for i in range(4)])]
    ppermute x24, starting transfers between devices: 28 us -> 32.9 us  [shift(): return lax.ppermute(a, axis, [(i, (i + by) % 4) for i in range(4)])]
    pallas_call x4 -> x3, Pallas kernels: 28.1 us -> 23.3 us  [forward(): pl.pallas_call(kernel, out_shape=(acc, acc, pltpu.VMEM((count, NCB, 2 * B...]
    pallas_call x2, Pallas kernels: 2.91 us -> 0.24 us  [stack_pairs(): pl.pallas_call(stack_kernel, out_shape=(two, two), in_specs=[VMEM] * 4, o...]
    ppermute x7, starting transfers between devices: 8.47 us -> 10.8 us  [swap(): return lax.ppermute(a, 'c', SWAP)]
  transfers between devices with their start and end apart: 31 -> 31, of which waited for: 18 -> 16; matrix products, arithmetic and copies ran while one was open for 0% -> 0% of each run, Pallas kernels for 18% -> 15%
where the time goes in v4:
time: 157 us
  waiting for transfers between devices  71 us (45%)
  starting transfers between devices  43.7 us (28%)
  Pallas kernels  39.5 us (25%)
    ppermute x24, waiting for transfers between devices, shift(): return lax.ppermute(a, axis, [(i, (i + by) % 4) for i in range(4)])  62.5 us
    ppermute x24, starting transfers between devices, shift(): return lax.ppermute(a, axis, [(i, (i + by) % 4) for i in range(4)])  32.9 us
    pallas_call x3, Pallas kernels, forward(): pl.pallas_call(kernel, out_shape=(acc, acc, pltpu.VMEM((count, NCB, 2 * B...  23.3 us
    pallas_call x2, Pallas kernels, backward(): pl.pallas_call(kernel, out_shape=(pltpu.VMEM((BLK, width), F32), pltpu.VM...  11.2 us
    ppermute x7, starting transfers between devices, swap(): return lax.ppermute(a, 'c', SWAP)  10.8 us
    ppermute x7, waiting for transfers between devices, swap(): return lax.ppermute(a, 'c', SWAP)  8.4 us
  transfers between devices with their start and end apart: 31, of which 16 were waited for; matrix products, arithmetic and copies ran while one was open for 0% of the time, Pallas kernels for 15%

profile of v4, /device:TPU:1, one launch (start us, length us, event | category | flops | bytes accessed | tf_op | source)
XLA Modules:
  0.0 156.9 jit_solution(3590325580159586898)
XLA Ops:
  7.1 2.7 %collective-permute-start.8 = (bf16[1808,128]{1,0:T(8,128)(2,1)S(1)}, bf16[1808,128]{1,0:T(8,128)(2,1)S(1)}, u32[]{:S(2)}, u32[]{:S(2)}) collective-permute-start(bf16[1808,128]{1,0:T(8,128)(2,1)S(1)} %get-tuple-element.89.c.refs_1_), channel_id=1, source_target_pairs={{0,24},{8,0},{16,8},{24,16},{1,25},{9,1},{17,9},{25,17},{2,26},{10... | collective-permute-start | bytes 1388552 | tf_op jit(solution)/shard_map/b2/ppermute | solution.py:309
  11.3 1.6 %collective-permute-start.2 = (bf16[32,4096]{1,0:T(8,128)(2,1)S(1)}, bf16[32,4096]{1,0:T(8,128)(2,1)S(1)}, u32[]{:S(2)}, u32[]{:S(2)}) collective-permute-start(bf16[32,4096]{1,0:T(8,128)(2,1)S(1)} %copy-done.9), channel_id=1, source_target_pairs={{0,1},{1,2},{2,3},{3,0},{4,5},{5,6},{6,7},{7,4},{8,9},{9,10},{10,1... | collective-permute-start | bytes 786440 | tf_op jit(solution)/shard_map/tokens/ppermute | solution.py:309
  13.0 5.9 %collective-permute-done.7.b.refs_0_ = bf16[1808,128]{1,0:T(8,128)(2,1)S(1)} collective-permute-done((bf16[1808,128]{1,0:T(8,128)(2,1)S(1)}, bf16[1808,128]{1,0:T(8,128)(2,1)S(1)}, u32[]{:S(2)}, u32[]{:S(2)}) %collective-permute-start.7) | collective-permute-done | bytes 462880 | tf_op jit(solution)/shard_map/a1/ppermute | solution.py:309
  19.1 3.4 %collective-permute-start.10 = (bf16[1808,128]{1,0:T(8,128)(2,1)S(1)}, bf16[1808,128]{1,0:T(8,128)(2,1)S(1)}, u32[]{:S(2)}, u32[]{:S(2)}) collective-permute-start(bf16[1808,128]{1,0:T(8,128)(2,1)S(1)} %collective-permute-done.8.d.refs_5_), channel_id=1, source_target_pairs={{0,24},{8,0},{16,8},{24,16},{1,25},{9,1},{17,9},{25,17},{2,26},{10... | collective-permute-start | bytes 1388552 | tf_op jit(solution)/shard_map/b3/ppermute | solution.py:309
  23.8 3.8 %collective-permute-start.6 = (bf16[32,4096]{1,0:T(8,128)(2,1)S(1)}, bf16[32,4096]{1,0:T(8,128)(2,1)S(1)}, u32[]{:S(2)}, u32[]{:S(2)}) collective-permute-start(bf16[32,4096]{1,0:T(8,128)(2,1)S(1)} %copy-done.9), channel_id=1, source_target_pairs={{0,3},{1,0},{2,1},{3,2},{4,7},{5,4},{6,5},{7,6},{8,11},{9,8},{10,9... | collective-permute-start | bytes 786440 | tf_op jit(solution)/shard_map/tokens/ppermute | solution.py:309
  27.8 6.7 %collective-permute-done.5 = bf16[32,4096]{1,0:T(8,128)(2,1)S(1)} collective-permute-done((bf16[32,4096]{1,0:T(8,128)(2,1)S(1)}, bf16[32,4096]{1,0:T(8,128)(2,1)S(1)}, u32[]{:S(2)}, u32[]{:S(2)}) %collective-permute-start.5) | collective-permute-done | bytes 262176 | tf_op jit(solution)/shard_map/tokens/ppermute | solution.py:309
  34.5 3.3 %collective-permute-start.11 = (bf16[128,4096]{1,0:T(8,128)(2,1)S(1)}, bf16[128,4096]{1,0:T(8,128)(2,1)S(1)}, u32[]{:S(2)}, u32[]{:S(2)}) collective-permute-start(bf16[128,4096]{1,0:T(8,128)(2,1)S(1)} %constant_dynamic-update-slice_fusion.xo), channel_id=1, source_target_pairs={{0,4},{4,0},{1,5},{5,1},{2,6},{6,2},{3,7},{7,3},{8,12},{12,8},{9,1... | collective-permute-start | bytes 3145736 | tf_op jit(solution)/shard_map/swap_tokens/ppermute | solution.py:314
  39.7 2.7 %collective-permute-start.12 = (bf16[3616,128]{1,0:T(8,128)(2,1)S(1)}, bf16[3616,128]{1,0:T(8,128)(2,1)S(1)}, u32[]{:S(2)}, u32[]{:S(2)}) collective-permute-start(bf16[3616,128]{1,0:T(8,128)(2,1)S(1)} %get-tuple-element.101), channel_id=1, source_target_pairs={{0,24},{8,0},{16,8},{24,16},{1,25},{9,1},{17,9},{25,17},{2,26},{10... | collective-permute-start | bytes 2777096 | tf_op jit(solution)/shard_map/qa2/ppermute | solution.py:309
  42.4 17.3 %collective-permute-done.15.refs_6_ = bf16[3616,128]{1,0:T(8,128)(2,1)S(1)} collective-permute-done((bf16[3616,128]{1,0:T(8,128)(2,1)S(1)}, bf16[3616,128]{1,0:T(8,128)(2,1)S(1)}, u32[]{:S(2)}, u32[]{:S(2)}) %collective-permute-start.15) | collective-permute-done | bytes 925728 | tf_op jit(solution)/shard_map/pb2/ppermute | solution.py:309
  59.7 2.4 %collective-permute-done.14.refs_4_.refs_9_ = bf16[3616,128]{1,0:T(8,128)(2,1)S(1)} collective-permute-done((bf16[3616,128]{1,0:T(8,128)(2,1)S(1)}, bf16[3616,128]{1,0:T(8,128)(2,1)S(1)}, u32[]{:S(2)}, u32[]{:S(2)}) %collective-permute-start.14) | collective-permute-done | bytes 925728 | tf_op jit(solution)/shard_map/qb1/ppermute | solution.py:309
  62.1 2.4 %collective-permute-start.19 = (bf16[3616,128]{1,0:T(8,128)(2,1)S(1)}, bf16[3616,128]{1,0:T(8,128)(2,1)S(1)}, u32[]{:S(2)}, u32[]{:S(2)}) collective-permute-start(bf16[3616,128]{1,0:T(8,128)(2,1)S(1)} %collective-permute-done.15.refs_6_), channel_id=1, source_target_pairs={{0,96},{32,0},{64,32},{96,64},{1,97},{33,1},{65,33},{97,65},{2,98}... | collective-permute-start | bytes 2777096 | tf_op jit(solution)/shard_map/fpb/ppermute | solution.py:309
  64.5 2.7 %collective-permute-start.17 = (bf16[3616,128]{1,0:T(8,128)(2,1)S(1)}, bf16[3616,128]{1,0:T(8,128)(2,1)S(1)}, u32[]{:S(2)}, u32[]{:S(2)}) collective-permute-start(bf16[3616,128]{1,0:T(8,128)(2,1)S(1)} %get-tuple-element.100), channel_id=1, source_target_pairs={{0,24},{8,0},{16,8},{24,16},{1,25},{9,1},{17,9},{25,17},{2,26},{10... | collective-permute-start | bytes 2777096 | tf_op jit(solution)/shard_map/pa2/ppermute | solution.py:309
  67.2 8.2 %forward.3 = (f32[128,3584]{1,0:T(8,128)S(1)}, f32[128,3584]{1,0:T(8,128)S(1)}, bf16[5,28,256,128]{3,2,1,0:T(8,128)(2,1)S(1)}) custom-call(s32[16]{0:T(128)S(1)} %stack.102.chip_of, bf16[128,4096]{1,0:T(8,128)(2,1)S(1)} %constant_dynamic-update-slice_fusion.xo, bf16[128,4096]{1,0:T(8,128)(2,1)S(1)} %collective-permute-done.11.xt, ...), custom_call_target="tpu_custom_call" | custom-call | flops 10000000000 | bytes 30000000 | tf_op jit(solution)/shard_map/forward/pallas_call | solution.py:170
  75.4 6.9 %collective-permute-done.19.refs_3_ = bf16[3616,128]{1,0:T(8,128)(2,1)S(1)} collective-permute-done((bf16[3616,128]{1,0:T(8,128)(2,1)S(1)}, bf16[3616,128]{1,0:T(8,128)(2,1)S(1)}, u32[]{:S(2)}, u32[]{:S(2)}) %collective-permute-start.19) | collective-permute-done | bytes 925728 | tf_op jit(solution)/shard_map/fpb/ppermute | solution.py:309
  82.4 3.0 %collective-permute-done.20.refs_1_ = bf16[3616,128]{1,0:T(8,128)(2,1)S(1)} collective-permute-done((bf16[3616,128]{1,0:T(8,128)(2,1)S(1)}, bf16[3616,128]{1,0:T(8,128)(2,1)S(1)}, u32[]{:S(2)}, u32[]{:S(2)}) %collective-permute-start.20) | collective-permute-done | bytes 925728 | tf_op jit(solution)/shard_map/pb1/ppermute | solution.py:309
  85.4 2.4 %collective-permute-start.21 = (bf16[3616,128]{1,0:T(8,128)(2,1)S(1)}, bf16[3616,128]{1,0:T(8,128)(2,1)S(1)}, u32[]{:S(2)}, u32[]{:S(2)}) collective-permute-start(bf16[3616,128]{1,0:T(8,128)(2,1)S(1)} %get-tuple-element.105), channel_id=1, source_target_pairs={{0,96},{32,0},{64,32},{96,64},{1,97},{33,1},{65,33},{97,65},{2,98}... | collective-permute-start | bytes 2777096 | tf_op jit(solution)/shard_map/qb2/ppermute | solution.py:309
  88.0 2.5 %collective-permute-start.23 = (bf16[3616,128]{1,0:T(8,128)(2,1)}, bf16[3616,128]{1,0:T(8,128)(2,1)S(1)}, u32[]{:S(2)}, u32[]{:S(2)}) collective-permute-start(bf16[3616,128]{1,0:T(8,128)(2,1)} %copy-done.13), channel_id=1, source_target_pairs={{0,24},{8,0},{16,8},{24,16},{1,25},{9,1},{17,9},{25,17},{2,26},{10... | collective-permute-start | bytes 2777096 | tf_op jit(solution)/shard_map/fqa/ppermute | solution.py:309
  90.5 10.8 %forward.4 = (f32[128,3584]{1,0:T(8,128)S(1)}, f32[128,3584]{1,0:T(8,128)S(1)}, bf16[7,28,256,128]{3,2,1,0:T(8,128)(2,1)S(1)}) custom-call(s32[16]{0:T(128)S(1)} %stack.102.chip_of, bf16[128,4096]{1,0:T(8,128)(2,1)S(1)} %constant_dynamic-update-slice_fusion.xo, ...), custom_call_target="tpu_custom_call", output_to_operand_aliasing={{0}: (13, {}), {1}: (14, {})} | custom-call | flops 13200000000 | bytes 39600000 | tf_op jit(solution)/shard_map/forward/pallas_call | solution.py:170
  101.4 2.8 %collective-permute-done.21.refs_1_ = bf16[3616,128]{1,0:T(8,128)(2,1)S(1)} collective-permute-done((bf16[3616,128]{1,0:T(8,128)(2,1)S(1)}, bf16[3616,128]{1,0:T(8,128)(2,1)S(1)}, u32[]{:S(2)}, u32[]{:S(2)}) %collective-permute-start.21) | collective-permute-done | bytes 925728 | tf_op jit(solution)/shard_map/qb2/ppermute | solution.py:309
  104.2 3.2 %collective-permute-done.22.refs_2_ = bf16[3616,128]{1,0:T(8,128)(2,1)S(1)} collective-permute-done((bf16[3616,128]{1,0:T(8,128)(2,1)}, bf16[3616,128]{1,0:T(8,128)(2,1)S(1)}, u32[]{:S(2)}, u32[]{:S(2)}) %collective-permute-start.22) | collective-permute-done | bytes 925728 | tf_op jit(solution)/shard_map/fqb/ppermute | solution.py:309
  107.4 4.2 %forward.5 = (f32[128,3584]{1,0:T(8,128)S(1)}, f32[128,3584]{1,0:T(8,128)S(1)}, bf16[4,28,256,128]{3,2,1,0:T(8,128)(2,1)S(1)}) custom-call(s32[16]{0:T(128)S(1)} %stack.102.chip_of, bf16[128,4096]{1,0:T(8,128)(2,1)S(1)} %constant_dynamic-update-slice_fusion.xo, ...), custom_call_target="tpu_custom_call", output_to_operand_aliasing={{0}: (7, {}), {1}: (8, {})} | custom-call | flops 8400000000 | bytes 25200000 | tf_op jit(solution)/shard_map/forward/pallas_call | solution.py:170
  111.7 4.9 %collective-permute-start.24 = (f32[128,3584]{1,0:T(8,128)S(1)}, f32[128,3584]{1,0:T(8,128)S(1)}, u32[]{:S(2)}, u32[]{:S(2)}) collective-permute-start(f32[128,3584]{1,0:T(8,128)S(1)} %get-tuple-element.117), channel_id=1, source_target_pairs={{0,4},{4,0},{1,5},{5,1},{2,6},{6,2},{3,7},{7,3},{8,12},{12,8},{9,1... | collective-permute-start | bytes 5505032 | tf_op jit(solution)/shard_map/swap_gate_up/ppermute | solution.py:314
  116.6 3.4 %collective-permute-done.24.got = f32[128,3584]{1,0:T(8,128)S(1)} collective-permute-done((f32[128,3584]{1,0:T(8,128)S(1)}, f32[128,3584]{1,0:T(8,128)S(1)}, u32[]{:S(2)}, u32[]{:S(2)}) %collective-permute-start.24) | collective-permute-done | bytes 1835040 | tf_op jit(solution)/shard_map/swap_gate_up/ppermute | solution.py:314
  120.0 2.6 %activate.1 = (bf16[128,3584]{1,0:T(8,128)(2,1)}, bf16[128,3584]{1,0:T(8,128)(2,1)S(1)}, bf16[128,3584]{1,0:T(8,128)(2,1)S(1)}) custom-call(s32[3]{0:T(128)S(1)} %pad_add_fusion.scal, f32[128,3584]{1,0:T(8,128)S(1)} %get-tuple-element.116.mine, f32[128,3584]{1,0:T(8,128)S(1)} %collective-permute-done.24.got, bf16[128,3584]{1,0:T(8,128)(2,1)S(1)} %copy-done), custom_call_target="tpu_custom_call" | custom-call | flops 4000000000 | bytes 12000000 | tf_op jit(solution)/shard_map/activate/pallas_call | solution.py:210
  123.0 2.1 %collective-permute-done.25.other = bf16[128,3584]{1,0:T(8,128)(2,1)S(1)} collective-permute-done((bf16[128,3584]{1,0:T(8,128)(2,1)S(1)}, bf16[128,3584]{1,0:T(8,128)(2,1)S(1)}, u32[]{:S(2)}, u32[]{:S(2)}) %collective-permute-start.25) | collective-permute-done | bytes 917536 | tf_op jit(solution)/shard_map/swap_d/ppermute | solution.py:314
  125.1 6.3 %backward.3 = (f32[128,2304]{1,0:T(8,128)S(1)}, bf16[128,2304]{1,0:T(8,128)(2,1)S(1)}) custom-call(bf16[128,3584]{1,0:T(8,128)(2,1)S(1)} %get-tuple-element.119.own, bf16[128,3584]{1,0:T(8,128)(2,1)S(1)} %collective-permute-done.25.other, bf16[5,28,256,128]{3,2,1,0:T(8,128)(2,1)S(1)} %get-tuple-element.123.refs_0_, ...), custom_call_target="tpu_custom_call" | custom-call | flops 8650000384 | bytes 25950000 | tf_op jit(solution)/shard_map/backward/pallas_call | solution.py:243
  131.8 4.9 %backward.2 = (f32[128,1792]{1,0:T(8,128)S(1)}, bf16[128,1792]{1,0:T(8,128)(2,1)S(1)}) custom-call(bf16[128,3584]{1,0:T(8,128)(2,1)S(1)} %get-tuple-element.119.own, bf16[128,3584]{1,0:T(8,128)(2,1)S(1)} %collective-permute-done.25.other, bf16[7,28,256,128]{3,2,1,0:T(8,128)(2,1)S(1)} %get-tuple-element.121.refs_0_), custom_call_target="tpu_custom_call" | custom-call | flops 6950000128 | bytes 20850000 | tf_op jit(solution)/shard_map/backward/pallas_call | solution.py:243
  136.9 1.7 %collective-permute-done.26.refs_2_ = bf16[128,1792]{1,0:T(8,128)(2,1)S(1)} collective-permute-done((bf16[128,1792]{1,0:T(8,128)(2,1)S(1)}, bf16[128,1792]{1,0:T(8,128)(2,1)S(1)}, u32[]{:S(2)}, u32[]{:S(2)}) %collective-permute-start.26) | collective-permute-done | bytes 458784 | tf_op jit(solution)/shard_map/swap_part/ppermute | solution.py:314
  138.8 2.0 %collective-permute-start.28 = (bf16[32,4096]{1,0:T(8,128)(2,1)S(1)}, bf16[32,4096]{1,0:T(8,128)(2,1)S(1)}, u32[]{:S(2)}, u32[]{:S(2)}) collective-permute-start(bf16[32,4096]{1,0:T(8,128)(2,1)S(1)} %get-tuple-element.129), channel_id=1, source_target_pairs={{0,3},{1,0},{2,1},{3,2},{4,7},{5,4},{6,5},{7,6},{8,11},{9,8},{10,9... | collective-permute-start | bytes 786440 | tf_op jit(solution)/shard_map/send_back/ppermute | solution.py:309
  141.6 5.0 %collective-permute-done.28.refs_1_ = bf16[32,4096]{1,0:T(8,128)(2,1)S(1)} collective-permute-done((bf16[32,4096]{1,0:T(8,128)(2,1)S(1)}, bf16[32,4096]{1,0:T(8,128)(2,1)S(1)}, u32[]{:S(2)}, u32[]{:S(2)}) %collective-permute-start.28) | collective-permute-done | bytes 262176 | tf_op jit(solution)/shard_map/send_back/ppermute | solution.py:309
  146.6 3.2 %collective-permute-done.29.refs_2_ = bf16[32,4096]{1,0:T(8,128)(2,1)S(1)} collective-permute-done((bf16[32,4096]{1,0:T(8,128)(2,1)S(1)}, bf16[32,4096]{1,0:T(8,128)(2,1)S(1)}, u32[]{:S(2)}, u32[]{:S(2)}) %collective-permute-start.29) | collective-permute-done | bytes 262176 | tf_op jit(solution)/shard_map/send_back/ppermute | solution.py:309
  149.8 5.8 %collective-permute-done.30.refs_3_ = bf16[32,4096]{1,0:T(8,128)(2,1)S(1)} collective-permute-done((bf16[32,4096]{1,0:T(8,128)(2,1)S(1)}, bf16[32,4096]{1,0:T(8,128)(2,1)S(1)}, u32[]{:S(2)}, u32[]{:S(2)}) %collective-permute-start.30) | collective-permute-done | bytes 262176 | tf_op jit(solution)/shard_map/send_back/ppermute | solution.py:309
  (90 shorter events, 14.9 us)
Async XLA Ops:
  2.0 3.1 %collective-permute-start.1 = (bf16[17,128,128]{2,1,0:T(8,128)(2,1)S(1)}, bf16[17,128,128]{2,1,0:T(8,128)(2,1)S(1)}, u32[]{:S(2)}, u32[]{:S(2)}) collective-permute-start(bf16[17,128,128]{2,1,0:T(8,128)(2,1)S(1)} %get-tuple-element.132), channel_id=1, source_target_pairs={{0,4},{4,0},{1,5},{5,1},{2,6},{6,2},{3,7},{7,3},{8,12},{12,8},{9,1... | collective-permute-start | bytes 1671176 | tf_op jit(solution)/shard_map/swap_blocks/ppermute | solution.py:314
  3.5 1.6 %collective-permute-start = (s32[17]{0:T(128)S(1)}, s32[17]{0:T(128)S(1)}, u32[]{:S(2)}, u32[]{:S(2)}) collective-permute-start(s32[17]{0:T(128)S(1)} %get-tuple-element.134), channel_id=1, source_target_pairs={{0,4},{4,0},{1,5},{5,1},{2,6},{6,2},{3,7},{7,3},{8,12},{12,8},{9,1... | collective-permute-start | bytes 212 | tf_op jit(solution)/shard_map/swap_index/ppermute | solution.py:314
  5.7 32.3 %copy-start.5 = (bf16[1808,128]{1,0:T(8,128)(2,1)}, bf16[1808,128]{1,0:T(8,128)(2,1)S(1)}, u32[]{:S(2)}) copy-start(bf16[1808,128]{1,0:T(8,128)(2,1)S(1)} %get-tuple-element.88.a.refs_0_) | copy-start | bytes 1388548
  5.7 13.1 %collective-permute-start.7 = (bf16[1808,128]{1,0:T(8,128)(2,1)S(1)}, bf16[1808,128]{1,0:T(8,128)(2,1)S(1)}, u32[]{:S(2)}, u32[]{:S(2)}) collective-permute-start(bf16[1808,128]{1,0:T(8,128)(2,1)S(1)} %get-tuple-element.88.a.refs_0_), channel_id=1, source_target_pairs={{0,32},{32,64},{64,96},{96,0},{1,33},{33,65},{65,97},{97,1},{2,34}... | collective-permute-start | bytes 1388552 | tf_op jit(solution)/shard_map/a1/ppermute | solution.py:309
  7.1 12.0 %collective-permute-start.8 = (bf16[1808,128]{1,0:T(8,128)(2,1)S(1)}, bf16[1808,128]{1,0:T(8,128)(2,1)S(1)}, u32[]{:S(2)}, u32[]{:S(2)}) collective-permute-start(bf16[1808,128]{1,0:T(8,128)(2,1)S(1)} %get-tuple-element.89.c.refs_1_), channel_id=1, source_target_pairs={{0,24},{8,0},{16,8},{24,16},{1,25},{9,1},{17,9},{25,17},{2,26},{10... | collective-permute-start | bytes 1388552 | tf_op jit(solution)/shard_map/b2/ppermute | solution.py:309
  9.8 13.9 %collective-permute-start.3 = (bf16[1808,128]{1,0:T(8,128)(2,1)S(1)}, bf16[1808,128]{1,0:T(8,128)(2,1)S(1)}, u32[]{:S(2)}, u32[]{:S(2)}) collective-permute-start(bf16[1808,128]{1,0:T(8,128)(2,1)S(1)} %get-tuple-element.88.a.refs_0_), channel_id=1, source_target_pairs={{0,96},{32,0},{64,32},{96,64},{1,97},{33,1},{65,33},{97,65},{2,98}... | collective-permute-start | bytes 1388552 | tf_op jit(solution)/shard_map/a2/ppermute | solution.py:309
  11.3 12.5 %collective-permute-start.4 = (bf16[1808,128]{1,0:T(8,128)(2,1)S(1)}, bf16[1808,128]{1,0:T(8,128)(2,1)S(1)}, u32[]{:S(2)}, u32[]{:S(2)}) collective-permute-start(bf16[1808,128]{1,0:T(8,128)(2,1)S(1)} %get-tuple-element.89.c.refs_1_), channel_id=1, source_target_pairs={{0,8},{8,16},{16,24},{24,0},{1,9},{9,17},{17,25},{25,1},{2,10},{10... | collective-permute-start | bytes 1388552 | tf_op jit(solution)/shard_map/b1/ppermute | solution.py:309
  11.3 12.5 %collective-permute-start.2 = (bf16[32,4096]{1,0:T(8,128)(2,1)S(1)}, bf16[32,4096]{1,0:T(8,128)(2,1)S(1)}, u32[]{:S(2)}, u32[]{:S(2)}) collective-permute-start(bf16[32,4096]{1,0:T(8,128)(2,1)S(1)} %copy-done.9), channel_id=1, source_target_pairs={{0,1},{1,2},{2,3},{3,0},{4,5},{5,6},{6,7},{7,4},{8,9},{9,10},{10,1... | collective-permute-start | bytes 786440 | tf_op jit(solution)/shard_map/tokens/ppermute | solution.py:309
  19.1 15.3 %collective-permute-start.10 = (bf16[1808,128]{1,0:T(8,128)(2,1)S(1)}, bf16[1808,128]{1,0:T(8,128)(2,1)S(1)}, u32[]{:S(2)}, u32[]{:S(2)}) collective-permute-start(bf16[1808,128]{1,0:T(8,128)(2,1)S(1)} %collective-permute-done.8.d.refs_5_), channel_id=1, source_target_pairs={{0,24},{8,0},{16,8},{24,16},{1,25},{9,1},{17,9},{25,17},{2,26},{10... | collective-permute-start | bytes 1388552 | tf_op jit(solution)/shard_map/b3/ppermute | solution.py:309
  22.6 11.9 %collective-permute-start.9 = (bf16[1808,128]{1,0:T(8,128)(2,1)S(1)}, bf16[1808,128]{1,0:T(8,128)(2,1)S(1)}, u32[]{:S(2)}, u32[]{:S(2)}) collective-permute-start(bf16[1808,128]{1,0:T(8,128)(2,1)S(1)} %collective-permute-done.7.b.refs_0_), channel_id=1, source_target_pairs={{0,32},{32,64},{64,96},{96,0},{1,33},{33,65},{65,97},{97,1},{2,34}... | collective-permute-start | bytes 1388552 | tf_op jit(solution)/shard_map/a3/ppermute | solution.py:309
  23.8 10.6 %collective-permute-start.6 = (bf16[32,4096]{1,0:T(8,128)(2,1)S(1)}, bf16[32,4096]{1,0:T(8,128)(2,1)S(1)}, u32[]{:S(2)}, u32[]{:S(2)}) collective-permute-start(bf16[32,4096]{1,0:T(8,128)(2,1)S(1)} %copy-done.9), channel_id=1, source_target_pairs={{0,3},{1,0},{2,1},{3,2},{4,7},{5,4},{6,5},{7,6},{8,11},{9,8},{10,9... | collective-permute-start | bytes 786440 | tf_op jit(solution)/shard_map/tokens/ppermute | solution.py:309
  27.7 6.8 %collective-permute-start.5 = (bf16[32,4096]{1,0:T(8,128)(2,1)S(1)}, bf16[32,4096]{1,0:T(8,128)(2,1)S(1)}, u32[]{:S(2)}, u32[]{:S(2)}) collective-permute-start(bf16[32,4096]{1,0:T(8,128)(2,1)S(1)} %collective-permute-done.2), channel_id=1, source_target_pairs={{0,1},{1,2},{2,3},{3,0},{4,5},{5,6},{6,7},{7,4},{8,9},{9,10},{10,1... | collective-permute-start | bytes 786440 | tf_op jit(solution)/shard_map/tokens/ppermute | solution.py:309
  34.5 32.7 %collective-permute-start.11 = (bf16[128,4096]{1,0:T(8,128)(2,1)S(1)}, bf16[128,4096]{1,0:T(8,128)(2,1)S(1)}, u32[]{:S(2)}, u32[]{:S(2)}) collective-permute-start(bf16[128,4096]{1,0:T(8,128)(2,1)S(1)} %constant_dynamic-update-slice_fusion.xo), channel_id=1, source_target_pairs={{0,4},{4,0},{1,5},{5,1},{2,6},{6,2},{3,7},{7,3},{8,12},{12,8},{9,1... | collective-permute-start | bytes 3145736 | tf_op jit(solution)/shard_map/swap_tokens/ppermute | solution.py:314
  38.2 21.5 %collective-permute-start.15 = (bf16[3616,128]{1,0:T(8,128)(2,1)S(1)}, bf16[3616,128]{1,0:T(8,128)(2,1)S(1)}, u32[]{:S(2)}, u32[]{:S(2)}) collective-permute-start(bf16[3616,128]{1,0:T(8,128)(2,1)S(1)} %get-tuple-element.104), channel_id=1, source_target_pairs={{0,96},{32,0},{64,32},{96,64},{1,97},{33,1},{65,33},{97,65},{2,98}... | collective-permute-start | bytes 2777096 | tf_op jit(solution)/shard_map/pb2/ppermute | solution.py:309
  39.7 22.4 %collective-permute-start.14 = (bf16[3616,128]{1,0:T(8,128)(2,1)S(1)}, bf16[3616,128]{1,0:T(8,128)(2,1)S(1)}, u32[]{:S(2)}, u32[]{:S(2)}) collective-permute-start(bf16[3616,128]{1,0:T(8,128)(2,1)S(1)} %get-tuple-element.105), channel_id=1, source_target_pairs={{0,32},{32,64},{64,96},{96,0},{1,33},{33,65},{65,97},{97,1},{2,34}... | collective-permute-start | bytes 2777096 | tf_op jit(solution)/shard_map/qb1/ppermute | solution.py:309
  39.7 22.4 %collective-permute-start.13 = (bf16[3616,128]{1,0:T(8,128)(2,1)S(1)}, bf16[3616,128]{1,0:T(8,128)(2,1)S(1)}, u32[]{:S(2)}, u32[]{:S(2)}) collective-permute-start(bf16[3616,128]{1,0:T(8,128)(2,1)S(1)} %get-tuple-element.100), channel_id=1, source_target_pairs={{0,8},{8,16},{16,24},{24,0},{1,9},{9,17},{17,25},{25,1},{2,10},{10... | collective-permute-start | bytes 2777096 | tf_op jit(solution)/shard_map/pa1/ppermute | solution.py:309
  39.7 22.4 %collective-permute-start.12 = (bf16[3616,128]{1,0:T(8,128)(2,1)S(1)}, bf16[3616,128]{1,0:T(8,128)(2,1)S(1)}, u32[]{:S(2)}, u32[]{:S(2)}) collective-permute-start(bf16[3616,128]{1,0:T(8,128)(2,1)S(1)} %get-tuple-element.101), channel_id=1, source_target_pairs={{0,24},{8,0},{16,8},{24,16},{1,25},{9,1},{17,9},{25,17},{2,26},{10... | collective-permute-start | bytes 2777096 | tf_op jit(solution)/shard_map/qa2/ppermute | solution.py:309
  62.1 20.3 %collective-permute-start.19 = (bf16[3616,128]{1,0:T(8,128)(2,1)S(1)}, bf16[3616,128]{1,0:T(8,128)(2,1)S(1)}, u32[]{:S(2)}, u32[]{:S(2)}) collective-permute-start(bf16[3616,128]{1,0:T(8,128)(2,1)S(1)} %collective-permute-done.15.refs_6_), channel_id=1, source_target_pairs={{0,96},{32,0},{64,32},{96,64},{1,97},{33,1},{65,33},{97,65},{2,98}... | collective-permute-start | bytes 2777096 | tf_op jit(solution)/shard_map/fpb/ppermute | solution.py:309
  64.5 20.9 %collective-permute-start.20 = (bf16[3616,128]{1,0:T(8,128)(2,1)S(1)}, bf16[3616,128]{1,0:T(8,128)(2,1)S(1)}, u32[]{:S(2)}, u32[]{:S(2)}) collective-permute-start(bf16[3616,128]{1,0:T(8,128)(2,1)S(1)} %get-tuple-element.104), channel_id=1, source_target_pairs={{0,32},{32,64},{64,96},{96,0},{1,33},{33,65},{65,97},{97,1},{2,34}... | collective-permute-start | bytes 2777096 | tf_op jit(solution)/shard_map/pb1/ppermute | solution.py:309
  64.5 20.9 %collective-permute-start.16 = (bf16[3616,128]{1,0:T(8,128)(2,1)S(1)}, bf16[3616,128]{1,0:T(8,128)(2,1)S(1)}, u32[]{:S(2)}, u32[]{:S(2)}) collective-permute-start(bf16[3616,128]{1,0:T(8,128)(2,1)S(1)} %collective-permute-done.13.refs_2_), channel_id=1, source_target_pairs={{0,8},{8,16},{16,24},{24,0},{1,9},{9,17},{17,25},{25,1},{2,10},{10... | collective-permute-start | bytes 2777096 | tf_op jit(solution)/shard_map/fpa/ppermute | solution.py:309
  64.5 20.9 %collective-permute-start.17 = (bf16[3616,128]{1,0:T(8,128)(2,1)S(1)}, bf16[3616,128]{1,0:T(8,128)(2,1)S(1)}, u32[]{:S(2)}, u32[]{:S(2)}) collective-permute-start(bf16[3616,128]{1,0:T(8,128)(2,1)S(1)} %get-tuple-element.100), channel_id=1, source_target_pairs={{0,24},{8,0},{16,8},{24,16},{1,25},{9,1},{17,9},{25,17},{2,26},{10... | collective-permute-start | bytes 2777096 | tf_op jit(solution)/shard_map/pa2/ppermute | solution.py:309
  85.4 18.8 %collective-permute-start.21 = (bf16[3616,128]{1,0:T(8,128)(2,1)S(1)}, bf16[3616,128]{1,0:T(8,128)(2,1)S(1)}, u32[]{:S(2)}, u32[]{:S(2)}) collective-permute-start(bf16[3616,128]{1,0:T(8,128)(2,1)S(1)} %get-tuple-element.105), channel_id=1, source_target_pairs={{0,96},{32,0},{64,32},{96,64},{1,97},{33,1},{65,33},{97,65},{2,98}... | collective-permute-start | bytes 2777096 | tf_op jit(solution)/shard_map/qb2/ppermute | solution.py:309
  87.8 19.6 %collective-permute-start.22 = (bf16[3616,128]{1,0:T(8,128)(2,1)}, bf16[3616,128]{1,0:T(8,128)(2,1)S(1)}, u32[]{:S(2)}, u32[]{:S(2)}) collective-permute-start(bf16[3616,128]{1,0:T(8,128)(2,1)} %copy-done.12), channel_id=1, source_target_pairs={{0,32},{32,64},{64,96},{96,0},{1,33},{33,65},{65,97},{97,1},{2,34}... | collective-permute-start | bytes 2777096 | tf_op jit(solution)/shard_map/fqb/ppermute | solution.py:309
  87.8 19.6 %collective-permute-start.18 = (bf16[3616,128]{1,0:T(8,128)(2,1)S(1)}, bf16[3616,128]{1,0:T(8,128)(2,1)S(1)}, u32[]{:S(2)}, u32[]{:S(2)}) collective-permute-start(bf16[3616,128]{1,0:T(8,128)(2,1)S(1)} %get-tuple-element.101), channel_id=1, source_target_pairs={{0,8},{8,16},{16,24},{24,0},{1,9},{9,17},{17,25},{25,1},{2,10},{10... | collective-permute-start | bytes 2777096 | tf_op jit(solution)/shard_map/qa1/ppermute | solution.py:309
  88.0 19.4 %collective-permute-start.23 = (bf16[3616,128]{1,0:T(8,128)(2,1)}, bf16[3616,128]{1,0:T(8,128)(2,1)S(1)}, u32[]{:S(2)}, u32[]{:S(2)}) collective-permute-start(bf16[3616,128]{1,0:T(8,128)(2,1)} %copy-done.13), channel_id=1, source_target_pairs={{0,24},{8,0},{16,8},{24,16},{1,25},{9,1},{17,9},{25,17},{2,26},{10... | collective-permute-start | bytes 2777096 | tf_op jit(solution)/shard_map/fqa/ppermute | solution.py:309
  111.7 8.3 %collective-permute-start.24 = (f32[128,3584]{1,0:T(8,128)S(1)}, f32[128,3584]{1,0:T(8,128)S(1)}, u32[]{:S(2)}, u32[]{:S(2)}) collective-permute-start(f32[128,3584]{1,0:T(8,128)S(1)} %get-tuple-element.117), channel_id=1, source_target_pairs={{0,4},{4,0},{1,5},{5,1},{2,6},{6,2},{3,7},{7,3},{8,12},{12,8},{9,1... | collective-permute-start | bytes 5505032 | tf_op jit(solution)/shard_map/swap_gate_up/ppermute | solution.py:314
  122.6 2.5 %collective-permute-start.25 = (bf16[128,3584]{1,0:T(8,128)(2,1)S(1)}, bf16[128,3584]{1,0:T(8,128)(2,1)S(1)}, u32[]{:S(2)}, u32[]{:S(2)}) collective-permute-start(bf16[128,3584]{1,0:T(8,128)(2,1)S(1)} %get-tuple-element.120), channel_id=1, source_target_pairs={{0,4},{4,0},{1,5},{5,1},{2,6},{6,2},{3,7},{7,3},{8,12},{12,8},{9,1... | collective-permute-start | bytes 2752520 | tf_op jit(solution)/shard_map/swap_d/ppermute | solution.py:314
  131.4 7.3 %collective-permute-start.27 = (bf16[128,2304]{1,0:T(8,128)(2,1)S(1)}, bf16[128,2304]{1,0:T(8,128)(2,1)S(1)}, u32[]{:S(2)}, u32[]{:S(2)}) collective-permute-start(bf16[128,2304]{1,0:T(8,128)(2,1)S(1)} %get-tuple-element.127), channel_id=1, source_target_pairs={{0,4},{4,0},{1,5},{5,1},{2,6},{6,2},{3,7},{7,3},{8,12},{12,8},{9,1... | collective-permute-start | bytes 1769480 | tf_op jit(solution)/shard_map/swap_part/ppermute | solution.py:314
  136.7 1.9 %collective-permute-start.26 = (bf16[128,1792]{1,0:T(8,128)(2,1)S(1)}, bf16[128,1792]{1,0:T(8,128)(2,1)S(1)}, u32[]{:S(2)}, u32[]{:S(2)}) collective-permute-start(bf16[128,1792]{1,0:T(8,128)(2,1)S(1)} %get-tuple-element.126), channel_id=1, source_target_pairs={{0,4},{4,0},{1,5},{5,1},{2,6},{6,2},{3,7},{7,3},{8,12},{12,8},{9,1... | collective-permute-start | bytes 1376264 | tf_op jit(solution)/shard_map/swap_part/ppermute | solution.py:314
  138.8 7.8 %collective-permute-start.28 = (bf16[32,4096]{1,0:T(8,128)(2,1)S(1)}, bf16[32,4096]{1,0:T(8,128)(2,1)S(1)}, u32[]{:S(2)}, u32[]{:S(2)}) collective-permute-start(bf16[32,4096]{1,0:T(8,128)(2,1)S(1)} %get-tuple-element.129), channel_id=1, source_target_pairs={{0,3},{1,0},{2,1},{3,2},{4,7},{5,4},{6,5},{7,6},{8,11},{9,8},{10,9... | collective-permute-start | bytes 786440 | tf_op jit(solution)/shard_map/send_back/ppermute | solution.py:309
  140.8 9.0 %collective-permute-start.29 = (bf16[32,4096]{1,0:T(8,128)(2,1)S(1)}, bf16[32,4096]{1,0:T(8,128)(2,1)S(1)}, u32[]{:S(2)}, u32[]{:S(2)}) collective-permute-start(bf16[32,4096]{1,0:T(8,128)(2,1)S(1)} %get-tuple-element.130), channel_id=1, source_target_pairs={{0,2},{1,3},{2,0},{3,1},{4,6},{5,7},{6,4},{7,5},{8,10},{9,11},{10,... | collective-permute-start | bytes 786440 | tf_op jit(solution)/shard_map/send_back/ppermute | solution.py:309
  140.8 14.8 %collective-permute-start.30 = (bf16[32,4096]{1,0:T(8,128)(2,1)S(1)}, bf16[32,4096]{1,0:T(8,128)(2,1)S(1)}, u32[]{:S(2)}, u32[]{:S(2)}) collective-permute-start(bf16[32,4096]{1,0:T(8,128)(2,1)S(1)} %get-tuple-element.131), channel_id=1, source_target_pairs={{0,1},{1,2},{2,3},{3,0},{4,5},{5,6},{6,7},{7,4},{8,9},{9,10},{10,1... | collective-permute-start | bytes 786440 | tf_op jit(solution)/shard_map/send_back/ppermute | solution.py:309
  (19 other events, 176.6 us)

commit v5 on v4

--- a/solution.py
+++ b/solution.py
@@ -102,7 +102,7 @@
 
     def kernel(chip_of, xo, xt, *refs):
         parts, refs = refs[:given], refs[given + len(carry) :]
-        acc_own, acc_other, panels, buf, tiles, ints, marks, sem_t, sem_b, sem_m = refs
+        acc_own, *acc_other, panels, buf, tiles, ints, marks, sem_t, sem_b, sem_m = refs
         direct = all(inside)
         if not direct:
             moved = []
@@ -121,7 +121,8 @@
                         ).start()
         if not carry:
             acc_own[...] = jnp.zeros_like(acc_own)
-            acc_other[...] = jnp.zeros_like(acc_other)
+            for acc in acc_other:
+                acc[...] = jnp.zeros_like(acc)
         for i in range(2 * count):
             if direct:
                 part, row, rows, to = units[i // 2][i % 2][-1]
@@ -157,7 +158,8 @@
                 r = jnp.dot(x, w, preferred_element_type=F32)
                 span = pl.ds(c * 2 * BLK, 2 * BLK)
                 acc_own[:, span] += r[:BLK]
-                acc_other[:, span] += r[BLK:]
+                there = pl.ds(c % (NCB // 4) * 2 * BLK, 2 * BLK)
+                acc_other[c // (NCB // 4)][:, there] += r[BLK:]
             return 0
 
         if direct:
@@ -166,12 +168,12 @@
         else:
             lax.fori_loop(0, count, step, 0)
 
-    acc = pltpu.VMEM((BLK, HID), F32)
+    acc, half = pltpu.VMEM((BLK, HID), F32), pltpu.VMEM((BLK, HID // 2), F32)
     return pl.pallas_call(
         kernel,
-        out_shape=(acc, acc, pltpu.VMEM((count, NCB, 2 * BLK, BLK), BF16)),
+        out_shape=(acc, half, half, pltpu.VMEM((count, NCB, 2 * BLK, BLK), BF16)),
         in_specs=[SMEM, VMEM, VMEM] + [VMEM if i else HBM for i in inside] + [VMEM] * len(carry),
-        out_specs=(VMEM, VMEM, VMEM),
+        out_specs=(VMEM,) * 4,
         scratch_shapes=[
             pltpu.VMEM((count, 2, UNIT, BLK), BF16),
             pltpu.VMEM((2 * count, 16, BLK), BF16),
@@ -188,32 +190,35 @@
     )(chips, x_own, x_other, *[p if i else pltpu.with_memory_space_constraint(p, pltpu.HBM) for p, i in zip(pieces, inside)], *carry)
 
 
-def act_kernel(scal, mine, got, d_hidden, hidden, d_mine, d_send):
-    def work(gate_ref, up_ref, d_gate, d_up):
-        for k in range(4):
-            rel = pl.ds(k * ROWS, ROWS)
-            real = pl.ds(pl.multiple_of((scal[1] - k + 4) % 4 * ROWS, ROWS), ROWS)
-            gate, up = gate_ref[rel, :], up_ref[rel, :]
-            d = d_hidden[real, :].astype(F32)
-            sig = jax.nn.sigmoid(gate)
-            active = gate * sig
-            hidden[real, :] = (active * up).astype(BF16)
-            d_gate[rel, :] = (d * up * sig * (1.0 + gate * (1.0 - sig))).astype(BF16)
-            d_up[rel, :] = (d * active).astype(BF16)
-
-    pl.when(scal[0] == 0)(lambda: work(mine, got, d_mine, d_send))
-    pl.when(scal[0] != 0)(lambda: work(got, mine, d_send, d_mine))
-
-
-def activate(scal, mine, got, d_hidden):
-    one = pltpu.VMEM((BLK, HID), BF16)
-    return pl.pallas_call(
-        act_kernel,
-        out_shape=(jax.ShapeDtypeStruct((BLK, HID), BF16), one, one),
+def activate(half, scal, mine, got, d_hidden):
+    wide = HID // 2
+    part = slice(half * wide, (half + 1) * wide)
+
+    def kernel(scal, mine, got, d_hidden, hidden, d_mine, d_send):
+        def work(gate_of, up_of, d_gate, d_up):
+            for k in range(4):
+                rel = pl.ds(k * ROWS, ROWS)
+                real = pl.ds(pl.multiple_of((scal[1] - k + 4) % 4 * ROWS, ROWS), ROWS)
+                gate, up = gate_of(rel), up_of(rel)
+                d = d_hidden[real, part].astype(F32)
+                sig = jax.nn.sigmoid(gate)
+                active = gate * sig
+                hidden[real, :] = (active * up).astype(BF16)
+                d_gate[rel, :] = (d * up * sig * (1.0 + gate * (1.0 - sig))).astype(BF16)
+                d_up[rel, :] = (d * active).astype(BF16)
+
+        here, there = (lambda rows: mine[rows, part]), (lambda rows: got[rows, :])
+        pl.when(scal[0] == 0)(lambda: work(here, there, d_mine, d_send))
+        pl.when(scal[0] != 0)(lambda: work(there, here, d_send, d_mine))
+
+    one = pltpu.VMEM((BLK, wide), BF16)
+    return pl.pallas_call(
+        kernel,
+        out_shape=(one, one, one),
         in_specs=[SMEM, VMEM, VMEM, VMEM],
         out_specs=(VMEM, VMEM, VMEM),
         compiler_params=params(8),
-        cost_estimate=cost(4),
+        cost_estimate=cost(2),
         name="activate",
     )(scal, mine, got, d_hidden)
 
@@ -222,10 +227,10 @@
     count = [p.shape[0] for p in panels]
     width = sum(count) * 2 * BLK
 
-    def kernel(own, other, *refs):
-        parts, (out_own, out_other, both) = refs[:-3], refs[-3:]
-        both[:BLK] = own[...]
-        both[BLK:] = other[...]
+    def kernel(*refs):
+        parts, (out_own, out_other, both) = refs[4:-3], refs[-3:]
+        for i in range(4):
+            both[i // 2 * BLK : (i // 2 + 1) * BLK, i % 2 * (HID // 2) : (i % 2 + 1) * (HID // 2)] = refs[i][...]
         done = 0
         for part, n in zip(parts, count):
 
@@ -237,19 +242,19 @@
                 out_other[:, cols] = r[BLK:].astype(BF16)
                 return 0
 
-            lax.fori_loop(0, n, step, 0)
+            lax.fori_loop(0, n, step, 0, unroll=True)
             done += n
 
     return pl.pallas_call(
         kernel,
         out_shape=(pltpu.VMEM((BLK, width), F32), pltpu.VMEM((BLK, width), BF16)),
-        in_specs=[VMEM] * (2 + len(panels)),
+        in_specs=[VMEM] * (4 + len(panels)),
         out_specs=(VMEM, VMEM),
         scratch_shapes=[pltpu.VMEM((2 * BLK, HID), BF16)],
         compiler_params=params(8),
         cost_estimate=cost(0.85 * sum(count) + 1),
         name="backward",
-    )(d_own, d_other, *panels)
+    )(*d_own, *d_other, *panels)
 
 
 def join(owns, gots):
@@ -397,12 +402,13 @@
         carry, panel = stage(which, at, carry, (qa1, qb2, fqa, fqb))
         panels.append(panel)
         at += len(which)
-    acc_own, acc_other = carry
-    got = swap(acc_other, "swap_gate_up")
-    hidden, d_mine, d_send = activate(scal, acc_own, got, d_hidden)
-    d_other = swap(d_send, "swap_d")
+    acc_own, *acc_other = carry
+    got = [swap(acc, "swap_gate_up") for acc in acc_other]
+    done = [activate(half, scal, acc_own, got[half], d_hidden) for half in range(2)]
+    hidden = jnp.concatenate([d[0] for d in done], axis=1)
+    d_mine, d_other = [d[1] for d in done], [swap(d[2], "swap_d") for d in done]
     parts = []
-    for some in (panels[1:2], panels[0::2]):
+    for some in (panels[1::-1], panels[2:]):
         part_own, part_other = backward(d_mine, d_other, some)
         parts.append((part_own, swap(part_other, "swap_part")))
     keep, *sends = join([p[0] for p in parts], [p[1] for p in parts])

time: 157 us -> 153 us (0.975)
  Pallas kernels: 39.5 us -> 36 us
  waiting for transfers between devices: 71 us -> 67.6 us
    pallas_call x2, Pallas kernels: 11.2 us -> 7.96 us  [backward(): pl.pallas_call(kernel, out_shape=(pltpu.VMEM((BLK, width), F32), pltpu.VM...]
    ppermute x7 -> x9, waiting for transfers between devices: 8.4 us -> 5.97 us  [swap(): return lax.ppermute(a, 'c', SWAP)]
    ppermute x7 -> x9, starting transfers between devices: 10.8 us -> 11.4 us  [swap(): return lax.ppermute(a, 'c', SWAP)]
    pallas_call x4 -> x5, Pallas kernels: 25.9 us -> 25.5 us  [the longest x3 23.3 us: forward(): pl.pallas_call(kernel, out_shape=(acc, half, half, pltpu.VMEM((count, NCB...]
  transfers between devices with their start and end apart: 31 -> 33, of which waited for: 16 -> 17; matrix products, arithmetic and copies ran while one was open for 0% -> 1% of each run, Pallas kernels for 15% -> 15%
where the time goes in v5:
time: 153 us
  waiting for transfers between devices  67.6 us (44%)
  starting transfers between devices  44.2 us (29%)
  Pallas kernels  36 us (24%)
  other arithmetic  2.36 us (2%)
  local copies, waits for them, and re-layouts  1.75 us (1%)
    ppermute x24, waiting for transfers between devices, shift(): return lax.ppermute(a, axis, [(i, (i + by) % 4) for i in range(4)])  61.6 us
    ppermute x24, starting transfers between devices, shift(): return lax.ppermute(a, axis, [(i, (i + by) % 4) for i in range(4)])  32.8 us
    pallas_call x3, Pallas kernels, forward(): pl.pallas_call(kernel, out_shape=(acc, half, half, pltpu.VMEM((count, NCB...  23.3 us
    ppermute x9, starting transfers between devices, swap(): return lax.ppermute(a, 'c', SWAP)  11.4 us
    pallas_call x2, Pallas kernels, backward(): pl.pallas_call(kernel, out_shape=(pltpu.VMEM((BLK, width), F32), pltpu.VM...  7.96 us
    ppermute x9, waiting for transfers between devices, swap(): return lax.ppermute(a, 'c', SWAP)  5.97 us
  transfers between devices with their start and end apart: 33, of which 17 were waited for; matrix products, arithmetic and copies ran while one was open for 1% of the time, Pallas kernels for 15%

profile of v5, /device:TPU:1, one launch (start us, length us, event | category | flops | bytes accessed | tf_op | source)
XLA Modules:
  0.0 153.0 jit_solution(15812329667437416661)
XLA Ops:
  2.0 1.5 collective-permute-start.1
  7.1 2.7 %collective-permute-start.8 = (bf16[1808,128]{1,0:T(8,128)(2,1)S(1)}, bf16[1808,128]{1,0:T(8,128)(2,1)S(1)}, u32[]{:S(2)}, u32[]{:S(2)}) collective-permute-start(bf16[1808,128]{1,0:T(8,128)(2,1)S(1)} %get-tuple-element.96.c.refs_1_), channel_id=1, source_target_pairs={{0,24},{8,0},{16,8},{24,16},{1,25},{9,1},{17,9},{25,17},{2,26},{10... | collective-permute-start | bytes 1388552 | tf_op jit(solution)/shard_map/b2/ppermute | solution.py:314
  11.3 1.6 %collective-permute-start.2 = (bf16[32,4096]{1,0:T(8,128)(2,1)S(1)}, bf16[32,4096]{1,0:T(8,128)(2,1)S(1)}, u32[]{:S(2)}, u32[]{:S(2)}) collective-permute-start(bf16[32,4096]{1,0:T(8,128)(2,1)S(1)} %copy-done.11), channel_id=1, source_target_pairs={{0,1},{1,2},{2,3},{3,0},{4,5},{5,6},{6,7},{7,4},{8,9},{9,10},{10,1... | collective-permute-start | bytes 786440 | tf_op jit(solution)/shard_map/tokens/ppermute | solution.py:314
  13.0 5.9 %collective-permute-done.7.b.refs_0_ = bf16[1808,128]{1,0:T(8,128)(2,1)S(1)} collective-permute-done((bf16[1808,128]{1,0:T(8,128)(2,1)S(1)}, bf16[1808,128]{1,0:T(8,128)(2,1)S(1)}, u32[]{:S(2)}, u32[]{:S(2)}) %collective-permute-start.7) | collective-permute-done | bytes 462880 | tf_op jit(solution)/shard_map/a1/ppermute | solution.py:314
  19.2 3.4 %collective-permute-start.10 = (bf16[1808,128]{1,0:T(8,128)(2,1)S(1)}, bf16[1808,128]{1,0:T(8,128)(2,1)S(1)}, u32[]{:S(2)}, u32[]{:S(2)}) collective-permute-start(bf16[1808,128]{1,0:T(8,128)(2,1)S(1)} %collective-permute-done.8.d.refs_5_), channel_id=1, source_target_pairs={{0,24},{8,0},{16,8},{24,16},{1,25},{9,1},{17,9},{25,17},{2,26},{10... | collective-permute-start | bytes 1388552 | tf_op jit(solution)/shard_map/b3/ppermute | solution.py:314
  23.8 3.8 %collective-permute-start.6 = (bf16[32,4096]{1,0:T(8,128)(2,1)S(1)}, bf16[32,4096]{1,0:T(8,128)(2,1)S(1)}, u32[]{:S(2)}, u32[]{:S(2)}) collective-permute-start(bf16[32,4096]{1,0:T(8,128)(2,1)S(1)} %copy-done.11), channel_id=1, source_target_pairs={{0,3},{1,0},{2,1},{3,2},{4,7},{5,4},{6,5},{7,6},{8,11},{9,8},{10,9... | collective-permute-start | bytes 786440 | tf_op jit(solution)/shard_map/tokens/ppermute | solution.py:314
  27.8 6.7 %collective-permute-done.5 = bf16[32,4096]{1,0:T(8,128)(2,1)S(1)} collective-permute-done((bf16[32,4096]{1,0:T(8,128)(2,1)S(1)}, bf16[32,4096]{1,0:T(8,128)(2,1)S(1)}, u32[]{:S(2)}, u32[]{:S(2)}) %collective-permute-start.5) | collective-permute-done | bytes 262176 | tf_op jit(solution)/shard_map/tokens/ppermute | solution.py:314
  34.5 3.3 %collective-permute-start.11 = (bf16[128,4096]{1,0:T(8,128)(2,1)S(1)}, bf16[128,4096]{1,0:T(8,128)(2,1)S(1)}, u32[]{:S(2)}, u32[]{:S(2)}) collective-permute-start(bf16[128,4096]{1,0:T(8,128)(2,1)S(1)} %constant_dynamic-update-slice_fusion.xo), channel_id=1, source_target_pairs={{0,4},{4,0},{1,5},{5,1},{2,6},{6,2},{3,7},{7,3},{8,12},{12,8},{9,1... | collective-permute-start | bytes 3145736 | tf_op jit(solution)/shard_map/swap_tokens/ppermute | solution.py:319
  38.2 1.5 %collective-permute-start.15 = (bf16[3616,128]{1,0:T(8,128)(2,1)S(1)}, bf16[3616,128]{1,0:T(8,128)(2,1)S(1)}, u32[]{:S(2)}, u32[]{:S(2)}) collective-permute-start(bf16[3616,128]{1,0:T(8,128)(2,1)S(1)} %get-tuple-element.112), channel_id=1, source_target_pairs={{0,96},{32,0},{64,32},{96,64},{1,97},{33,1},{65,33},{97,65},{2,98}... | collective-permute-start | bytes 2777096 | tf_op jit(solution)/shard_map/pb2/ppermute | solution.py:314
  39.7 2.7 %collective-permute-start.12 = (bf16[3616,128]{1,0:T(8,128)(2,1)S(1)}, bf16[3616,128]{1,0:T(8,128)(2,1)S(1)}, u32[]{:S(2)}, u32[]{:S(2)}) collective-permute-start(bf16[3616,128]{1,0:T(8,128)(2,1)S(1)} %get-tuple-element.109), channel_id=1, source_target_pairs={{0,24},{8,0},{16,8},{24,16},{1,25},{9,1},{17,9},{25,17},{2,26},{10... | collective-permute-start | bytes 2777096 | tf_op jit(solution)/shard_map/qa2/ppermute | solution.py:314
  42.4 17.3 %collective-permute-done.15.refs_6_ = bf16[3616,128]{1,0:T(8,128)(2,1)S(1)} collective-permute-done((bf16[3616,128]{1,0:T(8,128)(2,1)S(1)}, bf16[3616,128]{1,0:T(8,128)(2,1)S(1)}, u32[]{:S(2)}, u32[]{:S(2)}) %collective-permute-start.15) | collective-permute-done | bytes 925728 | tf_op jit(solution)/shard_map/pb2/ppermute | solution.py:314
  59.7 2.4 %collective-permute-done.14.refs_4_.refs_9_ = bf16[3616,128]{1,0:T(8,128)(2,1)S(1)} collective-permute-done((bf16[3616,128]{1,0:T(8,128)(2,1)S(1)}, bf16[3616,128]{1,0:T(8,128)(2,1)S(1)}, u32[]{:S(2)}, u32[]{:S(2)}) %collective-permute-start.14) | collective-permute-done | bytes 925728 | tf_op jit(solution)/shard_map/qb1/ppermute | solution.py:314
  62.1 2.4 %collective-permute-start.19 = (bf16[3616,128]{1,0:T(8,128)(2,1)S(1)}, bf16[3616,128]{1,0:T(8,128)(2,1)S(1)}, u32[]{:S(2)}, u32[]{:S(2)}) collective-permute-start(bf16[3616,128]{1,0:T(8,128)(2,1)S(1)} %collective-permute-done.15.refs_6_), channel_id=1, source_target_pairs={{0,96},{32,0},{64,32},{96,64},{1,97},{33,1},{65,33},{97,65},{2,98}... | collective-permute-start | bytes 2777096 | tf_op jit(solution)/shard_map/fpb/ppermute | solution.py:314
  64.5 2.7 %collective-permute-start.17 = (bf16[3616,128]{1,0:T(8,128)(2,1)S(1)}, bf16[3616,128]{1,0:T(8,128)(2,1)S(1)}, u32[]{:S(2)}, u32[]{:S(2)}) collective-permute-start(bf16[3616,128]{1,0:T(8,128)(2,1)S(1)} %get-tuple-element.108), channel_id=1, source_target_pairs={{0,24},{8,0},{16,8},{24,16},{1,25},{9,1},{17,9},{25,17},{2,26},{10... | collective-permute-start | bytes 2777096 | tf_op jit(solution)/shard_map/pa2/ppermute | solution.py:314
  67.2 8.2 %forward.3 = (f32[128,3584]{1,0:T(8,128)S(1)}, f32[128,1792]{1,0:T(8,128)S(1)}, f32[128,1792]{1,0:T(8,128)S(1)}, bf16[5,28,256,128]{3,2,1,0:T(8,128)(2,1)S(1)}) custom-call(s32[16]{0:T(128)S(1)} %stack.102.chip_of, bf16[128,4096]{1,0:T(8,128)(2,1)S(1)} %constant_dynamic-update-slice_fusion.xo, bf16[128,4096]{1,0:T(8,128)(2,1)S(1)} %collective-permute-done.11.xt, ...), custom_call_target="tpu_custom_call" | custom-call | flops 10000000000 | bytes 30000000 | tf_op jit(solution)/shard_map/forward/pallas_call | solution.py:172
  75.5 6.9 %collective-permute-done.19.refs_3_ = bf16[3616,128]{1,0:T(8,128)(2,1)S(1)} collective-permute-done((bf16[3616,128]{1,0:T(8,128)(2,1)S(1)}, bf16[3616,128]{1,0:T(8,128)(2,1)S(1)}, u32[]{:S(2)}, u32[]{:S(2)}) %collective-permute-start.19) | collective-permute-done | bytes 925728 | tf_op jit(solution)/shard_map/fpb/ppermute | solution.py:314
  82.4 3.0 %collective-permute-done.20.refs_1_ = bf16[3616,128]{1,0:T(8,128)(2,1)S(1)} collective-permute-done((bf16[3616,128]{1,0:T(8,128)(2,1)S(1)}, bf16[3616,128]{1,0:T(8,128)(2,1)S(1)}, u32[]{:S(2)}, u32[]{:S(2)}) %collective-permute-start.20) | collective-permute-done | bytes 925728 | tf_op jit(solution)/shard_map/pb1/ppermute | solution.py:314
  85.4 2.4 %collective-permute-start.21 = (bf16[3616,128]{1,0:T(8,128)(2,1)S(1)}, bf16[3616,128]{1,0:T(8,128)(2,1)S(1)}, u32[]{:S(2)}, u32[]{:S(2)}) collective-permute-start(bf16[3616,128]{1,0:T(8,128)(2,1)S(1)} %get-tuple-element.113), channel_id=1, source_target_pairs={{0,96},{32,0},{64,32},{96,64},{1,97},{33,1},{65,33},{97,65},{2,98}... | collective-permute-start | bytes 2777096 | tf_op jit(solution)/shard_map/qb2/ppermute | solution.py:314
  88.0 2.5 %collective-permute-start.23 = (bf16[3616,128]{1,0:T(8,128)(2,1)}, bf16[3616,128]{1,0:T(8,128)(2,1)S(1)}, u32[]{:S(2)}, u32[]{:S(2)}) collective-permute-start(bf16[3616,128]{1,0:T(8,128)(2,1)} %copy-done.15), channel_id=1, source_target_pairs={{0,24},{8,0},{16,8},{24,16},{1,25},{9,1},{17,9},{25,17},{2,26},{10... | collective-permute-start | bytes 2777096 | tf_op jit(solution)/shard_map/fqa/ppermute | solution.py:314
  90.6 10.8 %forward.4 = (f32[128,3584]{1,0:T(8,128)S(1)}, f32[128,1792]{1,0:T(8,128)S(1)}, f32[128,1792]{1,0:T(8,128)S(1)}, bf16[7,28,256,128]{3,2,1,0:T(8,128)(2,1)S(1)}) custom-call(s32[16]{0:T(128)S(1)} %stack.102.chip_of, bf16[128,4096]{1,0:T(8,128)(2,1)S(1)} %constant_dynamic-update-slice_fusion.xo, ...), custom_call_target="tpu_custom_call", output_to_operand_aliasing={{0}: (13, {}), {1}: (14, {}), {2}: (15, {})} | custom-call | flops 13200000000 | bytes 39600000 | tf_op jit(solution)/shard_map/forward/pallas_call | solution.py:172
  101.4 2.8 %collective-permute-done.21.refs_1_ = bf16[3616,128]{1,0:T(8,128)(2,1)S(1)} collective-permute-done((bf16[3616,128]{1,0:T(8,128)(2,1)S(1)}, bf16[3616,128]{1,0:T(8,128)(2,1)S(1)}, u32[]{:S(2)}, u32[]{:S(2)}) %collective-permute-start.21) | collective-permute-done | bytes 925728 | tf_op jit(solution)/shard_map/qb2/ppermute | solution.py:314
  104.2 3.2 %collective-permute-done.22.refs_2_ = bf16[3616,128]{1,0:T(8,128)(2,1)S(1)} collective-permute-done((bf16[3616,128]{1,0:T(8,128)(2,1)}, bf16[3616,128]{1,0:T(8,128)(2,1)S(1)}, u32[]{:S(2)}, u32[]{:S(2)}) %collective-permute-start.22) | collective-permute-done | bytes 925728 | tf_op jit(solution)/shard_map/fqb/ppermute | solution.py:314
  107.5 4.2 %forward.5 = (f32[128,3584]{1,0:T(8,128)S(1)}, f32[128,1792]{1,0:T(8,128)S(1)}, f32[128,1792]{1,0:T(8,128)S(1)}, bf16[4,28,256,128]{3,2,1,0:T(8,128)(2,1)S(1)}) custom-call(s32[16]{0:T(128)S(1)} %stack.102.chip_of, bf16[128,4096]{1,0:T(8,128)(2,1)S(1)} %constant_dynamic-update-slice_fusion.xo, ...), custom_call_target="tpu_custom_call", output_to_operand_aliasing={{0}: (7, {}), {1}: (8, {}), {2}: (9, {})} | custom-call | flops 8400000000 | bytes 25200000 | tf_op jit(solution)/shard_map/forward/pallas_call | solution.py:172
  111.7 4.8 %collective-permute-start.24 = (f32[128,1792]{1,0:T(8,128)S(1)}, f32[128,1792]{1,0:T(8,128)S(1)}, u32[]{:S(2)}, u32[]{:S(2)}) collective-permute-start(f32[128,1792]{1,0:T(8,128)S(1)} %get-tuple-element.127), channel_id=1, source_target_pairs={{0,4},{4,0},{1,5},{5,1},{2,6},{6,2},{3,7},{7,3},{8,12},{12,8},{9,1... | collective-permute-start | bytes 2752520 | tf_op jit(solution)/shard_map/swap_gate_up/ppermute | solution.py:319
  116.7 2.0 %collective-permute-done.24.got = f32[128,1792]{1,0:T(8,128)S(1)} collective-permute-done((f32[128,1792]{1,0:T(8,128)S(1)}, f32[128,1792]{1,0:T(8,128)S(1)}, u32[]{:S(2)}, u32[]{:S(2)}) %collective-permute-start.24) | collective-permute-done | bytes 917536 | tf_op jit(solution)/shard_map/swap_gate_up/ppermute | solution.py:319
  121.7 1.6 %collective-permute-done.27.refs_3_ = bf16[128,1792]{1,0:T(8,128)(2,1)S(1)} collective-permute-done((bf16[128,1792]{1,0:T(8,128)(2,1)S(1)}, bf16[128,1792]{1,0:T(8,128)(2,1)S(1)}, u32[]{:S(2)}, u32[]{:S(2)}) %collective-permute-start.27) | collective-permute-done | bytes 458784 | tf_op jit(solution)/shard_map/swap_d/ppermute | solution.py:319
  123.3 5.9 %backward.2 = (f32[128,3072]{1,0:T(8,128)S(1)}, bf16[128,3072]{1,0:T(8,128)(2,1)S(1)}) custom-call(bf16[128,1792]{1,0:T(8,128)(2,1)S(1)} %get-tuple-element.131.refs_0_, bf16[128,1792]{1,0:T(8,128)(2,1)S(1)} %get-tuple-element.132.refs_1_, bf16[128,1792]{1,0:T(8,128)(2,1)S(1)} %collective-permute-done.26.refs_2_, ...), custom_call_target="tpu_custom_call" | custom-call | flops 11200000000 | bytes 33600000 | tf_op jit(solution)/shard_map/backward/pallas_call | solution.py:248
  129.6 2.1 %backward.3 = (f32[128,1024]{1,0:T(8,128)S(1)}, bf16[128,1024]{1,0:T(8,128)(2,1)S(1)}) custom-call(bf16[128,1792]{1,0:T(8,128)(2,1)S(1)} %get-tuple-element.131.refs_0_, bf16[128,1792]{1,0:T(8,128)(2,1)S(1)} %get-tuple-element.132.refs_1_, bf16[128,1792]{1,0:T(8,128)(2,1)S(1)} %collective-permute-done.26.refs_2_, ...), custom_call_target="tpu_custom_call" | custom-call | flops 4400000000 | bytes 13200000 | tf_op jit(solution)/shard_map/backward/pallas_call | solution.py:248
  135.0 1.9 %collective-permute-start.30 = (bf16[32,4096]{1,0:T(8,128)(2,1)S(1)}, bf16[32,4096]{1,0:T(8,128)(2,1)S(1)}, u32[]{:S(2)}, u32[]{:S(2)}) collective-permute-start(bf16[32,4096]{1,0:T(8,128)(2,1)S(1)} %get-tuple-element.143), channel_id=1, source_target_pairs={{0,3},{1,0},{2,1},{3,2},{4,7},{5,4},{6,5},{7,6},{8,11},{9,8},{10,9... | collective-permute-start | bytes 786440 | tf_op jit(solution)/shard_map/send_back/ppermute | solution.py:314
  138.6 4.0 %collective-permute-done.30.refs_1_ = bf16[32,4096]{1,0:T(8,128)(2,1)S(1)} collective-permute-done((bf16[32,4096]{1,0:T(8,128)(2,1)S(1)}, bf16[32,4096]{1,0:T(8,128)(2,1)S(1)}, u32[]{:S(2)}, u32[]{:S(2)}) %collective-permute-start.30) | collective-permute-done | bytes 262176 | tf_op jit(solution)/shard_map/send_back/ppermute | solution.py:314
  142.6 3.1 %collective-permute-done.31.refs_2_ = bf16[32,4096]{1,0:T(8,128)(2,1)S(1)} collective-permute-done((bf16[32,4096]{1,0:T(8,128)(2,1)S(1)}, bf16[32,4096]{1,0:T(8,128)(2,1)S(1)}, u32[]{:S(2)}, u32[]{:S(2)}) %collective-permute-start.31) | collective-permute-done | bytes 262176 | tf_op jit(solution)/shard_map/send_back/ppermute | solution.py:314
  145.7 6.0 %collective-permute-done.32.refs_3_ = bf16[32,4096]{1,0:T(8,128)(2,1)S(1)} collective-permute-done((bf16[32,4096]{1,0:T(8,128)(2,1)S(1)}, bf16[32,4096]{1,0:T(8,128)(2,1)S(1)}, u32[]{:S(2)}, u32[]{:S(2)}) %collective-permute-start.32) | collective-permute-done | bytes 262176 | tf_op jit(solution)/shard_map/send_back/ppermute | solution.py:314
  (100 shorter events, 18.4 us)
Async XLA Ops:
  2.0 3.1 %collective-permute-start.1 = (bf16[17,128,128]{2,1,0:T(8,128)(2,1)S(1)}, bf16[17,128,128]{2,1,0:T(8,128)(2,1)S(1)}, u32[]{:S(2)}, u32[]{:S(2)}) collective-permute-start(bf16[17,128,128]{2,1,0:T(8,128)(2,1)S(1)} %get-tuple-element.146), channel_id=1, source_target_pairs={{0,4},{4,0},{1,5},{5,1},{2,6},{6,2},{3,7},{7,3},{8,12},{12,8},{9,1... | collective-permute-start | bytes 1671176 | tf_op jit(solution)/shard_map/swap_blocks/ppermute | solution.py:319
  5.7 13.1 %collective-permute-start.7 = (bf16[1808,128]{1,0:T(8,128)(2,1)S(1)}, bf16[1808,128]{1,0:T(8,128)(2,1)S(1)}, u32[]{:S(2)}, u32[]{:S(2)}) collective-permute-start(bf16[1808,128]{1,0:T(8,128)(2,1)S(1)} %get-tuple-element.95.a.refs_0_), channel_id=1, source_target_pairs={{0,32},{32,64},{64,96},{96,0},{1,33},{33,65},{65,97},{97,1},{2,34}... | collective-permute-start | bytes 1388552 | tf_op jit(solution)/shard_map/a1/ppermute | solution.py:314
  7.1 12.0 %collective-permute-start.8 = (bf16[1808,128]{1,0:T(8,128)(2,1)S(1)}, bf16[1808,128]{1,0:T(8,128)(2,1)S(1)}, u32[]{:S(2)}, u32[]{:S(2)}) collective-permute-start(bf16[1808,128]{1,0:T(8,128)(2,1)S(1)} %get-tuple-element.96.c.refs_1_), channel_id=1, source_target_pairs={{0,24},{8,0},{16,8},{24,16},{1,25},{9,1},{17,9},{25,17},{2,26},{10... | collective-permute-start | bytes 1388552 | tf_op jit(solution)/shard_map/b2/ppermute | solution.py:314
  9.8 13.9 %collective-permute-start.3 = (bf16[1808,128]{1,0:T(8,128)(2,1)S(1)}, bf16[1808,128]{1,0:T(8,128)(2,1)S(1)}, u32[]{:S(2)}, u32[]{:S(2)}) collective-permute-start(bf16[1808,128]{1,0:T(8,128)(2,1)S(1)} %get-tuple-element.95.a.refs_0_), channel_id=1, source_target_pairs={{0,96},{32,0},{64,32},{96,64},{1,97},{33,1},{65,33},{97,65},{2,98}... | collective-permute-start | bytes 1388552 | tf_op jit(solution)/shard_map/a2/ppermute | solution.py:314
  11.3 12.5 %collective-permute-start.4 = (bf16[1808,128]{1,0:T(8,128)(2,1)S(1)}, bf16[1808,128]{1,0:T(8,128)(2,1)S(1)}, u32[]{:S(2)}, u32[]{:S(2)}) collective-permute-start(bf16[1808,128]{1,0:T(8,128)(2,1)S(1)} %get-tuple-element.96.c.refs_1_), channel_id=1, source_target_pairs={{0,8},{8,16},{16,24},{24,0},{1,9},{9,17},{17,25},{25,1},{2,10},{10... | collective-permute-start | bytes 1388552 | tf_op jit(solution)/shard_map/b1/ppermute | solution.py:314
  11.3 12.5 %collective-permute-start.2 = (bf16[32,4096]{1,0:T(8,128)(2,1)S(1)}, bf16[32,4096]{1,0:T(8,128)(2,1)S(1)}, u32[]{:S(2)}, u32[]{:S(2)}) collective-permute-start(bf16[32,4096]{1,0:T(8,128)(2,1)S(1)} %copy-done.11), channel_id=1, source_target_pairs={{0,1},{1,2},{2,3},{3,0},{4,5},{5,6},{6,7},{7,4},{8,9},{9,10},{10,1... | collective-permute-start | bytes 786440 | tf_op jit(solution)/shard_map/tokens/ppermute | solution.py:314
  19.2 15.3 %collective-permute-start.10 = (bf16[1808,128]{1,0:T(8,128)(2,1)S(1)}, bf16[1808,128]{1,0:T(8,128)(2,1)S(1)}, u32[]{:S(2)}, u32[]{:S(2)}) collective-permute-start(bf16[1808,128]{1,0:T(8,128)(2,1)S(1)} %collective-permute-done.8.d.refs_5_), channel_id=1, source_target_pairs={{0,24},{8,0},{16,8},{24,16},{1,25},{9,1},{17,9},{25,17},{2,26},{10... | collective-permute-start | bytes 1388552 | tf_op jit(solution)/shard_map/b3/ppermute | solution.py:314
  22.6 11.9 %collective-permute-start.9 = (bf16[1808,128]{1,0:T(8,128)(2,1)S(1)}, bf16[1808,128]{1,0:T(8,128)(2,1)S(1)}, u32[]{:S(2)}, u32[]{:S(2)}) collective-permute-start(bf16[1808,128]{1,0:T(8,128)(2,1)S(1)} %collective-permute-done.7.b.refs_0_), channel_id=1, source_target_pairs={{0,32},{32,64},{64,96},{96,0},{1,33},{33,65},{65,97},{97,1},{2,34}... | collective-permute-start | bytes 1388552 | tf_op jit(solution)/shard_map/a3/ppermute | solution.py:314
  23.8 10.6 %collective-permute-start.6 = (bf16[32,4096]{1,0:T(8,128)(2,1)S(1)}, bf16[32,4096]{1,0:T(8,128)(2,1)S(1)}, u32[]{:S(2)}, u32[]{:S(2)}) collective-permute-start(bf16[32,4096]{1,0:T(8,128)(2,1)S(1)} %copy-done.11), channel_id=1, source_target_pairs={{0,3},{1,0},{2,1},{3,2},{4,7},{5,4},{6,5},{7,6},{8,11},{9,8},{10,9... | collective-permute-start | bytes 786440 | tf_op jit(solution)/shard_map/tokens/ppermute | solution.py:314
  27.7 6.8 %collective-permute-start.5 = (bf16[32,4096]{1,0:T(8,128)(2,1)S(1)}, bf16[32,4096]{1,0:T(8,128)(2,1)S(1)}, u32[]{:S(2)}, u32[]{:S(2)}) collective-permute-start(bf16[32,4096]{1,0:T(8,128)(2,1)S(1)} %collective-permute-done.2), channel_id=1, source_target_pairs={{0,1},{1,2},{2,3},{3,0},{4,5},{5,6},{6,7},{7,4},{8,9},{9,10},{10,1... | collective-permute-start | bytes 786440 | tf_op jit(solution)/shard_map/tokens/ppermute | solution.py:314
  34.5 32.7 %collective-permute-start.11 = (bf16[128,4096]{1,0:T(8,128)(2,1)S(1)}, bf16[128,4096]{1,0:T(8,128)(2,1)S(1)}, u32[]{:S(2)}, u32[]{:S(2)}) collective-permute-start(bf16[128,4096]{1,0:T(8,128)(2,1)S(1)} %constant_dynamic-update-slice_fusion.xo), channel_id=1, source_target_pairs={{0,4},{4,0},{1,5},{5,1},{2,6},{6,2},{3,7},{7,3},{8,12},{12,8},{9,1... | collective-permute-start | bytes 3145736 | tf_op jit(solution)/shard_map/swap_tokens/ppermute | solution.py:319
  38.2 21.6 %collective-permute-start.15 = (bf16[3616,128]{1,0:T(8,128)(2,1)S(1)}, bf16[3616,128]{1,0:T(8,128)(2,1)S(1)}, u32[]{:S(2)}, u32[]{:S(2)}) collective-permute-start(bf16[3616,128]{1,0:T(8,128)(2,1)S(1)} %get-tuple-element.112), channel_id=1, source_target_pairs={{0,96},{32,0},{64,32},{96,64},{1,97},{33,1},{65,33},{97,65},{2,98}... | collective-permute-start | bytes 2777096 | tf_op jit(solution)/shard_map/pb2/ppermute | solution.py:314
  39.7 22.4 %collective-permute-start.14 = (bf16[3616,128]{1,0:T(8,128)(2,1)S(1)}, bf16[3616,128]{1,0:T(8,128)(2,1)S(1)}, u32[]{:S(2)}, u32[]{:S(2)}) collective-permute-start(bf16[3616,128]{1,0:T(8,128)(2,1)S(1)} %get-tuple-element.113), channel_id=1, source_target_pairs={{0,32},{32,64},{64,96},{96,0},{1,33},{33,65},{65,97},{97,1},{2,34}... | collective-permute-start | bytes 2777096 | tf_op jit(solution)/shard_map/qb1/ppermute | solution.py:314
  39.7 22.4 %collective-permute-start.13 = (bf16[3616,128]{1,0:T(8,128)(2,1)S(1)}, bf16[3616,128]{1,0:T(8,128)(2,1)S(1)}, u32[]{:S(2)}, u32[]{:S(2)}) collective-permute-start(bf16[3616,128]{1,0:T(8,128)(2,1)S(1)} %get-tuple-element.108), channel_id=1, source_target_pairs={{0,8},{8,16},{16,24},{24,0},{1,9},{9,17},{17,25},{25,1},{2,10},{10... | collective-permute-start | bytes 2777096 | tf_op jit(solution)/shard_map/pa1/ppermute | solution.py:314
  39.7 22.4 %collective-permute-start.12 = (bf16[3616,128]{1,0:T(8,128)(2,1)S(1)}, bf16[3616,128]{1,0:T(8,128)(2,1)S(1)}, u32[]{:S(2)}, u32[]{:S(2)}) collective-permute-start(bf16[3616,128]{1,0:T(8,128)(2,1)S(1)} %get-tuple-element.109), channel_id=1, source_target_pairs={{0,24},{8,0},{16,8},{24,16},{1,25},{9,1},{17,9},{25,17},{2,26},{10... | collective-permute-start | bytes 2777096 | tf_op jit(solution)/shard_map/qa2/ppermute | solution.py:314
  62.1 20.3 %collective-permute-start.19 = (bf16[3616,128]{1,0:T(8,128)(2,1)S(1)}, bf16[3616,128]{1,0:T(8,128)(2,1)S(1)}, u32[]{:S(2)}, u32[]{:S(2)}) collective-permute-start(bf16[3616,128]{1,0:T(8,128)(2,1)S(1)} %collective-permute-done.15.refs_6_), channel_id=1, source_target_pairs={{0,96},{32,0},{64,32},{96,64},{1,97},{33,1},{65,33},{97,65},{2,98}... | collective-permute-start | bytes 2777096 | tf_op jit(solution)/shard_map/fpb/ppermute | solution.py:314
  64.5 20.9 %collective-permute-start.20 = (bf16[3616,128]{1,0:T(8,128)(2,1)S(1)}, bf16[3616,128]{1,0:T(8,128)(2,1)S(1)}, u32[]{:S(2)}, u32[]{:S(2)}) collective-permute-start(bf16[3616,128]{1,0:T(8,128)(2,1)S(1)} %get-tuple-element.112), channel_id=1, source_target_pairs={{0,32},{32,64},{64,96},{96,0},{1,33},{33,65},{65,97},{97,1},{2,34}... | collective-permute-start | bytes 2777096 | tf_op jit(solution)/shard_map/pb1/ppermute | solution.py:314
  64.5 20.9 %collective-permute-start.16 = (bf16[3616,128]{1,0:T(8,128)(2,1)S(1)}, bf16[3616,128]{1,0:T(8,128)(2,1)S(1)}, u32[]{:S(2)}, u32[]{:S(2)}) collective-permute-start(bf16[3616,128]{1,0:T(8,128)(2,1)S(1)} %collective-permute-done.13.refs_2_), channel_id=1, source_target_pairs={{0,8},{8,16},{16,24},{24,0},{1,9},{9,17},{17,25},{25,1},{2,10},{10... | collective-permute-start | bytes 2777096 | tf_op jit(solution)/shard_map/fpa/ppermute | solution.py:314
  64.5 20.9 %collective-permute-start.17 = (bf16[3616,128]{1,0:T(8,128)(2,1)S(1)}, bf16[3616,128]{1,0:T(8,128)(2,1)S(1)}, u32[]{:S(2)}, u32[]{:S(2)}) collective-permute-start(bf16[3616,128]{1,0:T(8,128)(2,1)S(1)} %get-tuple-element.108), channel_id=1, source_target_pairs={{0,24},{8,0},{16,8},{24,16},{1,25},{9,1},{17,9},{25,17},{2,26},{10... | collective-permute-start | bytes 2777096 | tf_op jit(solution)/shard_map/pa2/ppermute | solution.py:314
  85.4 18.8 %collective-permute-start.21 = (bf16[3616,128]{1,0:T(8,128)(2,1)S(1)}, bf16[3616,128]{1,0:T(8,128)(2,1)S(1)}, u32[]{:S(2)}, u32[]{:S(2)}) collective-permute-start(bf16[3616,128]{1,0:T(8,128)(2,1)S(1)} %get-tuple-element.113), channel_id=1, source_target_pairs={{0,96},{32,0},{64,32},{96,64},{1,97},{33,1},{65,33},{97,65},{2,98}... | collective-permute-start | bytes 2777096 | tf_op jit(solution)/shard_map/qb2/ppermute | solution.py:314
  87.9 19.6 %collective-permute-start.22 = (bf16[3616,128]{1,0:T(8,128)(2,1)}, bf16[3616,128]{1,0:T(8,128)(2,1)S(1)}, u32[]{:S(2)}, u32[]{:S(2)}) collective-permute-start(bf16[3616,128]{1,0:T(8,128)(2,1)} %copy-done.14), channel_id=1, source_target_pairs={{0,32},{32,64},{64,96},{96,0},{1,33},{33,65},{65,97},{97,1},{2,34}... | collective-permute-start | bytes 2777096 | tf_op jit(solution)/shard_map/fqb/ppermute | solution.py:314
  87.9 19.6 %collective-permute-start.18 = (bf16[3616,128]{1,0:T(8,128)(2,1)S(1)}, bf16[3616,128]{1,0:T(8,128)(2,1)S(1)}, u32[]{:S(2)}, u32[]{:S(2)}) collective-permute-start(bf16[3616,128]{1,0:T(8,128)(2,1)S(1)} %get-tuple-element.109), channel_id=1, source_target_pairs={{0,8},{8,16},{16,24},{24,0},{1,9},{9,17},{17,25},{25,1},{2,10},{10... | collective-permute-start | bytes 2777096 | tf_op jit(solution)/shard_map/qa1/ppermute | solution.py:314
  88.0 19.4 %collective-permute-start.23 = (bf16[3616,128]{1,0:T(8,128)(2,1)}, bf16[3616,128]{1,0:T(8,128)(2,1)S(1)}, u32[]{:S(2)}, u32[]{:S(2)}) collective-permute-start(bf16[3616,128]{1,0:T(8,128)(2,1)} %copy-done.15), channel_id=1, source_target_pairs={{0,24},{8,0},{16,8},{24,16},{1,25},{9,1},{17,9},{25,17},{2,26},{10... | collective-permute-start | bytes 2777096 | tf_op jit(solution)/shard_map/fqa/ppermute | solution.py:314
  111.7 6.9 %collective-permute-start.24 = (f32[128,1792]{1,0:T(8,128)S(1)}, f32[128,1792]{1,0:T(8,128)S(1)}, u32[]{:S(2)}, u32[]{:S(2)}) collective-permute-start(f32[128,1792]{1,0:T(8,128)S(1)} %get-tuple-element.127), channel_id=1, source_target_pairs={{0,4},{4,0},{1,5},{5,1},{2,6},{6,2},{3,7},{7,3},{8,12},{12,8},{9,1... | collective-permute-start | bytes 2752520 | tf_op jit(solution)/shard_map/swap_gate_up/ppermute | solution.py:319
  116.6 3.7 %collective-permute-start.25 = (f32[128,1792]{1,0:T(8,128)S(1)}, f32[128,1792]{1,0:T(8,128)S(1)}, u32[]{:S(2)}, u32[]{:S(2)}) collective-permute-start(f32[128,1792]{1,0:T(8,128)S(1)} %get-tuple-element.129), channel_id=1, source_target_pairs={{0,4},{4,0},{1,5},{5,1},{2,6},{6,2},{3,7},{7,3},{8,12},{12,8},{9,1... | collective-permute-start | bytes 2752520 | tf_op jit(solution)/shard_map/swap_gate_up/ppermute | solution.py:319
  119.8 1.9 %collective-permute-start.26 = (bf16[128,1792]{1,0:T(8,128)(2,1)S(1)}, bf16[128,1792]{1,0:T(8,128)(2,1)S(1)}, u32[]{:S(2)}, u32[]{:S(2)}) collective-permute-start(bf16[128,1792]{1,0:T(8,128)(2,1)S(1)} %get-tuple-element.133), channel_id=1, source_target_pairs={{0,4},{4,0},{1,5},{5,1},{2,6},{6,2},{3,7},{7,3},{8,12},{12,8},{9,1... | collective-permute-start | bytes 1376264 | tf_op jit(solution)/shard_map/swap_d/ppermute | solution.py:319
  121.4 1.9 %collective-permute-start.27 = (bf16[128,1792]{1,0:T(8,128)(2,1)S(1)}, bf16[128,1792]{1,0:T(8,128)(2,1)S(1)}, u32[]{:S(2)}, u32[]{:S(2)}) collective-permute-start(bf16[128,1792]{1,0:T(8,128)(2,1)S(1)} %get-tuple-element.134), channel_id=1, source_target_pairs={{0,4},{4,0},{1,5},{5,1},{2,6},{6,2},{3,7},{7,3},{8,12},{12,8},{9,1... | collective-permute-start | bytes 1376264 | tf_op jit(solution)/shard_map/swap_d/ppermute | solution.py:319
  129.2 4.2 %collective-permute-start.28 = (bf16[128,3072]{1,0:T(8,128)(2,1)S(1)}, bf16[128,3072]{1,0:T(8,128)(2,1)S(1)}, u32[]{:S(2)}, u32[]{:S(2)}) collective-permute-start(bf16[128,3072]{1,0:T(8,128)(2,1)S(1)} %get-tuple-element.140), channel_id=1, source_target_pairs={{0,4},{4,0},{1,5},{5,1},{2,6},{6,2},{3,7},{7,3},{8,12},{12,8},{9,1... | collective-permute-start | bytes 2359304 | tf_op jit(solution)/shard_map/swap_part/ppermute | solution.py:319
  131.7 1.6 %collective-permute-start.29 = (bf16[128,1024]{1,0:T(8,128)(2,1)S(1)}, bf16[128,1024]{1,0:T(8,128)(2,1)S(1)}, u32[]{:S(2)}, u32[]{:S(2)}) collective-permute-start(bf16[128,1024]{1,0:T(8,128)(2,1)S(1)} %get-tuple-element.141), channel_id=1, source_target_pairs={{0,4},{4,0},{1,5},{5,1},{2,6},{6,2},{3,7},{7,3},{8,12},{12,8},{9,1... | collective-permute-start | bytes 786440 | tf_op jit(solution)/shard_map/swap_part/ppermute | solution.py:319
  135.0 7.6 %collective-permute-start.30 = (bf16[32,4096]{1,0:T(8,128)(2,1)S(1)}, bf16[32,4096]{1,0:T(8,128)(2,1)S(1)}, u32[]{:S(2)}, u32[]{:S(2)}) collective-permute-start(bf16[32,4096]{1,0:T(8,128)(2,1)S(1)} %get-tuple-element.143), channel_id=1, source_target_pairs={{0,3},{1,0},{2,1},{3,2},{4,7},{5,4},{6,5},{7,6},{8,11},{9,8},{10,9... | collective-permute-start | bytes 786440 | tf_op jit(solution)/shard_map/send_back/ppermute | solution.py:314
  136.9 8.8 %collective-permute-start.31 = (bf16[32,4096]{1,0:T(8,128)(2,1)S(1)}, bf16[32,4096]{1,0:T(8,128)(2,1)S(1)}, u32[]{:S(2)}, u32[]{:S(2)}) collective-permute-start(bf16[32,4096]{1,0:T(8,128)(2,1)S(1)} %get-tuple-element.144), channel_id=1, source_target_pairs={{0,2},{1,3},{2,0},{3,1},{4,6},{5,7},{6,4},{7,5},{8,10},{9,11},{10,... | collective-permute-start | bytes 786440 | tf_op jit(solution)/shard_map/send_back/ppermute | solution.py:314
  136.9 14.8 %collective-permute-start.32 = (bf16[32,4096]{1,0:T(8,128)(2,1)S(1)}, bf16[32,4096]{1,0:T(8,128)(2,1)S(1)}, u32[]{:S(2)}, u32[]{:S(2)}) collective-permute-start(bf16[32,4096]{1,0:T(8,128)(2,1)S(1)} %get-tuple-element.145), channel_id=1, source_target_pairs={{0,1},{1,2},{2,3},{3,0},{4,5},{5,6},{6,7},{7,4},{8,9},{9,10},{10,1... | collective-permute-start | bytes 786440 | tf_op jit(solution)/shard_map/send_back/ppermute | solution.py:314
  (23 other events, 213.1 us)
